TPU v7x, 256 devices: a whole 4x4x8 slice. The times are simulated.
256 devices in a mesh: dp: 4 (over x), expert: 32 (over z, y), tensor: 2 (over core).
Axes of the slice: x: 4, y: 4, z: 8, core: 2. Of those that a mesh axis runs over, the one named last changes fastest.
Arguments:
- queries: bfloat16 [8192, 4096], P(('dp', 'expert'), 'tensor'), may hold values from -8 to 8
- fresh_keys: bfloat16 [8192, 512], P(('dp', 'expert'), 'tensor'), may hold values from -6 to 6
- fresh_values: bfloat16 [8192, 512], P(('dp', 'expert'), 'tensor'), may hold values from -6 to 6
- resident_keys: bfloat16 [128, 2048, 512], P(('dp', 'expert'), None, 'tensor'), may hold values from -8 to 8
- resident_values: bfloat16 [128, 2048, 512], P(('dp', 'expert'), None, 'tensor'), may hold values from -6 to 6
- out_weight: bfloat16 [4096, 2048], P('tensor', 'dp'), may hold values from -0.5 to 0.5
- residual: bfloat16 [8192, 2048], P(('dp', 'expert')), may hold values from -23 to 23
- norm_gain: float32 [2048], replicated, may hold values from 0.1 to 1.9
- expert_ids: int32 [8192, 8], P(('dp', 'expert')), may hold values from 0 to 127, all different within a row; in each aligned block of 64 rows (0 to 63, 64 to 127, ...) at most 6 rows name the same one
- gates: float32 [8192, 8], P(('dp', 'expert')), may hold values from 0.05 to 0.5
- w_gate: bfloat16 [128, 2048, 768], P(('dp', 'expert'), None, 'tensor'), may hold values from -0.125 to 0.125
- w_up: bfloat16 [128, 2048, 768], P(('dp', 'expert'), None, 'tensor'), may hold values from -0.125 to 0.125
- w_down: bfloat16 [128, 768, 2048], P(('dp', 'expert'), 'tensor'), may hold values from -0.21875 to 0.21875
Outputs:
- mixed: bfloat16 [8192, 2048], P(('dp', 'expert'), 'tensor')
Inputs may be any that keep to these rules, and one draw needn't show every extreme that they name: `expert_ids`: within the 64 tokens of one sequence no expert is named by more than 6 tokens, a bound that some block reaches; a token names 8 different experts.
All inputs are finite; a program needn't handle non-finite values.
Results may differ from a plain program's by a relative error of at most 0.0085.
Values may be sent and summed in bfloat16 or wider, within the bound.
No kernel may reach another device: no remote copies, remote signals or barrier semaphores. Data moves between devices by JAX's collectives and lax.ppermute only.
A program may use at most 64 MiB of HBM per device.

v0:
```python
import jax
import jax.numpy as jnp
from jax import lax
from jax.sharding import PartitionSpec as P

D = 2048
HEAD_WIDTH = 128


def attend_local(queries, fresh_keys, fresh_values, resident_keys, resident_values):
    tokens_here = queries.shape[0]
    kv_here = fresh_keys.shape[1] // HEAD_WIDTH
    query_group = queries.shape[1] // HEAD_WIDTH // kv_here
    context = resident_keys.shape[1]
    query_rows = queries.reshape(tokens_here, kv_here, query_group, HEAD_WIDTH)
    joined_keys = jnp.concatenate([resident_keys[0], fresh_keys], 0).reshape(
        context + tokens_here, kv_here, HEAD_WIDTH
    )
    joined_values = jnp.concatenate([resident_values[0], fresh_values], 0).reshape(
        context + tokens_here, kv_here, HEAD_WIDTH
    )
    score = jnp.einsum(
        "tjgd,sjd->jgts", query_rows, joined_keys, preferred_element_type=jnp.float32
    ) * HEAD_WIDTH ** (-0.5)
    places = jnp.arange(context + tokens_here)
    rows = jnp.arange(tokens_here)
    allowed = (places[None, :] < context) | (places[None, :] - context <= rows[:, None])
    score = jnp.where(allowed, score, jnp.float32(-1e30))
    top_score = jnp.max(score, axis=-1, keepdims=True)
    weight = jnp.exp(score - top_score)
    probs = (weight / jnp.sum(weight, axis=-1, keepdims=True)).astype(jnp.bfloat16)
    attended = jnp.einsum(
        "jgts,sjd->tjgd", probs, joined_values, preferred_element_type=jnp.float32
    )
    return attended.reshape(tokens_here, -1).astype(jnp.bfloat16)


def expert_rows(block, gate_mat, up_mat, down_mat):
    sources, items, width = block.shape
    flat = block.reshape(sources * items, width)
    gate_part = jnp.dot(flat, gate_mat, preferred_element_type=jnp.float32)
    up_part = jnp.dot(flat, up_mat, preferred_element_type=jnp.float32)
    act = (jax.nn.silu(gate_part) * up_part).astype(jnp.bfloat16)
    result = jnp.dot(act, down_mat, preferred_element_type=jnp.float32)
    return result.reshape(sources, items, -1)


def per_device(
    queries,
    fresh_keys,
    fresh_values,
    resident_keys,
    resident_values,
    out_weight,
    residual,
    norm_gain,
    expert_ids,
    gates,
    w_gate,
    w_up,
    w_down,
):
    attended = attend_local(queries, fresh_keys, fresh_values, resident_keys, resident_values)
    partial_sum = jnp.dot(
        attended,
        lax.all_gather(out_weight, "dp", axis=1, tiled=True),
        preferred_element_type=jnp.float32,
    )
    tokens_here = residual.shape[0]
    pairs = lax.axis_size("tensor")
    half = D // pairs
    lane = lax.axis_index("tensor")
    summed = lax.psum(partial_sum.astype(jnp.bfloat16), "tensor").astype(jnp.float32)
    hidden = residual.astype(jnp.float32) + summed
    mean_square = jnp.mean(hidden * hidden, axis=-1, keepdims=True)
    normed = (hidden * lax.rsqrt(mean_square + 1e-06) * norm_gain).astype(jnp.bfloat16)
    hidden_half = lax.dynamic_slice_in_dim(hidden, lane * half, half, 1)
    owners = lax.axis_size("dp") * lax.axis_size("expert")
    top = expert_ids.shape[1]
    slots = max(2, tokens_here * top * 3 // (2 * owners))
    onehot = (expert_ids[:, :, None] == jnp.arange(owners)[None, None, :]).astype(jnp.int32)
    per_token = jnp.sum(onehot, axis=1)
    before = jnp.cumsum(per_token, axis=0) - per_token
    slot = jnp.sum(onehot * before[:, None, :], axis=-1)
    token_rows = jnp.broadcast_to(
        jnp.arange(tokens_here, dtype=jnp.int32)[:, None], expert_ids.shape
    )
    owner_rows = jnp.full((owners, slots), -1, jnp.int32).at[expert_ids, slot].set(token_rows)
    valid = owner_rows >= 0
    outgoing = jnp.where(
        valid[:, :, None], normed[jnp.maximum(owner_rows, 0)], jnp.zeros((), jnp.bfloat16)
    )
    expert_part = expert_rows(
        lax.all_to_all(outgoing, ("dp", "expert"), split_axis=0, concat_axis=0, tiled=True),
        w_gate[0],
        w_up[0],
        w_down[0],
    )
    owned = lax.psum_scatter(
        expert_part.astype(jnp.bfloat16), "tensor", scatter_dimension=2, tiled=True
    )
    returned = lax.all_to_all(owned, ("dp", "expert"), split_axis=0, concat_axis=0, tiled=True)
    picked = returned[expert_ids, slot]
    moe = jnp.sum(gates[:, :, None] * picked.astype(jnp.float32), axis=1)
    return (hidden_half + moe).astype(jnp.bfloat16)


def solution(mesh):
    return jax.shard_map(
        per_device,
        mesh=mesh,
        in_specs=(
            P(("dp", "expert"), "tensor"),
            P(("dp", "expert"), "tensor"),
            P(("dp", "expert"), "tensor"),
            P(("dp", "expert"), None, "tensor"),
            P(("dp", "expert"), None, "tensor"),
            P("tensor", "dp"),
            P(("dp", "expert"), None),
            P(),
            P(("dp", "expert"), None),
            P(("dp", "expert"), None),
            P(("dp", "expert"), None, "tensor"),
            P(("dp", "expert"), None, "tensor"),
            P(("dp", "expert"), "tensor", None),
        ),
        out_specs=P(("dp", "expert"), "tensor"),
        check_vma=False,
    )
```

profile of v0, /device:TPU:32, one launch (start us, length us, event | category | flops | bytes accessed | tf_op | source)
XLA Modules:
  0.0 379.2 jit_solution(17011101792321861209)
XLA Ops:
  6.5 0.0 copy-start
  6.5 0.0 all-gather.2.cloned.1.call-start
  6.5 0.7 all-gather.2.cloned.1.call-update
  7.3 0.0 copy-start.4
  7.3 0.0 all-reduce.2.cloned.1.call-start
  7.3 1.5 copy.74
  8.8 1.4 copy.75
  10.2 0.0 copy-done.4
  10.3 0.0 copy-start.5
  10.3 0.0 copy-start.6
  10.3 1.5 copy.71
  11.8 1.3 copy.72
  13.1 0.0 copy-done.5
  13.1 0.0 copy-done.6
  13.1 0.1 fusion.26
  13.3 0.0 copy-start.2
  13.3 4.6 %fusion.46 = f32[2,8,64]{2,1,0:T(8,128)S(1)} fusion(pred[64,2112]{1,0:T(8,128)(4,1)S(1)} %fusion.26, bf16[64,2,128]{2,0,1:T(8,128)(2,1)S(1)} %get-tuple-element.9, bf16[2048,2,128]{2,0,1:T(8,128)(2,1)} %copy.75, bf16[64,2,8,128]{3,2,1,0:T(8,128)(2,1)S(1)} %bitcast.97), kind=kOutput, calls=%fused_computation.69 | convolution fusion | flops 564463680 | bytes 1482752 | tf_op jit(solution)/shard_map/sub | solution.py:30
  17.9 0.0 copy-done.2
  17.9 4.9 %fusion.19 = bf16[64,2,8,128]{3,0,2,1:T(8,128)(2,1)S(1)} fusion(f32[2,8,64]{2,1,0:T(8,128)S(1)} %fusion.46, bf16[64,2,128]{2,0,1:T(8,128)(2,1)S(1)} %get-tuple-element.10, bf16[2048,2,128]{2,0,1:T(8,128)(2,1)} %copy.72, pred[64,2112]{1,0:T(8,128)(4,1)S(1)} %fusion.26, bf16[64,2,128]{2,0,1:T(8,128)(2,1)S(1)} %get-tuple-element.9, ...), kind=kOutput, calls=%fused_computation.25 | convolution fusion | flops 1122569216 | bytes 2826240 | tf_op jit(solution)/shard_map/jgts,sjd->tjgd/dot_general | solution.py:32
  22.8 0.2 copy.78
  23.0 0.0 copy-done.7
  23.0 0.1 copy.80
  23.1 0.1 convert_reduce_fusion
  23.3 0.1 reduce_window_sum.11
  23.4 1.2 select_reduce_fusion
  24.6 0.1 copy.81
  24.7 0.1 copy.82
  24.8 0.1 reshape.80
  24.9 0.1 reshape.82
  25.0 22.0 %scatter_fusion = s32[128,6]{0,1:T(8,128)S(1)} fusion(s32[128,6]{0,1:T(8,128)S(1)} %broadcast_in_dim.26, s32[512]{0:T(512)S(1)} %reshape.80, s32[512]{0:T(512)S(1)} %reshape.82), kind=kCustom, calls=%fused_computation.2 | custom fusion | bytes 10240 | tf_op jit(solution)/shard_map/scatter | solution.py:88
  47.0 0.1 copy.84
  47.1 0.1 reshape.68
  47.3 50.1 %all-gather.2.cloned.1.call-done = bf16[2048,2048]{1,0:T(8,128)(2,1)} async-done(((bf16[2048,512]{1,0:T(8,128)(2,1)}), bf16[2048,2048]{1,0:T(8,128)(2,1)}) %all-gather.2.cloned.1.call-update) | async-done | bytes 8388624 | tf_op jit(solution)/shard_map/all_gather | solution.py:66
  97.4 5.7 %convolution_convert_fusion.1 = bf16[64,2048]{1,0:T(8,128)(2,1)} fusion(bf16[2048,2048]{1,0:T(8,128)(2,1)} %all-gather.2.cloned.1.call-done, bf16[8,8,16,128]{3,2,1,0:T(8,128)(2,1)S(1)} %bitcast.95), kind=kOutput, calls=%fused_computation.14 | convolution fusion | flops 537001984 | bytes 8912896 | tf_op jit(solution)/shard_map/dot_general | solution.py:64
  103.1 0.0 all-reduce.2.cloned.1.call-update
  103.1 0.2 reduce-scatter.2.cloned.1.call-start
  103.4 0.1 copy.83
  103.5 29.8 %all-reduce.2.cloned.1.call-done = bf16[64,2048]{1,0:T(8,128)(2,1)} async-done(((bf16[64,2048]{1,0:T(8,128)(2,1)}), bf16[64,2048]{1,0:T(8,128)(2,1)}) %all-reduce.2.cloned.1.call-update) | async-done | bytes 262160 | tf_op jit(solution)/shard_map/psum | solution.py:73
  133.3 0.0 copy-done.3
  133.3 1.9 convert_add_fusion
  135.3 1.1 multiply_convert_fusion
  136.3 4.3 %gather_fusion = bf16[768,2048]{1,0:T(8,128)(2,1)} fusion(bf16[64,2048]{1,0:T(8,128)(2,1)S(1)} %multiply_convert_fusion, s32[1024]{0:T(1024)S(1)} %pad_clamp_fusion), kind=kCustom, calls=%fused_computation | custom fusion | bytes 6294528 | tf_op jit(solution)/shard_map/gather | solution.py:91
  140.6 6.3 %reshape.67 = bf16[128,6,2048]{2,1,0:T(8,128)(2,1)} reshape(bf16[768,2048]{1,0:T(8,128)(2,1)} %gather_fusion) | data formatting | bytes 6291456 | tf_op jit(solution)/shard_map/gather | solution.py:91
  146.9 2.6 broadcast_select_fusion
  149.5 111.2 %all_to_all.10 = bf16[128,6,2048]{2,1,0:T(8,128)(2,1)} all-to-all(bf16[128,6,2048]{2,1,0:T(8,128)(2,1)S(1)} %broadcast_select_fusion), channel_id=1, replica_groups=mesh['dp'=4,'expert'=32,'tensor'=2] {'dp','expert'}, dimensions={0} | all-to-all | bytes 6291456 | tf_op jit(solution)/shard_map/all_to_all | solution.py:94
  260.8 6.3 %reshape.65 = bf16[768,2048]{1,0:T(8,128)(2,1)} reshape(bf16[128,6,2048]{2,1,0:T(8,128)(2,1)} %all_to_all.10) | data formatting | bytes 6291456 | tf_op jit(solution)/shard_map/reshape | solution.py:40
  267.1 4.3 %fusion.10 = f32[768,384]{1,0:T(8,128)S(1)} fusion(bf16[768,2048]{1,0:T(8,128)(2,1)} %reshape.65, bf16[1,2048,384]{2,1,0:T(8,128)(2,1)} %param.23), kind=kOutput, calls=%fused_computation.20 | convolution fusion | flops 1207959552 | bytes 5898240 | tf_op jit(solution)/shard_map/dot_general | solution.py:41
  271.4 0.0 copy-done.1
  271.4 0.0 copy-done.10
  271.4 1.8 fusion.15
  273.3 0.2 dot_general.25
  273.5 3.5 convolution_convert_fusion
  276.9 0.0 reduce-scatter.2.cloned.1.call-update
  277.0 11.5 %reduce-scatter.2.cloned.1.call-done = bf16[128,6,1024]{2,0,1:T(8,128)(2,1)} async-done(((bf16[128,6,2048]{2,0,1:T(8,128)(2,1)}), bf16[128,6,1024]{2,0,1:T(8,128)(2,1)}) %reduce-scatter.2.cloned.1.call-update) | async-done | bytes 1572880 | tf_op jit(solution)/shard_map/reduce_scatter | solution.py:99
  288.4 3.6 copy.86
  292.1 14.3 %all-to-all-start.1 = ((bf16[128,6,1024]{2,1,0:T(8,128)(2,1)}), bf16[128,6,1024]{2,1,0:T(8,128)(2,1)}, u32[]{:S(2)}, u32[]{:S(2)}) async-start(bf16[128,6,1024]{2,1,0:T(8,128)(2,1)} %copy.86), calls=%async_computation.2 | async-start | bytes 4194304 | tf_op jit(solution)/shard_map/all_to_all | solution.py:102
  306.4 0.1 copy.87
  306.5 0.1 reshape.74
  306.6 0.1 copy.79
  306.7 52.1 %all-to-all-done.1 = bf16[128,6,1024]{2,1,0:T(8,128)(2,1)} async-done(((bf16[128,6,1024]{2,1,0:T(8,128)(2,1)}), bf16[128,6,1024]{2,1,0:T(8,128)(2,1)}, u32[]{:S(2)}, u32[]{:S(2)}) %all-to-all-start.1) | async-done | bytes 1572896 | tf_op jit(solution)/shard_map/all_to_all | solution.py:102
  358.8 2.5 copy.88
  361.2 7.9 %gather_fusion.1 = bf16[512,1024]{1,0:T(8,128)(2,1)} fusion(bf16[128,6,1024]{2,0,1:T(8,128)(2,1)S(1)} %copy.88, s32[512]{0:T(512)S(1)} %reshape.74), kind=kCustom, calls=%fused_computation.1 | custom fusion | bytes 2101248 | tf_op jit(solution)/shard_map/gather | solution.py:103
  369.1 1.9 fusion.6
  371.0 1.6 add_convert_fusion
  (21 shorter events, 0.1 us)
Async XLA Ops:
  6.5 266.9 %copy-start = (bf16[1,384,2048]{2,1,0:T(8,128)(2,1)S(1)}, bf16[1,384,2048]{2,1,0:T(8,128)(2,1)}, u32[]{:S(2)}) copy-start(bf16[1,384,2048]{2,1,0:T(8,128)(2,1)} %param.25) | copy-start | bytes 4718596
  6.5 90.8 %all-gather.2.cloned.1.call-start = ((), (), s32[]{:S(2)}) async-start(), calls=%async_computation.3 | async-start | bytes 10485760 | tf_op jit(solution)/shard_map/all_gather | solution.py:66
  7.3 3.0 copy-start.4
  7.3 126.1 %all-reduce.2.cloned.1.call-start = ((), (), s32[]{:S(2)}) async-start(), calls=%async_computation.4 | async-start | bytes 524288 | tf_op jit(solution)/shard_map/psum | solution.py:73
  10.3 2.8 copy-start.5
  10.3 2.8 copy-start.6
  13.3 4.7 %copy-start.2 = (bf16[2048,2,128]{2,0,1:T(8,128)(2,1)S(1)}, bf16[2048,2,128]{2,0,1:T(8,128)(2,1)}, u32[]{:S(2)}) copy-start(bf16[2048,2,128]{2,0,1:T(8,128)(2,1)} %copy.75) | copy-start | bytes 3145732
  17.9 5.1 %copy-start.7 = (s32[64,8]{0,1:T(8,128)S(1)}, s32[64,8]{0,1:T(8,128)}, u32[]{:S(2)}) copy-start(s32[64,8]{0,1:T(8,128)} %param.21) | copy-start | bytes 6148
  97.4 35.9 %copy-start.3 = (bf16[64,2048]{1,0:T(8,128)(2,1)S(1)}, bf16[64,2048]{1,0:T(8,128)(2,1)}, u32[]{:S(2)}) copy-start(bf16[64,2048]{1,0:T(8,128)(2,1)} %param.19) | copy-start | bytes 786436
  97.4 37.9 %copy-start.8 = (f32[2048]{0:T(1024)S(1)}, f32[2048]{0:T(1024)}, u32[]{:S(2)}) copy-start(f32[2048]{0:T(1024)} %param.20) | copy-start | bytes 24580
  103.1 185.3 %reduce-scatter.2.cloned.1.call-start = ((), (), s32[]{:S(2)}) async-start(), calls=%async_computation.5 | async-start | bytes 4718592 | tf_op jit(solution)/shard_map/reduce_scatter | solution.py:99
  267.1 4.3 %copy-start.1 = (bf16[768,2048]{1,0:T(8,128)(2,1)S(1)}, bf16[768,2048]{1,0:T(8,128)(2,1)}, u32[]{:S(2)}) copy-start(bf16[768,2048]{1,0:T(8,128)(2,1)} %reshape.65) | copy-start | bytes 9437188
  267.1 4.3 %copy-start.10 = (bf16[1,2048,384]{2,1,0:T(8,128)(2,1)S(1)}, bf16[1,2048,384]{2,1,0:T(8,128)(2,1)}, u32[]{:S(2)}) copy-start(bf16[1,2048,384]{2,1,0:T(8,128)(2,1)} %param.24) | copy-start | bytes 4718596
  292.1 14.5 %copy-start.9 = (f32[64,8]{0,1:T(8,128)S(1)}, f32[64,8]{0,1:T(8,128)}, u32[]{:S(2)}) copy-start(f32[64,8]{0,1:T(8,128)} %param.22) | copy-start | bytes 6148
  292.1 66.7 %all-to-all-start.1 = ((bf16[128,6,1024]{2,1,0:T(8,128)(2,1)}), bf16[128,6,1024]{2,1,0:T(8,128)(2,1)}, u32[]{:S(2)}, u32[]{:S(2)}) async-start(bf16[128,6,1024]{2,1,0:T(8,128)(2,1)} %copy.86), calls=%async_computation.2 | async-start | bytes 4194304 | tf_op jit(solution)/shard_map/all_to_all | solution.py:102
Sparse Core Ops, SparseCore 0:
  9.1 88.1 all-gather.1
  103.2 30.0 all-reduce.1
  277.1 11.3 reduce-scatter.1
where the time goes:
time: 380 us; the launch traced here: 379 us
  waiting for transfers between devices  144 us (38%)
  blocking collectives  111 us (29%)
  local copies, waits for them, and re-layouts  60 us (16%)
  matrix products  24.9 us (7%)
  starting transfers between devices  14.6 us (4%)
  between operations  13.4 us (4%)
  other arithmetic  10.8 us (3%)
    all_to_all x1, blocking collectives, per_device(): lax.all_to_all(outgoing, ('dp', 'expert'), split_axis=0, concat_axis=0, t...  111 us
    all_to_all x1, waiting for transfers between devices, per_device(): lax.all_to_all(owned, ('dp', 'expert'), split_axis=0, concat_axis=0, tile...  52.1 us
    all_gather x1, waiting for transfers between devices, per_device(): lax.all_gather(out_weight, 'dp', axis=1, tiled=True)  50.1 us
    psum x1, waiting for transfers between devices, per_device(): lax.psum(partial_sum.astype(jnp.bfloat16), 'tensor').astype(jnp.float32)  29.8 us
    scatter x1, local copies, waits for them, and re-layouts, per_device(): jnp.full((owners, slots), -1, jnp.int32).at[expert_ids, slot]  22 us
    all_to_all x1, starting transfers between devices, per_device(): lax.all_to_all(owned, ('dp', 'expert'), split_axis=0, concat_axis=0, tile...  14.3 us
    reduce_scatter x1, waiting for transfers between devices, per_device(): lax.psum_scatter(expert_part.astype(jnp.bfloat16), 'tensor', scatter_dime...  11.5 us
    gather x2, local copies, waits for them, and re-layouts, per_device(): normed[jnp.maximum(owner_rows, 0)]  10.5 us
  transfers between devices with their start and end apart: 4, of which 4 were waited for; matrix products, arithmetic and copies ran while one was open for 11% of the time, Pallas kernels for 0%

commit v1 on v0

--- a/solution.py
+++ b/solution.py
@@ -5,6 +5,7 @@
 
 D = 2048
 HEAD_WIDTH = 128
+CAP = 6
 
 
 def attend_local(queries, fresh_keys, fresh_values, resident_keys, resident_values):
@@ -35,14 +36,8 @@
     return attended.reshape(tokens_here, -1).astype(jnp.bfloat16)
 
 
-def expert_rows(block, gate_mat, up_mat, down_mat):
-    sources, items, width = block.shape
-    flat = block.reshape(sources * items, width)
-    gate_part = jnp.dot(flat, gate_mat, preferred_element_type=jnp.float32)
-    up_part = jnp.dot(flat, up_mat, preferred_element_type=jnp.float32)
-    act = (jax.nn.silu(gate_part) * up_part).astype(jnp.bfloat16)
-    result = jnp.dot(act, down_mat, preferred_element_type=jnp.float32)
-    return result.reshape(sources, items, -1)
+def swap_pair(x):
+    return lax.ppermute(x, "tensor", [(0, 1), (1, 0)])
 
 
 def per_device(
@@ -60,48 +55,56 @@
     w_up,
     w_down,
 ):
+    tokens_here = residual.shape[0]
+    lane = lax.axis_index("tensor")
+    half = D // lax.axis_size("tensor")
+    groups = lax.axis_size("dp")
     attended = attend_local(queries, fresh_keys, fresh_values, resident_keys, resident_values)
-    partial_sum = jnp.dot(
-        attended,
-        lax.all_gather(out_weight, "dp", axis=1, tiled=True),
-        preferred_element_type=jnp.float32,
-    )
-    tokens_here = residual.shape[0]
-    pairs = lax.axis_size("tensor")
-    half = D // pairs
-    lane = lax.axis_index("tensor")
-    summed = lax.psum(partial_sum.astype(jnp.bfloat16), "tensor").astype(jnp.float32)
+
+    gathered = lax.all_gather(attended, "dp", axis=0, tiled=True)
+    part = jnp.dot(gathered, out_weight, preferred_element_type=jnp.float32)
+    part = part.reshape(groups, tokens_here, -1)
+    mine = lax.all_to_all(part, "dp", split_axis=0, concat_axis=0, tiled=True)
+    mine = mine.transpose(1, 0, 2).reshape(tokens_here, D)
+    summed = mine + swap_pair(mine)
     hidden = residual.astype(jnp.float32) + summed
     mean_square = jnp.mean(hidden * hidden, axis=-1, keepdims=True)
     normed = (hidden * lax.rsqrt(mean_square + 1e-06) * norm_gain).astype(jnp.bfloat16)
     hidden_half = lax.dynamic_slice_in_dim(hidden, lane * half, half, 1)
+    normed_half = lax.dynamic_slice_in_dim(normed, lane * half, half, 1)
+
     owners = lax.axis_size("dp") * lax.axis_size("expert")
-    top = expert_ids.shape[1]
-    slots = max(2, tokens_here * top * 3 // (2 * owners))
     onehot = (expert_ids[:, :, None] == jnp.arange(owners)[None, None, :]).astype(jnp.int32)
     per_token = jnp.sum(onehot, axis=1)
     before = jnp.cumsum(per_token, axis=0) - per_token
     slot = jnp.sum(onehot * before[:, None, :], axis=-1)
-    token_rows = jnp.broadcast_to(
-        jnp.arange(tokens_here, dtype=jnp.int32)[:, None], expert_ids.shape
-    )
-    owner_rows = jnp.full((owners, slots), -1, jnp.int32).at[expert_ids, slot].set(token_rows)
-    valid = owner_rows >= 0
-    outgoing = jnp.where(
-        valid[:, :, None], normed[jnp.maximum(owner_rows, 0)], jnp.zeros((), jnp.bfloat16)
-    )
-    expert_part = expert_rows(
-        lax.all_to_all(outgoing, ("dp", "expert"), split_axis=0, concat_axis=0, tiled=True),
-        w_gate[0],
-        w_up[0],
-        w_down[0],
-    )
-    owned = lax.psum_scatter(
-        expert_part.astype(jnp.bfloat16), "tensor", scatter_dimension=2, tiled=True
-    )
-    returned = lax.all_to_all(owned, ("dp", "expert"), split_axis=0, concat_axis=0, tiled=True)
-    picked = returned[expert_ids, slot]
-    moe = jnp.sum(gates[:, :, None] * picked.astype(jnp.float32), axis=1)
+    code = expert_ids * CAP + slot
+    pick = (code[:, :, None] == jnp.arange(owners * CAP)[None, None, :]).astype(jnp.bfloat16)
+    spread = jnp.sum(pick, axis=1)
+    outgoing = jnp.einsum(
+        "tr,tf->rf", spread, normed_half, preferred_element_type=jnp.float32
+    ).astype(jnp.bfloat16)
+    received = lax.all_to_all(
+        outgoing.reshape(owners, CAP, half), ("dp", "expert"), split_axis=0, concat_axis=0, tiled=True
+    ).reshape(owners * CAP, half)
+    other = swap_pair(received)
+    first = jnp.where(lane == 0, received, other)
+    second = jnp.where(lane == 0, other, received)
+    flat = jnp.concatenate([first, second], axis=1)
+
+    gate_part = jnp.dot(flat, w_gate[0], preferred_element_type=jnp.float32)
+    up_part = jnp.dot(flat, w_up[0], preferred_element_type=jnp.float32)
+    act = (jax.nn.silu(gate_part) * up_part).astype(jnp.bfloat16)
+    result = jnp.dot(act, w_down[0], preferred_element_type=jnp.float32)
+    own = lax.dynamic_slice_in_dim(result, lane * half, half, 1)
+    theirs = lax.dynamic_slice_in_dim(result, (1 - lane) * half, half, 1)
+    expert_out = (own + swap_pair(theirs)).astype(jnp.bfloat16)
+
+    returned = lax.all_to_all(
+        expert_out.reshape(owners, CAP, half), ("dp", "expert"), split_axis=0, concat_axis=0, tiled=True
+    ).reshape(owners * CAP, half)
+    picked = jnp.einsum("tkr,rf->tkf", pick, returned, preferred_element_type=jnp.float32)
+    moe = jnp.sum(gates[:, :, None] * picked, axis=1)
     return (hidden_half + moe).astype(jnp.bfloat16)
 
 

time: 380 us -> 257 us (0.68)
  blocking collectives: 111 us -> 64.9 us
  waiting for transfers between devices: 144 us -> 98.8 us
  local copies, waits for them, and re-layouts: 60 us -> 28.1 us
  matrix products: 24.9 us -> 29.7 us
    all_to_all x1, blocking collectives: 111 us -> 64.9 us  [per_device(): lax.all_to_all(outgoing.reshape(owners, CAP, half), ('dp', 'expert'), spl...]
    psum x1 -> x0, waiting for transfers between devices: 29.8 us -> none  [per_device(): lax.psum(partial_sum.astype(jnp.bfloat16), 'tensor').astype(jnp.float32)]
    scatter x1 -> x0, local copies, waits for them, and re-layouts: 22 us -> none  [per_device(): jnp.full((owners, slots), -1, jnp.int32).at[expert_ids, slot]]
    all_gather x1, waiting for transfers between devices: 50.1 us -> 29.4 us  [per_device(): gathered = lax.all_gather(attended, 'dp', axis=0, tiled=True)]
    gather x3 -> x0, local copies, waits for them, and re-layouts: 18.4 us -> none  [the longest x2 10.5 us: per_device(): normed[jnp.maximum(owner_rows, 0)]]
    reduce_scatter x1 -> x0, waiting for transfers between devices: 11.5 us -> none  [per_device(): lax.psum_scatter(expert_part.astype(jnp.bfloat16), 'tensor', scatter_dime...]
    ppermute x0 -> x3, waiting for transfers between devices: none -> 9.27 us  [swap_pair(): return lax.ppermute(x, 'tensor', [(0, 1), (1, 0)])]
    reshape x1 -> x5, local copies, waits for them, and re-layouts: 6.33 us -> 14.8 us  [the longest x1 3.72 us: per_device(): received = lax.all_to_all(outgoing.reshape(owners, CAP, half), ('dp', 'ex...]
  transfers between devices with their start and end apart: 4 -> 6, of which waited for: 4 -> 5; matrix products, arithmetic and copies ran while one was open for 11% -> 1% of each run, Pallas kernels for 0% -> 0%
where the time goes in v1:
time: 257 us; the launch traced here: 256 us
  waiting for transfers between devices  98.8 us (38%)
  blocking collectives  64.9 us (25%)
  matrix products  29.7 us (12%)
  local copies, waits for them, and re-layouts  28.1 us (11%)
  between operations  13.6 us (5%)
  starting transfers between devices  12 us (5%)
  other arithmetic  9.14 us (4%)
    all_to_all x1, blocking collectives, per_device(): lax.all_to_all(outgoing.reshape(owners, CAP, half), ('dp', 'expert'), spl...  64.9 us
    all_to_all x1, waiting for transfers between devices, per_device(): lax.all_to_all(expert_out.reshape(owners, CAP, half), ('dp', 'expert'), s...  52.2 us
    all_gather x1, waiting for transfers between devices, per_device(): gathered = lax.all_gather(attended, 'dp', axis=0, tiled=True)  29.4 us
    dot_general x1, matrix products, per_device(): result = jnp.dot(act, w_down[0], preferred_element_type=jnp.float32)  9.28 us
    ppermute x3, waiting for transfers between devices, swap_pair(): return lax.ppermute(x, 'tensor', [(0, 1), (1, 0)])  9.27 us
    all_to_all x1, waiting for transfers between devices, per_device(): mine = lax.all_to_all(part, 'dp', split_axis=0, concat_axis=0, tiled=True)  7.95 us
    all_to_all x1, starting transfers between devices, per_device(): lax.all_to_all(expert_out.reshape(owners, CAP, half), ('dp', 'expert'), s...  7.93 us
    unnamed x34, local copies, waits for them, and re-layouts  6.45 us
  transfers between devices with their start and end apart: 6, of which 5 were waited for; matrix products, arithmetic and copies ran while one was open for 1% of the time, Pallas kernels for 0%

profile of v1, /device:TPU:32, one launch (start us, length us, event | category | flops | bytes accessed | tf_op | source)
XLA Modules:
  0.0 256.3 jit_solution(13007185668899665555)
XLA Ops:
  6.5 0.0 copy-start
  6.5 0.0 all-gather.2.cloned.1.call-start
  6.5 0.6 iota_add_fusion
  7.1 1.5 copy.47
  8.7 1.3 copy.48
  10.0 0.0 copy-done.5
  10.0 0.8 copy.62
  10.8 1.5 copy.44
  12.3 1.3 copy.45
  13.7 0.0 copy-done.8
  13.7 0.0 copy-done.9
  13.7 0.6 copy_bitcast_fusion.1
  14.3 0.8 fusion.27
  15.1 0.0 copy-done.6
  15.1 0.0 copy-start.4
  15.1 4.7 %fusion.48 = f32[2,8,64]{2,1,0:T(8,128)S(1)} fusion(pred[64,2112]{1,0:T(8,128)(4,1)S(1)} %fusion.27, bf16[64,2,128]{2,0,1:T(8,128)(2,1)} %get-tuple-element.9, bf16[2048,2,128]{2,0,1:T(8,128)(2,1)} %copy.48, bf16[64,2,8,128]{3,2,1,0:T(8,128)(2,1)S(1)} %bitcast.82), kind=kOutput, calls=%fused_computation.65 | convolution fusion | flops 564463680 | bytes 1482752 | tf_op jit(solution)/shard_map/sub | solution.py:31
  19.8 0.0 copy-done.4
  19.8 5.6 %fusion.14 = bf16[64,2,8,128]{3,0,2,1:T(8,128)(2,1)} fusion(f32[2,8,64]{2,1,0:T(8,128)S(1)} %fusion.48, bf16[64,2,128]{2,0,1:T(8,128)(2,1)} %get-tuple-element.10, bf16[2048,2,128]{2,0,1:T(8,128)(2,1)} %copy.45, pred[64,2112]{1,0:T(8,128)(4,1)S(1)} %fusion.27, bf16[64,2,128]{2,0,1:T(8,128)(2,1)} %get-tuple-element.9, ...), kind=kOutput, calls=%fused_computation.25 | convolution fusion | flops 1122569216 | bytes 2826240 | tf_op jit(solution)/shard_map/jgts,sjd->tjgd/dot_general | solution.py:33
  25.4 1.1 copy.51
  26.5 0.8 copy.78
  27.3 0.0 all-gather.2.cloned.1.call-update
  27.3 0.0 copy-start.10
  27.4 29.4 %all-gather.2.cloned.1.call-done = bf16[256,2048]{1,0:T(8,128)(2,1)} async-done(((bf16[64,2048]{1,0:T(8,128)(2,1)}), bf16[256,2048]{1,0:T(8,128)(2,1)}) %all-gather.2.cloned.1.call-update) | async-done | bytes 1048592 | tf_op jit(solution)/shard_map/all_gather | solution.py:64
  56.7 0.0 copy-done
  56.7 2.7 %fusion.51 = f32[256,512]{1,0:T(8,128)} fusion(bf16[256,2048]{1,0:T(8,128)(2,1)} %all-gather.2.cloned.1.call-done, bf16[2048,512]{1,0:T(8,128)(2,1)S(1)} %copy-done), kind=kOutput, calls=%fused_computation.66 | convolution fusion | flops 536870912 | bytes 3670016 | tf_op jit(solution)/shard_map/dot_general | solution.py:65
  59.5 3.6 %all-to-all-start = ((f32[4,64,512]{2,1,0:T(8,128)}), f32[4,64,512]{2,1,0:T(8,128)S(1)}, u32[]{:S(2)}, u32[]{:S(2)}) async-start(f32[4,64,512]{2,1,0:T(8,128)} %bitcast.8), calls=%async_computation | async-start | bytes 1048576 | tf_op jit(solution)/shard_map/all_to_all | solution.py:67
  63.1 0.0 copy-done.10
  63.1 0.1 copy.54
  63.2 8.0 %all-to-all-done = f32[4,64,512]{2,1,0:T(8,128)S(1)} async-done(((f32[4,64,512]{2,1,0:T(8,128)}), f32[4,64,512]{2,1,0:T(8,128)S(1)}, u32[]{:S(2)}, u32[]{:S(2)}) %all-to-all-start) | async-done | bytes 524320 | tf_op jit(solution)/shard_map/all_to_all | solution.py:67
  71.2 0.3 collective-permute-start
  71.5 0.1 convert_reduce_fusion
  71.6 0.1 reduce_window_sum.11
  71.7 1.2 select_reduce_fusion
  73.0 0.1 copy.55
  73.0 0.1 copy.56
  73.1 0.0 copy-done.12
  73.2 0.5 fusion.19
  73.7 0.0 collective-permute-done
  73.7 1.2 multiply_reduce_fusion.1
  75.0 1.8 convolution_convert_fusion
  76.7 3.7 %reshape.67 = bf16[128,6,1024]{2,1,0:T(8,128)(2,1)} reshape(bf16[768,1024]{1,0:T(8,128)(2,1)} %convolution_convert_fusion) | data formatting | bytes 3145728 | tf_op jit(solution)/shard_map/reshape | solution.py:88
  80.4 64.9 %all_to_all.15 = bf16[128,6,1024]{2,1,0:T(8,128)(2,1)} all-to-all(bf16[128,6,1024]{2,1,0:T(8,128)(2,1)} %reshape.67), channel_id=1, replica_groups=mesh['dp'=4,'expert'=32,'tensor'=2] {'dp','expert'}, dimensions={0} | all-to-all | bytes 3145728 | tf_op jit(solution)/shard_map/all_to_all | solution.py:87
  145.4 3.7 %reshape.68 = bf16[768,1024]{1,0:T(8,128)(2,1)} reshape(bf16[128,6,1024]{2,1,0:T(8,128)(2,1)} %all_to_all.15) | data formatting | bytes 3145728 | tf_op jit(solution)/shard_map/reshape | solution.py:89
  149.1 0.0 collective-permute-start.1
  149.1 3.7 %collective-permute-done.1 = bf16[768,1024]{1,0:T(8,128)(2,1)} collective-permute-done((bf16[768,1024]{1,0:T(8,128)(2,1)}, bf16[768,1024]{1,0:T(8,128)(2,1)}, u32[]{:S(2)}, u32[]{:S(2)}) %collective-permute-start.1) | collective-permute-done | bytes 1572896 | tf_op jit(solution)/shard_map/ppermute | solution.py:40
  152.8 2.1 broadcast_select_fusion.1
  154.9 0.0 copy-start.2
  154.9 0.0 copy-start.3
  154.9 1.2 copy-done.2
  156.2 0.4 copy-done.3
  156.6 2.8 %fusion.6 = f32[768,384]{1,0:T(8,128)} fusion(bf16[768,1024]{1,0:T(8,128)(2,1)S(1)} %get-tuple-element.8, bf16[768,1024]{1,0:T(8,128)(2,1)S(1)} %get-tuple-element.7, bf16[1,2048,384]{2,1,0:T(8,128)(2,1)S(1)} %copy-done.13), kind=kOutput, calls=%fused_computation.12 | convolution fusion | flops 1214251008 | bytes 5898240 | tf_op jit(solution)/shard_map/dot_general | solution.py:96
  159.3 9.3 %fusion.8 = f32[768,2048]{1,0:T(8,128)} fusion(bf16[1,384,2048]{2,1,0:T(8,128)(2,1)} %param.25, f32[768,384]{1,0:T(8,128)} %fusion.6, bf16[768,1024]{1,0:T(8,128)(2,1)} %copy-done.3, bf16[768,1024]{1,0:T(8,128)(2,1)} %copy-done.2, bf16[1,2048,384]{2,1,0:T(8,128)(2,1)} %param.23), kind=kOutput, calls=%fused_computation.15 | convolution fusion | flops 2423980032 | bytes 13762560 | tf_op jit(solution)/shard_map/dot_general | solution.py:98
  168.6 2.3 constant_dynamic-slice_fusion
  170.9 0.2 collective-permute-start.2
  171.1 5.5 %collective-permute-done.2 = f32[768,1024]{1,0:T(8,128)S(1)} collective-permute-done((f32[768,1024]{1,0:T(8,128)S(1)}, f32[768,1024]{1,0:T(8,128)S(1)}, u32[]{:S(2)}, u32[]{:S(2)}) %collective-permute-start.2) | collective-permute-done | bytes 3145760 | tf_op jit(solution)/shard_map/ppermute | solution.py:40
  176.6 0.0 copy-done.1
  176.6 1.7 add_convert_fusion
  178.3 3.7 %reshape.69 = bf16[128,6,1024]{2,1,0:T(8,128)(2,1)} reshape(bf16[768,1024]{1,0:T(8,128)(2,1)} %add_convert_fusion) | data formatting | bytes 3145728 | tf_op jit(solution)/shard_map/reshape | solution.py:104
  182.0 7.9 %all-to-all-start.2 = ((bf16[128,6,1024]{2,1,0:T(8,128)(2,1)}), bf16[128,6,1024]{2,1,0:T(8,128)(2,1)}, u32[]{:S(2)}, u32[]{:S(2)}) async-start(bf16[128,6,1024]{2,1,0:T(8,128)(2,1)} %reshape.69), calls=%async_computation.2 | async-start | bytes 4194304 | tf_op jit(solution)/shard_map/all_to_all | solution.py:103
  190.0 0.1 copy.53
  190.0 52.2 %all-to-all-done.2 = bf16[128,6,1024]{2,1,0:T(8,128)(2,1)} async-done(((bf16[128,6,1024]{2,1,0:T(8,128)(2,1)}), bf16[128,6,1024]{2,1,0:T(8,128)(2,1)}, u32[]{:S(2)}, u32[]{:S(2)}) %all-to-all-start.2) | async-done | bytes 1572896 | tf_op jit(solution)/shard_map/all_to_all | solution.py:103
  242.2 3.7 %reshape.73 = bf16[768,1024,1]{1,0,2:T(8,128)(2,1)} reshape(bf16[128,6,1024]{2,1,0:T(8,128)(2,1)} %all-to-all-done.2) | data formatting | bytes 3145728 | tf_op jit(solution)/shard_map/reshape | solution.py:105
  246.0 2.8 %multiply_reduce_fusion = f32[64,1024]{1,0:T(8,128)S(1)} fusion(bf16[768,1024,1]{1,0,2:T(8,128)(2,1)} %reshape.73, f32[64,8]{1,0:T(8,128)S(1)} %copy.53, s32[64,8]{1,0:T(8,128)S(1)} %copy.56), kind=kOutput, calls=%fused_computation.11 | convolution fusion | flops 806682624 | bytes 1839104 | tf_op jit(solution)/shard_map/tkr,rf->tkf/dot_general | solution.py:106
  248.8 0.7 add_convert_fusion.1
  (18 shorter events, 0.1 us)
Async XLA Ops:
  6.5 50.2 %copy-start = (bf16[2048,512]{1,0:T(8,128)(2,1)S(1)}, bf16[2048,512]{1,0:T(8,128)(2,1)}, u32[]{:S(2)}) copy-start(bf16[2048,512]{1,0:T(8,128)(2,1)} %param.18) | copy-start | bytes 6291460
  6.5 50.2 %all-gather.2.cloned.1.call-start = ((), (), s32[]{:S(2)}) async-start(), calls=%async_computation.3 | async-start | bytes 1310720 | tf_op jit(solution)/shard_map/all_gather | solution.py:64
  7.1 2.9 %copy-start.5 = (bf16[64,2048]{1,0:T(8,128)(2,1)S(1)}, bf16[64,2048]{1,0:T(8,128)(2,1)}, u32[]{:S(2)}) copy-start(bf16[64,2048]{1,0:T(8,128)(2,1)} %param.13) | copy-start | bytes 786436
  10.8 2.9 %copy-start.8 = (bf16[64,256]{1,0:T(8,128)(2,1)S(1)}, bf16[64,256]{1,0:T(8,128)(2,1)}, u32[]{:S(2)}) copy-start(bf16[64,256]{1,0:T(8,128)(2,1)} %param.15) | copy-start | bytes 98308
  10.8 2.9 %copy-start.9 = (bf16[64,256]{1,0:T(8,128)(2,1)S(1)}, bf16[64,256]{1,0:T(8,128)(2,1)}, u32[]{:S(2)}) copy-start(bf16[64,256]{1,0:T(8,128)(2,1)} %param.14) | copy-start | bytes 98308
  10.8 4.3 %copy-start.6 = (bf16[8,8,16,128]{3,2,1,0:T(8,128)(2,1)S(1)}, bf16[8,8,16,128]{3,2,1,0:T(8,128)(2,1)}, u32[]{:S(2)}) copy-start(bf16[8,8,16,128]{3,2,1,0:T(8,128)(2,1)} %copy.62) | copy-start | bytes 786436
  15.1 4.7 %copy-start.4 = (bf16[2048,2,128]{2,0,1:T(8,128)(2,1)S(1)}, bf16[2048,2,128]{2,0,1:T(8,128)(2,1)}, u32[]{:S(2)}) copy-start(bf16[2048,2,128]{2,0,1:T(8,128)(2,1)} %copy.48) | copy-start | bytes 3145732
  27.3 35.8 %copy-start.10 = (s32[64,8]{0,1:T(8,128)S(1)}, s32[64,8]{0,1:T(8,128)}, u32[]{:S(2)}) copy-start(s32[64,8]{0,1:T(8,128)} %param.21) | copy-start | bytes 6148
  59.5 13.7 %copy-start.12 = (f32[2048]{0:T(1024)S(1)}, f32[2048]{0:T(1024)}, u32[]{:S(2)}) copy-start(f32[2048]{0:T(1024)} %param.20) | copy-start | bytes 24580
  59.5 14.2 %copy-start.7 = (bf16[64,2048]{1,0:T(8,128)(2,1)S(1)}, bf16[64,2048]{1,0:T(8,128)(2,1)}, u32[]{:S(2)}) copy-start(bf16[64,2048]{1,0:T(8,128)(2,1)} %param.19) | copy-start | bytes 786436
  59.5 11.7 %all-to-all-start = ((f32[4,64,512]{2,1,0:T(8,128)}), f32[4,64,512]{2,1,0:T(8,128)S(1)}, u32[]{:S(2)}, u32[]{:S(2)}) async-start(f32[4,64,512]{2,1,0:T(8,128)} %bitcast.8), calls=%async_computation | async-start | bytes 1048576 | tf_op jit(solution)/shard_map/all_to_all | solution.py:67
  71.2 2.5 collective-permute-start
  149.1 3.8 %collective-permute-start.1 = (bf16[768,1024]{1,0:T(8,128)(2,1)}, bf16[768,1024]{1,0:T(8,128)(2,1)}, u32[]{:S(2)}, u32[]{:S(2)}) collective-permute-start(bf16[768,1024]{1,0:T(8,128)(2,1)} %reshape.68), channel_id=1, source_target_pairs={{0,1},{1,0},{2,3},{3,2},{4,5},{5,4},{6,7},{7,6},{8,9},{9,8},{10,11... | collective-permute-start | bytes 4718600 | tf_op jit(solution)/shard_map/ppermute | solution.py:40
  149.1 7.5 %copy-start.13 = (bf16[1,2048,384]{2,1,0:T(8,128)(2,1)S(1)}, bf16[1,2048,384]{2,1,0:T(8,128)(2,1)}, u32[]{:S(2)}) copy-start(bf16[1,2048,384]{2,1,0:T(8,128)(2,1)} %param.24) | copy-start | bytes 4718596
  154.9 1.2 copy-start.2
  154.9 1.6 copy-start.3
  168.6 8.0 %copy-start.1 = (f32[768,2048]{1,0:T(8,128)S(1)}, f32[768,2048]{1,0:T(8,128)}, u32[]{:S(2)}) copy-start(f32[768,2048]{1,0:T(8,128)} %fusion.8) | copy-start | bytes 18874372
  170.9 5.7 %collective-permute-start.2 = (f32[768,1024]{1,0:T(8,128)S(1)}, f32[768,1024]{1,0:T(8,128)S(1)}, u32[]{:S(2)}, u32[]{:S(2)}) collective-permute-start(f32[768,1024]{1,0:T(8,128)S(1)} %constant_dynamic-slice_fusion), channel_id=1, source_target_pairs={{0,1},{1,0},{2,3},{3,2},{4,5},{5,4},{6,7},{7,6},{8,9},{9,8},{10,11... | collective-permute-start | bytes 9437192 | tf_op jit(solution)/shard_map/ppermute | solution.py:40
  182.0 7.9 %copy-start.11 = (f32[64,8]{0,1:T(8,128)S(1)}, f32[64,8]{0,1:T(8,128)}, u32[]{:S(2)}) copy-start(f32[64,8]{0,1:T(8,128)} %param.22) | copy-start | bytes 6148
  182.0 60.2 %all-to-all-start.2 = ((bf16[128,6,1024]{2,1,0:T(8,128)(2,1)}), bf16[128,6,1024]{2,1,0:T(8,128)(2,1)}, u32[]{:S(2)}, u32[]{:S(2)}) async-start(bf16[128,6,1024]{2,1,0:T(8,128)(2,1)} %reshape.69), calls=%async_computation.2 | async-start | bytes 4194304 | tf_op jit(solution)/shard_map/all_to_all | solution.py:103
Sparse Core Ops, SparseCore 0:
  27.5 29.2 all-gather.1

commit v2 on v1

--- a/solution.py
+++ b/solution.py
@@ -61,11 +61,17 @@
     groups = lax.axis_size("dp")
     attended = attend_local(queries, fresh_keys, fresh_values, resident_keys, resident_values)
 
-    gathered = lax.all_gather(attended, "dp", axis=0, tiled=True)
-    part = jnp.dot(gathered, out_weight, preferred_element_type=jnp.float32)
-    part = part.reshape(groups, tokens_here, -1)
-    mine = lax.all_to_all(part, "dp", split_axis=0, concat_axis=0, tiled=True)
-    mine = mine.transpose(1, 0, 2).reshape(tokens_here, D)
+    here = lax.axis_index("dp")
+    blocks = [jnp.dot(attended, out_weight, preferred_element_type=jnp.float32)]
+    for shift in range(1, groups):
+        onward = [(i, (i + shift) % groups) for i in range(groups)]
+        backward = [(i, (i - shift) % groups) for i in range(groups)]
+        arrived = lax.ppermute(attended, "dp", onward)
+        product = jnp.dot(arrived, out_weight, preferred_element_type=jnp.float32)
+        blocks.append(lax.ppermute(product, "dp", backward))
+    stacked = jnp.stack(blocks)
+    order = (jnp.arange(groups) - here) % groups
+    mine = stacked[order].transpose(1, 0, 2).reshape(tokens_here, D)
     summed = mine + swap_pair(mine)
     hidden = residual.astype(jnp.float32) + summed
     mean_square = jnp.mean(hidden * hidden, axis=-1, keepdims=True)
@@ -81,30 +87,39 @@
     code = expert_ids * CAP + slot
     pick = (code[:, :, None] == jnp.arange(owners * CAP)[None, None, :]).astype(jnp.bfloat16)
     spread = jnp.sum(pick, axis=1)
+    lanes = 128
+    width = half // lanes
     outgoing = jnp.einsum(
-        "tr,tf->rf", spread, normed_half, preferred_element_type=jnp.float32
+        "tr,tjl->rjl", spread, normed_half.reshape(tokens_here, width, lanes),
+        preferred_element_type=jnp.float32,
     ).astype(jnp.bfloat16)
     received = lax.all_to_all(
-        outgoing.reshape(owners, CAP, half), ("dp", "expert"), split_axis=0, concat_axis=0, tiled=True
-    ).reshape(owners * CAP, half)
+        outgoing.reshape(owners, CAP * width, lanes), ("dp", "expert"), split_axis=0, concat_axis=0, tiled=True
+    ).reshape(owners * CAP, width, lanes)
     other = swap_pair(received)
     first = jnp.where(lane == 0, received, other)
     second = jnp.where(lane == 0, other, received)
     flat = jnp.concatenate([first, second], axis=1)
 
-    gate_part = jnp.dot(flat, w_gate[0], preferred_element_type=jnp.float32)
-    up_part = jnp.dot(flat, w_up[0], preferred_element_type=jnp.float32)
+    gate_part = jnp.einsum(
+        "rjl,jlh->rh", flat, w_gate[0].reshape(2 * width, lanes, -1), preferred_element_type=jnp.float32
+    )
+    up_part = jnp.einsum(
+        "rjl,jlh->rh", flat, w_up[0].reshape(2 * width, lanes, -1), preferred_element_type=jnp.float32
+    )
     act = (jax.nn.silu(gate_part) * up_part).astype(jnp.bfloat16)
-    result = jnp.dot(act, w_down[0], preferred_element_type=jnp.float32)
-    own = lax.dynamic_slice_in_dim(result, lane * half, half, 1)
-    theirs = lax.dynamic_slice_in_dim(result, (1 - lane) * half, half, 1)
+    result = jnp.einsum(
+        "rh,hjl->rjl", act, w_down[0].reshape(act.shape[1], 2 * width, lanes), preferred_element_type=jnp.float32
+    )
+    own = lax.dynamic_slice_in_dim(result, lane * width, width, 1)
+    theirs = lax.dynamic_slice_in_dim(result, (1 - lane) * width, width, 1)
     expert_out = (own + swap_pair(theirs)).astype(jnp.bfloat16)
 
     returned = lax.all_to_all(
-        expert_out.reshape(owners, CAP, half), ("dp", "expert"), split_axis=0, concat_axis=0, tiled=True
-    ).reshape(owners * CAP, half)
-    picked = jnp.einsum("tkr,rf->tkf", pick, returned, preferred_element_type=jnp.float32)
-    moe = jnp.sum(gates[:, :, None] * picked, axis=1)
+        expert_out.reshape(owners, CAP * width, lanes), ("dp", "expert"), split_axis=0, concat_axis=0, tiled=True
+    ).reshape(owners * CAP, width, lanes)
+    picked = jnp.einsum("tkr,rjl->tkjl", pick, returned, preferred_element_type=jnp.float32)
+    moe = jnp.sum(gates[:, :, None, None] * picked, axis=1).reshape(tokens_here, half)
     return (hidden_half + moe).astype(jnp.bfloat16)
 
 

time: 257 us -> 189 us (0.74)
  waiting for transfers between devices: 98.8 us -> 58.1 us
  between operations: 13.6 us -> 0.37 us
  matrix products: 29.7 us -> 21 us
  blocking collectives: 64.9 us -> 56.8 us
  starting transfers between devices: 12 us -> 19.8 us
  local copies, waits for them, and re-layouts: 28.1 us -> 20.6 us
  other arithmetic: 9.14 us -> 11.9 us
    all_gather x1 -> x0, waiting for transfers between devices: 29.4 us -> none  [per_device(): gathered = lax.all_gather(attended, 'dp', axis=0, tiled=True)]
    all_to_all x2 -> x1, waiting for transfers between devices: 60.2 us -> 41.3 us  [per_device(): lax.all_to_all(expert_out.reshape(owners, CAP * width, lanes), ('dp', 'ex...]
    reshape x5 -> x2, local copies, waits for them, and re-layouts: 14.8 us -> 1.61 us  [the longest x1 1.57 us: per_device(): received = lax.all_to_all(outgoing.reshape(owners, CAP * width, lanes), (...]
    ppermute x0 -> x6, starting transfers between devices: none -> 11.9 us  [the longest x3 6.72 us: per_device(): blocks.append(lax.ppermute(product, 'dp', backward))]
    ppermute x0 -> x6, waiting for transfers between devices: none -> 10.3 us  [the longest x3 7.3 us: per_device(): arrived = lax.ppermute(attended, 'dp', onward)]
    dot_general x5 -> x9, matrix products: 19.4 us -> 10.7 us  [the longest x1 2.78 us: per_device(): jnp.einsum('tkr,rjl->tkjl', pick, returned, preferred_element_type=jnp.fl...]
    all_to_all x1, blocking collectives: 64.9 us -> 56.8 us  [per_device(): lax.all_to_all(outgoing.reshape(owners, CAP * width, lanes), ('dp', 'expe...]
    all_to_all x2 -> x1, starting transfers between devices: 11.5 us -> 7.65 us  [per_device(): lax.all_to_all(expert_out.reshape(owners, CAP * width, lanes), ('dp', 'ex...]
  transfers between devices with their start and end apart: 6 -> 10, of which waited for: 5 -> 7; matrix products, arithmetic and copies ran while one was open for 1% -> 4% of each run, Pallas kernels for 0% -> 0%
where the time goes in v2:
time: 189 us
  waiting for transfers between devices  58.1 us (31%)
  blocking collectives  56.8 us (30%)
  matrix products  21 us (11%)
  local copies, waits for them, and re-layouts  20.6 us (11%)
  starting transfers between devices  19.8 us (10%)
  other arithmetic  11.9 us (6%)
    all_to_all x1, blocking collectives, per_device(): lax.all_to_all(outgoing.reshape(owners, CAP * width, lanes), ('dp', 'expe...  56.8 us
    all_to_all x1, waiting for transfers between devices, per_device(): lax.all_to_all(expert_out.reshape(owners, CAP * width, lanes), ('dp', 'ex...  41.3 us
    unnamed x39, local copies, waits for them, and re-layouts  8.63 us
    all_to_all x1, starting transfers between devices, per_device(): lax.all_to_all(expert_out.reshape(owners, CAP * width, lanes), ('dp', 'ex...  7.65 us
    ppermute x3, waiting for transfers between devices, per_device(): arrived = lax.ppermute(attended, 'dp', onward)  7.3 us
    ppermute x3, starting transfers between devices, per_device(): blocks.append(lax.ppermute(product, 'dp', backward))  6.72 us
    ppermute x3, waiting for transfers between devices, swap_pair(): return lax.ppermute(x, 'tensor', [(0, 1), (1, 0)])  6.58 us
    dot_general x1, matrix products, attend_local(): jnp.einsum('jgts,sjd->tjgd', probs, joined_values, preferred_element_type...  5.64 us
  transfers between devices with their start and end apart: 10, of which 7 were waited for; matrix products, arithmetic and copies ran while one was open for 4% of the time, Pallas kernels for 0%

profile of v2, /device:TPU:32, one launch (start us, length us, event | category | flops | bytes accessed | tf_op | source)
XLA Modules:
  0.0 188.5 jit_solution(11918787786018424103)
XLA Ops:
  0.0 0.6 iota_add_fusion
  0.6 1.5 copy.63
  2.1 0.0 copy-start.5
  2.1 1.3 copy.64
  3.5 0.8 copy.88
  4.2 1.5 copy.60
  5.7 0.0 copy-start.10
  5.7 0.0 copy-start.11
  5.7 1.3 copy.61
  7.1 0.6 copy_bitcast_fusion.1
  7.7 0.8 fusion.27
  8.5 4.7 %fusion.51 = f32[2,8,64]{2,1,0:T(8,128)S(1)} fusion(pred[64,2112]{1,0:T(8,128)(4,1)S(1)} %fusion.27, bf16[64,2,128]{2,0,1:T(8,128)(2,1)} %get-tuple-element.9, bf16[2048,2,128]{2,0,1:T(8,128)(2,1)} %copy.64, bf16[64,2,8,128]{3,2,1,0:T(8,128)(2,1)S(1)} %bitcast.129), kind=kOutput, calls=%fused_computation.80 | convolution fusion | flops 564463680 | bytes 1482752 | tf_op jit(solution)/shard_map/sub | solution.py:31
  13.2 5.6 %fusion.18 = bf16[64,2,8,128]{3,0,2,1:T(8,128)(2,1)} fusion(f32[2,8,64]{2,1,0:T(8,128)S(1)} %fusion.51, bf16[64,2,128]{2,0,1:T(8,128)(2,1)} %get-tuple-element.10, bf16[2048,2,128]{2,0,1:T(8,128)(2,1)} %copy.61, pred[64,2112]{1,0:T(8,128)(4,1)S(1)} %fusion.27, bf16[64,2,128]{2,0,1:T(8,128)(2,1)} %get-tuple-element.9, ...), kind=kOutput, calls=%fused_computation.29 | convolution fusion | flops 1122569216 | bytes 2826240 | tf_op jit(solution)/shard_map/jgts,sjd->tjgd/dot_general | solution.py:33
  18.8 1.1 copy.67
  19.9 0.1 copy.120
  20.0 3.1 %collective-permute-start.2 = (bf16[64,2048]{1,0:T(8,128)(2,1)S(1)}, bf16[64,2048]{1,0:T(8,128)(2,1)S(1)}, u32[]{:S(2)}, u32[]{:S(2)}) collective-permute-start(bf16[64,2048]{1,0:T(8,128)(2,1)S(1)} %bitcast.126), channel_id=1, source_target_pairs={{0,128},{64,192},{128,0},{192,64},{1,129},{65,193},{129,1},{193,65... | collective-permute-start | bytes 786440 | tf_op jit(solution)/shard_map/ppermute | solution.py:69
  23.1 1.1 collective-permute-start.4
  24.3 0.9 collective-permute-start
  25.1 0.4 convolution_bitcast_fusion
  25.6 5.2 %collective-permute-done.2 = bf16[64,2048]{1,0:T(8,128)(2,1)S(1)} collective-permute-done((bf16[64,2048]{1,0:T(8,128)(2,1)S(1)}, bf16[64,2048]{1,0:T(8,128)(2,1)S(1)}, u32[]{:S(2)}, u32[]{:S(2)}) %collective-permute-start.2) | collective-permute-done | bytes 262176 | tf_op jit(solution)/shard_map/ppermute | solution.py:69
  30.8 0.5 fusion.55
  31.3 3.1 %collective-permute-start.3 = (f32[64,512]{1,0:T(8,128)S(1)}, f32[64,512]{1,0:T(8,128)S(1)}, u32[]{:S(2)}, u32[]{:S(2)}) collective-permute-start(f32[64,512]{1,0:T(8,128)S(1)} %fusion.55), channel_id=1, source_target_pairs={{0,128},{64,192},{128,0},{192,64},{1,129},{65,193},{129,1},{193,65... | collective-permute-start | bytes 393224 | tf_op jit(solution)/shard_map/ppermute | solution.py:71
  34.4 2.1 %collective-permute-done.4 = bf16[64,2048]{1,0:T(8,128)(2,1)S(1)} collective-permute-done((bf16[64,2048]{1,0:T(8,128)(2,1)S(1)}, bf16[64,2048]{1,0:T(8,128)(2,1)S(1)}, u32[]{:S(2)}, u32[]{:S(2)}) %collective-permute-start.4) | collective-permute-done | bytes 262176 | tf_op jit(solution)/shard_map/ppermute | solution.py:69
  36.5 0.5 fusion.56
  37.0 0.0 copy-start.12
  37.0 1.6 collective-permute-start.5
  38.6 0.5 fusion.54
  39.1 2.0 %collective-permute-start.1 = (f32[64,512]{1,0:T(8,128)S(1)}, f32[64,512]{1,0:T(8,128)S(1)}, u32[]{:S(2)}, u32[]{:S(2)}) collective-permute-start(f32[64,512]{1,0:T(8,128)S(1)} %fusion.54), channel_id=1, source_target_pairs={{0,192},{64,0},{128,64},{192,128},{1,193},{65,1},{129,65},{193,129... | collective-permute-start | bytes 393224 | tf_op jit(solution)/shard_map/ppermute | solution.py:71
  41.1 0.1 copy.70
  41.2 2.3 %collective-permute-done.5 = f32[64,512]{1,0:T(8,128)S(1)} collective-permute-done((f32[64,512]{1,0:T(8,128)S(1)}, f32[64,512]{1,0:T(8,128)S(1)}, u32[]{:S(2)}, u32[]{:S(2)}) %collective-permute-start.5) | collective-permute-done | bytes 131104 | tf_op jit(solution)/shard_map/ppermute | solution.py:71
  43.5 0.7 collective-permute-done.1
  44.2 1.0 pad_maximum_fusion.7
  45.2 0.0 copy-start.7
  45.2 0.6 gather_fusion
  45.8 0.1 collective-permute-start.6
  45.9 0.1 convert_reduce_fusion
  46.1 0.1 reduce_window_sum.11
  46.2 1.2 select_reduce_fusion
  47.5 0.1 copy.71
  47.5 0.1 copy.72
  47.6 0.5 fusion.23
  48.2 1.2 multiply_reduce_fusion.1
  49.4 0.6 convolution_convert_fusion
  50.1 1.0 copy.74
  51.1 56.8 %all_to_all.10 = bf16[128,48,128]{2,1,0:T(8,128)(2,1)S(1)} all-to-all(bf16[128,48,128]{2,1,0:T(8,128)(2,1)S(1)} %bitcast.116), channel_id=1, replica_groups=mesh['dp'=4,'expert'=32,'tensor'=2] {'dp','expert'}, dimensions={0} | all-to-all | bytes 3145728 | tf_op jit(solution)/shard_map/all_to_all | solution.py:96
  107.8 1.6 copy.76
  109.4 0.0 copy-done.2
  109.5 3.0 %copy.90 = bf16[48,8,16,128]{3,2,1,0:T(8,128)(2,1)} copy(bf16[48,8,16,128]{3,1,2,0:T(8,128)(2,1)} %bitcast.124) | data formatting | bytes 3145728
  112.4 0.8 collective-permute-done.7
  113.2 2.4 %broadcast_select_fusion.1 = (bf16[768,8,128]{2,0,1:T(8,128)(2,1)S(1)}, bf16[768,8,128]{2,0,1:T(8,128)(2,1)S(1)}) fusion(bf16[768,8,128]{2,0,1:T(8,128)(2,1)} %collective-permute-done.7, pred[]{:T(512)S(6)} %eq.38, bf16[768,8,128]{2,1,0:T(8,128)(2,1)} %bitcast.113), kind=kLoop, calls=%fused_computation.24 | loop fusion | flops 1572864 | bytes 6291457 | tf_op jit(solution)/shard_map/jit(_where)/select_n | solution.py:100
  115.6 1.8 fusion.15
  117.4 1.8 fusion.16
  119.2 1.8 fusion.10
  121.1 2.0 %constant_dynamic-slice_fusion = f32[768,8,128]{2,0,1:T(8,128)} fusion(f32[768,16,128]{2,0,1:T(8,128)S(1)} %fusion.10, s32[]{:T(128)S(6)} %select_n.58), kind=kLoop, calls=%fused_computation.68 | loop fusion | bytes 6291460 | tf_op jit(solution)/shard_map/dynamic_slice | solution.py:115
  123.1 1.6 copy-done.1
  124.6 0.2 collective-permute-start.8
  124.8 5.8 %collective-permute-done.8 = f32[768,8,128]{2,0,1:T(8,128)} collective-permute-done((f32[768,8,128]{2,0,1:T(8,128)}, f32[768,8,128]{2,0,1:T(8,128)}, u32[]{:S(2)}, u32[]{:S(2)}) %collective-permute-start.8) | collective-permute-done | bytes 3145760 | tf_op jit(solution)/shard_map/ppermute | solution.py:40
  130.7 3.2 %add_convert_fusion = bf16[768,8,128]{2,0,1:T(8,128)(2,1)S(1)} fusion(f32[768,8,128]{2,0,1:T(8,128)} %collective-permute-done.8, f32[768,16,128]{2,0,1:T(8,128)} %copy-done.1, s32[]{:T(128)S(6)} %select_n.57), kind=kLoop, calls=%fused_computation.11 | loop fusion | flops 1572864 | bytes 7864324 | tf_op jit(solution)/shard_map/convert_element_type | solution.py:116
  133.8 2.2 %copy.79 = bf16[768,8,128]{2,1,0:T(8,128)(2,1)} copy(bf16[768,8,128]{2,0,1:T(8,128)(2,1)S(1)} %add_convert_fusion) | data formatting | bytes 3145728 | tf_op jit(solution)/shard_map/convert_element_type | solution.py:116
  136.0 7.7 %all-to-all-start.1 = ((bf16[128,48,128]{2,1,0:T(8,128)(2,1)}), bf16[128,48,128]{2,1,0:T(8,128)(2,1)}, u32[]{:S(2)}, u32[]{:S(2)}) async-start(bf16[128,48,128]{2,1,0:T(8,128)(2,1)} %bitcast.115), calls=%async_computation.1 | async-start | bytes 3145728 | tf_op jit(solution)/shard_map/all_to_all | solution.py:118
  143.6 0.1 copy.69
  143.7 41.3 %all-to-all-done.1 = bf16[128,48,128]{2,1,0:T(8,128)(2,1)} async-done(((bf16[128,48,128]{2,1,0:T(8,128)(2,1)}), bf16[128,48,128]{2,1,0:T(8,128)(2,1)}, u32[]{:S(2)}, u32[]{:S(2)}) %all-to-all-start.1) | async-done | bytes 1572896 | tf_op jit(solution)/shard_map/all_to_all | solution.py:118
  185.0 2.8 %multiply_reduce_fusion = f32[64,8,128]{2,1,0:T(8,128)S(1)} fusion(bf16[768,8,128]{2,1,0:T(8,128)(2,1)} %bitcast.25, f32[64,8]{1,0:T(8,128)S(1)} %copy.69, s32[64,8]{1,0:T(8,128)S(1)} %copy.72), kind=kOutput, calls=%fused_computation.12 | convolution fusion | flops 806682624 | bytes 1839104 | tf_op jit(solution)/shard_map/tkr,rjl->tkjl/dot_general | solution.py:121
  187.8 0.7 fusion.28
  (38 shorter events, 0.1 us)
Async XLA Ops:
  0.0 25.1 %copy-start = (bf16[2048,512]{1,0:T(8,128)(2,1)S(1)}, bf16[2048,512]{1,0:T(8,128)(2,1)}, u32[]{:S(2)}) copy-start(bf16[2048,512]{1,0:T(8,128)(2,1)} %param.18) | copy-start | bytes 6291460
  2.1 1.3 copy-start.5
  5.7 1.4 copy-start.10
  5.7 1.4 copy-start.11
  5.7 2.8 %copy-start.6 = (bf16[8,8,16,128]{3,2,1,0:T(8,128)(2,1)S(1)}, bf16[8,8,16,128]{3,2,1,0:T(8,128)(2,1)}, u32[]{:S(2)}) copy-start(bf16[8,8,16,128]{3,2,1,0:T(8,128)(2,1)} %copy.88) | copy-start | bytes 786436
  8.5 4.7 %copy-start.4 = (bf16[2048,2,128]{2,0,1:T(8,128)(2,1)S(1)}, bf16[2048,2,128]{2,0,1:T(8,128)(2,1)}, u32[]{:S(2)}) copy-start(bf16[2048,2,128]{2,0,1:T(8,128)(2,1)} %copy.64) | copy-start | bytes 3145732
  20.0 10.8 %collective-permute-start.2 = (bf16[64,2048]{1,0:T(8,128)(2,1)S(1)}, bf16[64,2048]{1,0:T(8,128)(2,1)S(1)}, u32[]{:S(2)}, u32[]{:S(2)}) collective-permute-start(bf16[64,2048]{1,0:T(8,128)(2,1)S(1)} %bitcast.126), channel_id=1, source_target_pairs={{0,128},{64,192},{128,0},{192,64},{1,129},{65,193},{129,1},{193,65... | collective-permute-start | bytes 786440 | tf_op jit(solution)/shard_map/ppermute | solution.py:69
  23.1 13.4 %collective-permute-start.4 = (bf16[64,2048]{1,0:T(8,128)(2,1)S(1)}, bf16[64,2048]{1,0:T(8,128)(2,1)S(1)}, u32[]{:S(2)}, u32[]{:S(2)}) collective-permute-start(bf16[64,2048]{1,0:T(8,128)(2,1)S(1)} %bitcast.127), channel_id=1, source_target_pairs={{0,192},{64,0},{128,64},{192,128},{1,193},{65,1},{129,65},{193,129... | collective-permute-start | bytes 786440 | tf_op jit(solution)/shard_map/ppermute | solution.py:69
  24.3 14.3 %collective-permute-start = (bf16[64,2048]{1,0:T(8,128)(2,1)S(1)}, bf16[64,2048]{1,0:T(8,128)(2,1)S(1)}, u32[]{:S(2)}, u32[]{:S(2)}) collective-permute-start(bf16[64,2048]{1,0:T(8,128)(2,1)S(1)} %bitcast.128), channel_id=1, source_target_pairs={{0,64},{64,128},{128,192},{192,0},{1,65},{65,129},{129,193},{193,1... | collective-permute-start | bytes 786440 | tf_op jit(solution)/shard_map/ppermute | solution.py:69
  31.3 9.9 %collective-permute-start.3 = (f32[64,512]{1,0:T(8,128)S(1)}, f32[64,512]{1,0:T(8,128)S(1)}, u32[]{:S(2)}, u32[]{:S(2)}) collective-permute-start(f32[64,512]{1,0:T(8,128)S(1)} %fusion.55), channel_id=1, source_target_pairs={{0,128},{64,192},{128,0},{192,64},{1,129},{65,193},{129,1},{193,65... | collective-permute-start | bytes 393224 | tf_op jit(solution)/shard_map/ppermute | solution.py:71
  37.0 4.1 %copy-start.12 = (s32[64,8]{0,1:T(8,128)S(1)}, s32[64,8]{0,1:T(8,128)}, u32[]{:S(2)}) copy-start(s32[64,8]{0,1:T(8,128)} %param.21) | copy-start | bytes 6148
  37.0 6.4 %collective-permute-start.5 = (f32[64,512]{1,0:T(8,128)S(1)}, f32[64,512]{1,0:T(8,128)S(1)}, u32[]{:S(2)}, u32[]{:S(2)}) collective-permute-start(f32[64,512]{1,0:T(8,128)S(1)} %fusion.56), channel_id=1, source_target_pairs={{0,64},{64,128},{128,192},{192,0},{1,65},{65,129},{129,193},{193,1... | collective-permute-start | bytes 393224 | tf_op jit(solution)/shard_map/ppermute | solution.py:71
  39.1 5.1 %collective-permute-start.1 = (f32[64,512]{1,0:T(8,128)S(1)}, f32[64,512]{1,0:T(8,128)S(1)}, u32[]{:S(2)}, u32[]{:S(2)}) collective-permute-start(f32[64,512]{1,0:T(8,128)S(1)} %fusion.54), channel_id=1, source_target_pairs={{0,192},{64,0},{128,64},{192,128},{1,193},{65,1},{129,65},{193,129... | collective-permute-start | bytes 393224 | tf_op jit(solution)/shard_map/ppermute | solution.py:71
  41.2 3.0 %copy-start.8 = (f32[64,512]{1,0:T(8,128)}, f32[64,512]{1,0:T(8,128)S(1)}, u32[]{:S(2)}) copy-start(f32[64,512]{1,0:T(8,128)S(1)} %collective-permute-done.3) | copy-start | bytes 393220
  43.5 0.7 copy-start.9
  45.2 3.0 %copy-start.7 = (bf16[64,2048]{1,0:T(8,128)(2,1)S(1)}, bf16[64,2048]{1,0:T(8,128)(2,1)}, u32[]{:S(2)}) copy-start(bf16[64,2048]{1,0:T(8,128)(2,1)} %param.19) | copy-start | bytes 786436
  45.8 2.3 %collective-permute-start.6 = (f32[64,2048]{1,0:T(8,128)S(1)}, f32[64,2048]{1,0:T(8,128)}, u32[]{:S(2)}, u32[]{:S(2)}) collective-permute-start(f32[64,2048]{1,0:T(8,128)S(1)} %bitcast.122), channel_id=1, source_target_pairs={{0,1},{1,0},{2,3},{3,2},{4,5},{5,4},{6,7},{7,6},{8,9},{9,8},{10,11... | collective-permute-start | bytes 1572872 | tf_op jit(solution)/shard_map/ppermute | solution.py:40
  47.6 1.8 dynamic-slice-start
  107.8 1.6 copy-start.2
  109.5 3.8 %collective-permute-start.7 = (bf16[768,8,128]{2,0,1:T(8,128)(2,1)}, bf16[768,8,128]{2,0,1:T(8,128)(2,1)}, u32[]{:S(2)}, u32[]{:S(2)}) collective-permute-start(bf16[768,8,128]{2,0,1:T(8,128)(2,1)} %copy.76), channel_id=1, source_target_pairs={{0,1},{1,0},{2,3},{3,2},{4,5},{5,4},{6,7},{7,6},{8,9},{9,8},{10,11... | collective-permute-start | bytes 4718600 | tf_op jit(solution)/shard_map/ppermute | solution.py:40
  112.4 3.1 %copy-start.14 = (bf16[1,2048,384]{2,1,0:T(8,128)(2,1)S(1)}, bf16[1,2048,384]{2,1,0:T(8,128)(2,1)}, u32[]{:S(2)}) copy-start(bf16[1,2048,384]{2,1,0:T(8,128)(2,1)} %param.23) | copy-start | bytes 4718596
  115.6 1.8 copy-start.15
  117.4 1.8 copy-start.3
  121.1 3.6 %copy-start.1 = (f32[768,16,128]{2,0,1:T(8,128)}, f32[768,16,128]{2,0,1:T(8,128)S(1)}, u32[]{:S(2)}) copy-start(f32[768,16,128]{2,0,1:T(8,128)S(1)} %fusion.10) | copy-start | bytes 18874372
  124.6 6.0 %collective-permute-start.8 = (f32[768,8,128]{2,0,1:T(8,128)}, f32[768,8,128]{2,0,1:T(8,128)}, u32[]{:S(2)}, u32[]{:S(2)}) collective-permute-start(f32[768,8,128]{2,0,1:T(8,128)} %constant_dynamic-slice_fusion), channel_id=1, source_target_pairs={{0,1},{1,0},{2,3},{3,2},{4,5},{5,4},{6,7},{7,6},{8,9},{9,8},{10,11... | collective-permute-start | bytes 9437192 | tf_op jit(solution)/shard_map/ppermute | solution.py:40
  136.0 7.7 %copy-start.13 = (f32[64,8]{0,1:T(8,128)S(1)}, f32[64,8]{0,1:T(8,128)}, u32[]{:S(2)}) copy-start(f32[64,8]{0,1:T(8,128)} %param.22) | copy-start | bytes 6148
  136.0 49.0 %all-to-all-start.1 = ((bf16[128,48,128]{2,1,0:T(8,128)(2,1)}), bf16[128,48,128]{2,1,0:T(8,128)(2,1)}, u32[]{:S(2)}, u32[]{:S(2)}) async-start(bf16[128,48,128]{2,1,0:T(8,128)(2,1)} %bitcast.115), calls=%async_computation.1 | async-start | bytes 3145728 | tf_op jit(solution)/shard_map/all_to_all | solution.py:118

commit v3 on v2

--- a/solution.py
+++ b/solution.py
@@ -1,6 +1,7 @@
 import jax
 import jax.numpy as jnp
 from jax import lax
+from jax.experimental import pallas as pl
 from jax.sharding import PartitionSpec as P
 
 D = 2048
@@ -34,6 +35,58 @@
         "jgts,sjd->tjgd", probs, joined_values, preferred_element_type=jnp.float32
     )
     return attended.reshape(tokens_here, -1).astype(jnp.bfloat16)
+
+
+def attention_kernel(q_ref, kn_ref, vn_ref, kr_ref, vr_ref, o_ref):
+    tokens = q_ref.shape[0]
+    group = q_ref.shape[1] // HEAD_WIDTH
+    k_res = kr_ref[0]
+    v_res = vr_ref[0]
+    k_new = kn_ref[...]
+    v_new = vn_ref[...]
+    rows = lax.broadcasted_iota(jnp.int32, (tokens, tokens), 0)
+    cols = lax.broadcasted_iota(jnp.int32, (tokens, tokens), 1)
+    visible = cols <= rows
+    scale = HEAD_WIDTH ** (-0.5)
+    dims = (((1,), (1,)), ((), ()))
+    for g in range(group):
+        q = q_ref[:, g * HEAD_WIDTH:(g + 1) * HEAD_WIDTH]
+        s_res = lax.dot_general(q, k_res, dims, preferred_element_type=jnp.float32) * scale
+        s_new = lax.dot_general(q, k_new, dims, preferred_element_type=jnp.float32) * scale
+        s_new = jnp.where(visible, s_new, jnp.float32(-1e30))
+        top = jnp.maximum(
+            jnp.max(s_res, axis=1, keepdims=True), jnp.max(s_new, axis=1, keepdims=True)
+        )
+        w_res = jnp.exp(s_res - top)
+        w_new = jnp.exp(s_new - top)
+        total = jnp.sum(w_res, axis=1, keepdims=True) + jnp.sum(w_new, axis=1, keepdims=True)
+        p_res = (w_res / total).astype(jnp.bfloat16)
+        p_new = (w_new / total).astype(jnp.bfloat16)
+        out = jnp.dot(p_res, v_res, preferred_element_type=jnp.float32) + jnp.dot(
+            p_new, v_new, preferred_element_type=jnp.float32
+        )
+        o_ref[:, g * HEAD_WIDTH:(g + 1) * HEAD_WIDTH] = out.astype(o_ref.dtype)
+
+
+def attend_kernel(queries, fresh_keys, fresh_values, resident_keys, resident_values, interpret=False):
+    tokens = queries.shape[0]
+    kv_here = fresh_keys.shape[1] // HEAD_WIDTH
+    width = queries.shape[1] // kv_here
+    context = resident_keys.shape[1]
+    return pl.pallas_call(
+        attention_kernel,
+        grid=(kv_here,),
+        in_specs=[
+            pl.BlockSpec((tokens, width), lambda j: (0, j)),
+            pl.BlockSpec((tokens, HEAD_WIDTH), lambda j: (0, j)),
+            pl.BlockSpec((tokens, HEAD_WIDTH), lambda j: (0, j)),
+            pl.BlockSpec((1, context, HEAD_WIDTH), lambda j: (0, 0, j)),
+            pl.BlockSpec((1, context, HEAD_WIDTH), lambda j: (0, 0, j)),
+        ],
+        out_specs=pl.BlockSpec((tokens, width), lambda j: (0, j)),
+        out_shape=jax.ShapeDtypeStruct(queries.shape, jnp.bfloat16),
+        interpret=interpret,
+    )(queries, fresh_keys, fresh_values, resident_keys, resident_values)
 
 
 def swap_pair(x):
@@ -59,7 +112,7 @@
     lane = lax.axis_index("tensor")
     half = D // lax.axis_size("tensor")
     groups = lax.axis_size("dp")
-    attended = attend_local(queries, fresh_keys, fresh_values, resident_keys, resident_values)
+    attended = attend_kernel(queries, fresh_keys, fresh_values, resident_keys, resident_values)
 
     here = lax.axis_index("dp")
     blocks = [jnp.dot(attended, out_weight, preferred_element_type=jnp.float32)]

time: 189 us -> 179 us (0.947)
  Pallas kernels: 0 us -> 12.1 us
  matrix products: 21 us -> 11.7 us
  local copies, waits for them, and re-layouts: 20.6 us -> 12.4 us
  other arithmetic: 11.9 us -> 9.55 us
  blocking collectives: 56.8 us -> 54.6 us
  waiting for transfers between devices: 58.1 us -> 60.2 us
    pallas_call x0 -> x1, Pallas kernels: none -> 12.1 us  [attend_kernel(): pl.pallas_call(attention_kernel, grid=(kv_here,), in_specs=[pl.BlockSpec(...]
    dot_general x1 -> x0, matrix products: 5.64 us -> none  [attend_local(): jnp.einsum('jgts,sjd->tjgd', probs, joined_values, preferred_element_type...]
    sub x1 -> x0, matrix products: 4.66 us -> none  [attend_local(): weight = jnp.exp(score - top_score)]
    unnamed x39 -> x21, local copies, waits for them, and re-layouts: 8.63 us -> 4.79 us
    ppermute x3, waiting for transfers between devices: 2.99 us -> 6.48 us  [per_device(): blocks.append(lax.ppermute(product, 'dp', backward))]
    concatenate x3 -> x0, local copies, waits for them, and re-layouts: 3.26 us -> none  [the longest x2 1.93 us: attend_local(): jnp.concatenate([resident_keys[0], fresh_keys], 0)]
    ppermute x3, starting transfers between devices: 6.72 us -> 4.29 us  [per_device(): blocks.append(lax.ppermute(product, 'dp', backward))]
    all_to_all x1, blocking collectives: 56.8 us -> 54.6 us  [per_device(): lax.all_to_all(outgoing.reshape(owners, CAP * width, lanes), ('dp', 'expe...]
  transfers between devices with their start and end apart: 10 -> 10, of which waited for: 7 -> 8; matrix products, arithmetic and copies ran while one was open for 4% -> 5% of each run, Pallas kernels for 0% -> 0%
where the time goes in v3:
time: 179 us
  waiting for transfers between devices  60.2 us (34%)
  blocking collectives  54.6 us (31%)
  starting transfers between devices  18.1 us (10%)
  local copies, waits for them, and re-layouts  12.4 us (7%)
  Pallas kernels  12.1 us (7%)
  matrix products  11.7 us (7%)
  other arithmetic  9.55 us (5%)
    all_to_all x1, blocking collectives, per_device(): lax.all_to_all(outgoing.reshape(owners, CAP * width, lanes), ('dp', 'expe...  54.6 us
    all_to_all x1, waiting for transfers between devices, per_device(): lax.all_to_all(expert_out.reshape(owners, CAP * width, lanes), ('dp', 'ex...  41.3 us
    pallas_call x1, Pallas kernels, attend_kernel(): pl.pallas_call(attention_kernel, grid=(kv_here,), in_specs=[pl.BlockSpec(...  12.1 us
    all_to_all x1, starting transfers between devices, per_device(): lax.all_to_all(expert_out.reshape(owners, CAP * width, lanes), ('dp', 'ex...  7.67 us
    ppermute x3, waiting for transfers between devices, swap_pair(): return lax.ppermute(x, 'tensor', [(0, 1), (1, 0)])  6.53 us
    ppermute x3, waiting for transfers between devices, per_device(): blocks.append(lax.ppermute(product, 'dp', backward))  6.48 us
    ppermute x3, waiting for transfers between devices, per_device(): arrived = lax.ppermute(attended, 'dp', onward)  5.88 us
    ppermute x3, starting transfers between devices, per_device(): arrived = lax.ppermute(attended, 'dp', onward)  5.65 us
  transfers between devices with their start and end apart: 10, of which 8 were waited for; matrix products, arithmetic and copies ran while one was open for 5% of the time, Pallas kernels for 0%

profile of v3, /device:TPU:32, one launch (start us, length us, event | category | flops | bytes accessed | tf_op | source)
XLA Modules:
  0.0 178.8 jit_solution(5245375023672324443)
XLA Ops:
  0.0 0.0 copy-start
  0.0 12.1 %shard_map.127 = bf16[64,2048]{1,0:T(8,128)(2,1)} custom-call(bf16[64,2048]{1,0:T(8,128)(2,1)} %q_ref.1, bf16[64,256]{1,0:T(8,128)(2,1)} %kn_ref.1, bf16[64,256]{1,0:T(8,128)(2,1)} %vn_ref.1, bf16[1,2048,256]{2,1,0:T(8,128)(2,1)} %kr_ref.1, bf16[1,2048,256]{2,1,0:T(8,128)(2,1)} %vr_ref.1), custom_call_target="tpu_custom_call" | custom-call | tf_op jit(solution)/shard_map/pallas_call | solution.py:76
  12.1 1.5 collective-permute-start
  13.6 2.7 %collective-permute-start.2 = (bf16[64,2048]{1,0:T(8,128)(2,1)}, bf16[64,2048]{1,0:T(8,128)(2,1)S(1)}, u32[]{:S(2)}, u32[]{:S(2)}) collective-permute-start(bf16[64,2048]{1,0:T(8,128)(2,1)} %shard_map.127), channel_id=1, source_target_pairs={{0,128},{64,192},{128,0},{192,64},{1,129},{65,193},{129,1},{193,65... | collective-permute-start | bytes 786440 | tf_op jit(solution)/shard_map/ppermute | solution.py:122
  16.3 1.4 collective-permute-start.4
  17.7 0.0 copy-done
  17.7 1.4 convolution_bitcast_fusion
  19.2 2.5 %collective-permute-done = bf16[64,2048]{1,0:T(8,128)(2,1)S(1)} collective-permute-done((bf16[64,2048]{1,0:T(8,128)(2,1)}, bf16[64,2048]{1,0:T(8,128)(2,1)S(1)}, u32[]{:S(2)}, u32[]{:S(2)}) %collective-permute-start) | collective-permute-done | bytes 262176 | tf_op jit(solution)/shard_map/ppermute | solution.py:122
  21.7 0.5 fusion.24
  22.2 2.6 %collective-permute-start.1 = (f32[64,512]{1,0:T(8,128)S(1)}, f32[64,512]{1,0:T(8,128)S(1)}, u32[]{:S(2)}, u32[]{:S(2)}) collective-permute-start(f32[64,512]{1,0:T(8,128)S(1)} %fusion.24), channel_id=1, source_target_pairs={{0,192},{64,0},{128,64},{192,128},{1,193},{65,1},{129,65},{193,129... | collective-permute-start | bytes 393224 | tf_op jit(solution)/shard_map/ppermute | solution.py:124
  24.8 3.4 %collective-permute-done.2 = bf16[64,2048]{1,0:T(8,128)(2,1)S(1)} collective-permute-done((bf16[64,2048]{1,0:T(8,128)(2,1)}, bf16[64,2048]{1,0:T(8,128)(2,1)S(1)}, u32[]{:S(2)}, u32[]{:S(2)}) %collective-permute-start.2) | collective-permute-done | bytes 262176 | tf_op jit(solution)/shard_map/ppermute | solution.py:122
  28.1 0.5 fusion.25
  28.6 0.0 copy-start.5
  28.6 0.9 collective-permute-start.3
  29.5 0.0 collective-permute-done.4
  29.5 0.5 fusion.26
  30.0 0.8 collective-permute-start.5
  30.8 0.0 copy-done.5
  30.8 0.1 copy.45
  30.9 1.1 collective-permute-done.1
  32.0 4.0 %collective-permute-done.3 = f32[64,512]{1,0:T(8,128)S(1)} collective-permute-done((f32[64,512]{1,0:T(8,128)S(1)}, f32[64,512]{1,0:T(8,128)S(1)}, u32[]{:S(2)}, u32[]{:S(2)}) %collective-permute-start.3) | collective-permute-done | bytes 131104 | tf_op jit(solution)/shard_map/ppermute | solution.py:124
  36.0 1.4 collective-permute-done.5
  37.4 0.0 copy-start.4
  37.4 0.6 gather_fusion
  38.1 0.3 collective-permute-start.6
  38.4 0.1 convert_reduce_fusion
  38.5 0.1 reduce_window_sum.11
  38.6 1.2 select_reduce_fusion
  39.9 0.1 copy.46
  39.9 0.1 copy.47
  40.0 0.0 dynamic-slice-start
  40.0 0.5 fusion.11
  40.6 0.0 collective-permute-done.6
  40.6 0.0 copy-done.4
  40.6 1.2 multiply_reduce_fusion.1
  41.8 0.0 dynamic-slice-done
  41.9 0.6 convolution_convert_fusion
  42.5 1.0 copy.49
  43.5 54.6 %all_to_all.10 = bf16[128,48,128]{2,1,0:T(8,128)(2,1)S(1)} all-to-all(bf16[128,48,128]{2,1,0:T(8,128)(2,1)S(1)} %bitcast.63), channel_id=1, replica_groups=mesh['dp'=4,'expert'=32,'tensor'=2] {'dp','expert'}, dimensions={0} | all-to-all | bytes 3145728 | tf_op jit(solution)/shard_map/all_to_all | solution.py:149
  98.1 1.6 copy.51
  99.7 0.0 copy-done.2
  99.7 0.0 collective-permute-start.7
  99.7 3.0 %copy.59 = bf16[48,8,16,128]{3,2,1,0:T(8,128)(2,1)} copy(bf16[48,8,16,128]{3,1,2,0:T(8,128)(2,1)} %bitcast.67) | data formatting | bytes 3145728
  102.7 0.8 collective-permute-done.7
  103.5 2.4 %broadcast_select_fusion.1 = (bf16[768,8,128]{2,0,1:T(8,128)(2,1)S(1)}, bf16[768,8,128]{2,0,1:T(8,128)(2,1)S(1)}) fusion(bf16[768,8,128]{2,0,1:T(8,128)(2,1)} %collective-permute-done.7, pred[]{:T(512)S(6)} %eq.38, bf16[768,8,128]{2,1,0:T(8,128)(2,1)} %bitcast.60), kind=kLoop, calls=%fused_computation.15 | loop fusion | flops 1572864 | bytes 6291457 | tf_op jit(solution)/shard_map/jit(_where)/select_n | solution.py:153
  105.8 0.0 copy-done.7
  105.8 0.0 copy-start.8
  105.9 1.8 fusion.9
  107.6 0.0 copy-done.8
  107.7 0.0 copy-start.3
  107.7 1.8 fusion.10
  109.5 0.0 copy-done.3
  109.5 1.8 %fusion.4 = f32[768,16,128]{2,0,1:T(8,128)S(1)} fusion(bf16[384,16,128]{2,1,0:T(8,128)(2,1)S(1)} %bitcast.61, f32[768,384]{1,0:T(8,128)S(1)} %fusion.10, f32[768,384]{1,0:T(8,128)S(1)} %fusion.9), kind=kOutput, calls=%fused_computation.9 | convolution fusion | flops 1209729024 | bytes 10223616 | tf_op jit(solution)/shard_map/rh,hjl->rjl/dot_general | solution.py:164
  111.3 2.0 %constant_dynamic-slice_fusion = f32[768,8,128]{2,0,1:T(8,128)} fusion(f32[768,16,128]{2,0,1:T(8,128)S(1)} %fusion.4, s32[]{:T(128)S(6)} %select_n.53), kind=kLoop, calls=%fused_computation.42 | loop fusion | bytes 6291460 | tf_op jit(solution)/shard_map/dynamic_slice | solution.py:168
  113.4 1.6 copy-done.1
  114.9 0.2 collective-permute-start.8
  115.1 5.8 %collective-permute-done.8 = f32[768,8,128]{2,0,1:T(8,128)} collective-permute-done((f32[768,8,128]{2,0,1:T(8,128)}, f32[768,8,128]{2,0,1:T(8,128)}, u32[]{:S(2)}, u32[]{:S(2)}) %collective-permute-start.8) | collective-permute-done | bytes 3145760 | tf_op jit(solution)/shard_map/ppermute | solution.py:93
  120.9 3.2 %add_convert_fusion = bf16[768,8,128]{2,0,1:T(8,128)(2,1)S(1)} fusion(f32[768,8,128]{2,0,1:T(8,128)} %collective-permute-done.8, f32[768,16,128]{2,0,1:T(8,128)} %copy-done.1, s32[]{:T(128)S(6)} %select_n.52), kind=kLoop, calls=%fused_computation.2 | loop fusion | flops 1572864 | bytes 7864324 | tf_op jit(solution)/shard_map/convert_element_type | solution.py:169
  124.1 2.2 %copy.54 = bf16[768,8,128]{2,1,0:T(8,128)(2,1)} copy(bf16[768,8,128]{2,0,1:T(8,128)(2,1)S(1)} %add_convert_fusion) | data formatting | bytes 3145728 | tf_op jit(solution)/shard_map/convert_element_type | solution.py:169
  126.3 7.7 %all-to-all-start.1 = ((bf16[128,48,128]{2,1,0:T(8,128)(2,1)}), bf16[128,48,128]{2,1,0:T(8,128)(2,1)}, u32[]{:S(2)}, u32[]{:S(2)}) async-start(bf16[128,48,128]{2,1,0:T(8,128)(2,1)} %bitcast.62), calls=%async_computation.1 | async-start | bytes 3145728 | tf_op jit(solution)/shard_map/all_to_all | solution.py:171
  133.9 0.1 copy.44
  134.0 41.3 %all-to-all-done.1 = bf16[128,48,128]{2,1,0:T(8,128)(2,1)} async-done(((bf16[128,48,128]{2,1,0:T(8,128)(2,1)}), bf16[128,48,128]{2,1,0:T(8,128)(2,1)}, u32[]{:S(2)}, u32[]{:S(2)}) %all-to-all-start.1) | async-done | bytes 1572896 | tf_op jit(solution)/shard_map/all_to_all | solution.py:171
  175.3 2.8 %multiply_reduce_fusion = f32[64,8,128]{2,1,0:T(8,128)S(1)} fusion(bf16[768,8,128]{2,1,0:T(8,128)(2,1)} %bitcast.17, f32[64,8]{1,0:T(8,128)S(1)} %copy.44, s32[64,8]{1,0:T(8,128)S(1)} %copy.47), kind=kOutput, calls=%fused_computation.3 | convolution fusion | flops 806682624 | bytes 1839104 | tf_op jit(solution)/shard_map/tkr,rjl->tkjl/dot_general | solution.py:174
  178.1 0.7 fusion.14
  (12 shorter events, 0.1 us)
Async XLA Ops:
  0.0 17.7 %copy-start = (bf16[2048,512]{1,0:T(8,128)(2,1)S(1)}, bf16[2048,512]{1,0:T(8,128)(2,1)}, u32[]{:S(2)}) copy-start(bf16[2048,512]{1,0:T(8,128)(2,1)} %param.18) | copy-start | bytes 6291460
  12.1 9.6 %collective-permute-start = (bf16[64,2048]{1,0:T(8,128)(2,1)}, bf16[64,2048]{1,0:T(8,128)(2,1)S(1)}, u32[]{:S(2)}, u32[]{:S(2)}) collective-permute-start(bf16[64,2048]{1,0:T(8,128)(2,1)} %shard_map.127), channel_id=1, source_target_pairs={{0,64},{64,128},{128,192},{192,0},{1,65},{65,129},{129,193},{193,1... | collective-permute-start | bytes 786440 | tf_op jit(solution)/shard_map/ppermute | solution.py:122
  13.6 14.6 %collective-permute-start.2 = (bf16[64,2048]{1,0:T(8,128)(2,1)}, bf16[64,2048]{1,0:T(8,128)(2,1)S(1)}, u32[]{:S(2)}, u32[]{:S(2)}) collective-permute-start(bf16[64,2048]{1,0:T(8,128)(2,1)} %shard_map.127), channel_id=1, source_target_pairs={{0,128},{64,192},{128,0},{192,64},{1,129},{65,193},{129,1},{193,65... | collective-permute-start | bytes 786440 | tf_op jit(solution)/shard_map/ppermute | solution.py:122
  16.3 13.3 %collective-permute-start.4 = (bf16[64,2048]{1,0:T(8,128)(2,1)}, bf16[64,2048]{1,0:T(8,128)(2,1)S(1)}, u32[]{:S(2)}, u32[]{:S(2)}) collective-permute-start(bf16[64,2048]{1,0:T(8,128)(2,1)} %shard_map.127), channel_id=1, source_target_pairs={{0,192},{64,0},{128,64},{192,128},{1,193},{65,1},{129,65},{193,129... | collective-permute-start | bytes 786440 | tf_op jit(solution)/shard_map/ppermute | solution.py:122
  22.2 9.8 %collective-permute-start.1 = (f32[64,512]{1,0:T(8,128)S(1)}, f32[64,512]{1,0:T(8,128)S(1)}, u32[]{:S(2)}, u32[]{:S(2)}) collective-permute-start(f32[64,512]{1,0:T(8,128)S(1)} %fusion.24), channel_id=1, source_target_pairs={{0,192},{64,0},{128,64},{192,128},{1,193},{65,1},{129,65},{193,129... | collective-permute-start | bytes 393224 | tf_op jit(solution)/shard_map/ppermute | solution.py:124
  28.6 2.2 %copy-start.5 = (s32[64,8]{0,1:T(8,128)S(1)}, s32[64,8]{0,1:T(8,128)}, u32[]{:S(2)}) copy-start(s32[64,8]{0,1:T(8,128)} %param.21) | copy-start | bytes 6148
  28.6 7.4 %collective-permute-start.3 = (f32[64,512]{1,0:T(8,128)S(1)}, f32[64,512]{1,0:T(8,128)S(1)}, u32[]{:S(2)}, u32[]{:S(2)}) collective-permute-start(f32[64,512]{1,0:T(8,128)S(1)} %fusion.25), channel_id=1, source_target_pairs={{0,128},{64,192},{128,0},{192,64},{1,129},{65,193},{129,1},{193,65... | collective-permute-start | bytes 393224 | tf_op jit(solution)/shard_map/ppermute | solution.py:124
  30.0 7.4 %collective-permute-start.5 = (f32[64,512]{1,0:T(8,128)S(1)}, f32[64,512]{1,0:T(8,128)S(1)}, u32[]{:S(2)}, u32[]{:S(2)}) collective-permute-start(f32[64,512]{1,0:T(8,128)S(1)} %fusion.26), channel_id=1, source_target_pairs={{0,64},{64,128},{128,192},{192,0},{1,65},{65,129},{129,193},{193,1... | collective-permute-start | bytes 393224 | tf_op jit(solution)/shard_map/ppermute | solution.py:124
  37.4 3.2 %copy-start.4 = (bf16[64,2048]{1,0:T(8,128)(2,1)S(1)}, bf16[64,2048]{1,0:T(8,128)(2,1)}, u32[]{:S(2)}) copy-start(bf16[64,2048]{1,0:T(8,128)(2,1)} %param.19) | copy-start | bytes 786436
  38.1 2.5 %collective-permute-start.6 = (f32[64,2048]{1,0:T(8,128)S(1)}, f32[64,2048]{1,0:T(8,128)}, u32[]{:S(2)}, u32[]{:S(2)}) collective-permute-start(f32[64,2048]{1,0:T(8,128)S(1)} %bitcast.65), channel_id=1, source_target_pairs={{0,1},{1,0},{2,3},{3,2},{4,5},{5,4},{6,7},{7,6},{8,9},{9,8},{10,11... | collective-permute-start | bytes 1572872 | tf_op jit(solution)/shard_map/ppermute | solution.py:93
  40.0 1.8 %dynamic-slice-start = ((f32[2048]{0:T(1024)}, s32[]{:T(128)}), f32[1024]{0:T(1024)S(1)}, s32[]{:S(2)}) async-start(f32[2048]{0:T(1024)} %param.20, s32[]{:T(128)} %select_n.48), calls=%async_computation.2 | async-start | bytes 8704 | tf_op jit(solution)/shard_map/dynamic_slice | solution.py:133
  98.1 1.6 copy-start.2
  99.7 3.8 %collective-permute-start.7 = (bf16[768,8,128]{2,0,1:T(8,128)(2,1)}, bf16[768,8,128]{2,0,1:T(8,128)(2,1)}, u32[]{:S(2)}, u32[]{:S(2)}) collective-permute-start(bf16[768,8,128]{2,0,1:T(8,128)(2,1)} %copy.51), channel_id=1, source_target_pairs={{0,1},{1,0},{2,3},{3,2},{4,5},{5,4},{6,7},{7,6},{8,9},{9,8},{10,11... | collective-permute-start | bytes 4718600 | tf_op jit(solution)/shard_map/ppermute | solution.py:93
  102.7 3.1 %copy-start.7 = (bf16[1,2048,384]{2,1,0:T(8,128)(2,1)S(1)}, bf16[1,2048,384]{2,1,0:T(8,128)(2,1)}, u32[]{:S(2)}) copy-start(bf16[1,2048,384]{2,1,0:T(8,128)(2,1)} %param.23) | copy-start | bytes 4718596
  105.8 1.8 %copy-start.8 = (bf16[1,2048,384]{2,1,0:T(8,128)(2,1)S(1)}, bf16[1,2048,384]{2,1,0:T(8,128)(2,1)}, u32[]{:S(2)}) copy-start(bf16[1,2048,384]{2,1,0:T(8,128)(2,1)} %param.24) | copy-start | bytes 4718596
  107.7 1.8 %copy-start.3 = (bf16[48,8,16,128]{3,2,1,0:T(8,128)(2,1)S(1)}, bf16[48,8,16,128]{3,2,1,0:T(8,128)(2,1)}, u32[]{:S(2)}) copy-start(bf16[48,8,16,128]{3,2,1,0:T(8,128)(2,1)} %copy.59) | copy-start | bytes 4718596
  111.3 3.6 %copy-start.1 = (f32[768,16,128]{2,0,1:T(8,128)}, f32[768,16,128]{2,0,1:T(8,128)S(1)}, u32[]{:S(2)}) copy-start(f32[768,16,128]{2,0,1:T(8,128)S(1)} %fusion.4) | copy-start | bytes 18874372
  114.9 6.0 %collective-permute-start.8 = (f32[768,8,128]{2,0,1:T(8,128)}, f32[768,8,128]{2,0,1:T(8,128)}, u32[]{:S(2)}, u32[]{:S(2)}) collective-permute-start(f32[768,8,128]{2,0,1:T(8,128)} %constant_dynamic-slice_fusion), channel_id=1, source_target_pairs={{0,1},{1,0},{2,3},{3,2},{4,5},{5,4},{6,7},{7,6},{8,9},{9,8},{10,11... | collective-permute-start | bytes 9437192 | tf_op jit(solution)/shard_map/ppermute | solution.py:93
  126.3 7.7 %copy-start.6 = (f32[64,8]{0,1:T(8,128)S(1)}, f32[64,8]{0,1:T(8,128)}, u32[]{:S(2)}) copy-start(f32[64,8]{0,1:T(8,128)} %param.22) | copy-start | bytes 6148
  126.3 49.1 %all-to-all-start.1 = ((bf16[128,48,128]{2,1,0:T(8,128)(2,1)}), bf16[128,48,128]{2,1,0:T(8,128)(2,1)}, u32[]{:S(2)}, u32[]{:S(2)}) async-start(bf16[128,48,128]{2,1,0:T(8,128)(2,1)} %bitcast.62), calls=%async_computation.1 | async-start | bytes 3145728 | tf_op jit(solution)/shard_map/all_to_all | solution.py:171

commit v4 on v3

--- a/solution.py
+++ b/solution.py
@@ -2,6 +2,7 @@
 import jax.numpy as jnp
 from jax import lax
 from jax.experimental import pallas as pl
+from jax.experimental.pallas import tpu as pltpu
 from jax.sharding import PartitionSpec as P
 
 D = 2048
@@ -87,6 +88,57 @@
         out_shape=jax.ShapeDtypeStruct(queries.shape, jnp.bfloat16),
         interpret=interpret,
     )(queries, fresh_keys, fresh_values, resident_keys, resident_values)
+
+
+def expert_kernel(lane_ref, mine_ref, other_ref, g_own, g_other, u_own, u_other, d_own, d_other, own_ref, theirs_ref):
+    fold = g_own.shape[0] // HEAD_WIDTH
+    rows = own_ref.shape[0] // fold
+    gate = jnp.zeros((rows, g_own.shape[1]), jnp.float32)
+    up = jnp.zeros((rows, g_own.shape[1]), jnp.float32)
+    for j in range(fold):
+        part = pl.ds(j * HEAD_WIDTH, HEAD_WIDTH)
+        x_mine = mine_ref[pl.ds(j, rows, stride=fold), :]
+        x_other = other_ref[pl.ds(j, rows, stride=fold), :]
+        gate = gate + jnp.dot(x_mine, g_own[part, :], preferred_element_type=jnp.float32)
+        gate = gate + jnp.dot(x_other, g_other[part, :], preferred_element_type=jnp.float32)
+        up = up + jnp.dot(x_mine, u_own[part, :], preferred_element_type=jnp.float32)
+        up = up + jnp.dot(x_other, u_other[part, :], preferred_element_type=jnp.float32)
+    act = (gate / (1.0 + jnp.exp(-gate)) * up).astype(jnp.bfloat16)
+    for j in range(fold):
+        part = pl.ds(j * HEAD_WIDTH, HEAD_WIDTH)
+        own_ref[pl.ds(j, rows, stride=fold), :] = jnp.dot(
+            act, d_own[:, part], preferred_element_type=jnp.float32
+        )
+        theirs_ref[pl.ds(j, rows, stride=fold), :] = jnp.dot(
+            act, d_other[:, part], preferred_element_type=jnp.float32
+        )
+
+
+def expert_ffn(lane, mine, other, gate_mat, up_mat, down_mat, block_rows=256, interpret=False):
+    folded, lanes = mine.shape
+    half, hidden = gate_mat.shape[0] // 2, gate_mat.shape[1]
+    fold = half // lanes
+    rows = folded // fold
+    step = block_rows * fold
+    act_spec = pl.BlockSpec((step, lanes), lambda i, lane_ref: (i, 0))
+    own_rows = pl.BlockSpec((half, hidden), lambda i, lane_ref: (lane_ref[0], 0))
+    other_rows = pl.BlockSpec((half, hidden), lambda i, lane_ref: (1 - lane_ref[0], 0))
+    own_cols = pl.BlockSpec((hidden, half), lambda i, lane_ref: (0, lane_ref[0]))
+    other_cols = pl.BlockSpec((hidden, half), lambda i, lane_ref: (0, 1 - lane_ref[0]))
+    return pl.pallas_call(
+        expert_kernel,
+        grid_spec=pltpu.PrefetchScalarGridSpec(
+            num_scalar_prefetch=1,
+            grid=(rows // block_rows,),
+            in_specs=[act_spec, act_spec, own_rows, other_rows, own_rows, other_rows, own_cols, other_cols],
+            out_specs=[act_spec, act_spec],
+        ),
+        out_shape=[
+            jax.ShapeDtypeStruct((folded, lanes), jnp.float32),
+            jax.ShapeDtypeStruct((folded, lanes), jnp.float32),
+        ],
+        interpret=interpret,
+    )(lane, mine, other, gate_mat, gate_mat, up_mat, up_mat, down_mat, down_mat)
 
 
 def swap_pair(x):
@@ -148,25 +200,12 @@
     ).astype(jnp.bfloat16)
     received = lax.all_to_all(
         outgoing.reshape(owners, CAP * width, lanes), ("dp", "expert"), split_axis=0, concat_axis=0, tiled=True
-    ).reshape(owners * CAP, width, lanes)
+    ).reshape(owners * CAP * width, lanes)
     other = swap_pair(received)
-    first = jnp.where(lane == 0, received, other)
-    second = jnp.where(lane == 0, other, received)
-    flat = jnp.concatenate([first, second], axis=1)
-
-    gate_part = jnp.einsum(
-        "rjl,jlh->rh", flat, w_gate[0].reshape(2 * width, lanes, -1), preferred_element_type=jnp.float32
-    )
-    up_part = jnp.einsum(
-        "rjl,jlh->rh", flat, w_up[0].reshape(2 * width, lanes, -1), preferred_element_type=jnp.float32
-    )
-    act = (jax.nn.silu(gate_part) * up_part).astype(jnp.bfloat16)
-    result = jnp.einsum(
-        "rh,hjl->rjl", act, w_down[0].reshape(act.shape[1], 2 * width, lanes), preferred_element_type=jnp.float32
-    )
-    own = lax.dynamic_slice_in_dim(result, lane * width, width, 1)
-    theirs = lax.dynamic_slice_in_dim(result, (1 - lane) * width, width, 1)
-    expert_out = (own + swap_pair(theirs)).astype(jnp.bfloat16)
+    own, theirs = expert_ffn(
+        lane.astype(jnp.int32).reshape(1), received, other, w_gate[0], w_up[0], w_down[0]
+    )
+    expert_out = (own + swap_pair(theirs.astype(jnp.bfloat16)).astype(jnp.float32)).astype(jnp.bfloat16)
 
     returned = lax.all_to_all(
         expert_out.reshape(owners, CAP * width, lanes), ("dp", "expert"), split_axis=0, concat_axis=0, tiled=True

time: 179 us -> 177 us (0.989)
  Pallas kernels: 12.1 us -> 24.3 us
  local copies, waits for them, and re-layouts: 12.4 us -> 4.36 us
  matrix products: 11.7 us -> 6.26 us
    pallas_call x0 -> x1, Pallas kernels: none -> 12.2 us  [expert_ffn(): pl.pallas_call(expert_kernel, grid_spec=pltpu.PrefetchScalarGridSpec(num_...]
    dot_general x3 -> x0, matrix products: 5.41 us -> none  [the longest x1 1.84 us: per_device(): jnp.einsum('rh,hjl->rjl', act, w_down[0].reshape(act.shape[1], 2 * width,...]
    select_n x1 -> x0, other arithmetic: 2.36 us -> none  [per_device(): first = jnp.where(lane == 0, received, other)]
    unnamed x21 -> x18, local copies, waits for them, and re-layouts: 4.79 us -> 2.57 us
    convert_element_type x1 -> x0, local copies, waits for them, and re-layouts: 2.18 us -> none  [per_device(): expert_out = (own + swap_pair(theirs)).astype(jnp.bfloat16)]
    dynamic_slice x1 -> x0, local copies, waits for them, and re-layouts: 2.03 us -> none  [per_device(): theirs = lax.dynamic_slice_in_dim(result, (1 - lane) * width, width, 1)]
    convert_element_type x1 -> x2, other arithmetic: 3.15 us -> 3.66 us  [the longest x1 2.19 us: per_device(): theirs.astype(jnp.bfloat16)]
  transfers between devices with their start and end apart: 10 -> 10, of which waited for: 8 -> 8; matrix products, arithmetic and copies ran while one was open for 5% -> 3% of each run, Pallas kernels for 0% -> 0%
where the time goes in v4:
time: 177 us
  waiting for transfers between devices  60.3 us (34%)
  blocking collectives  54.6 us (31%)
  Pallas kernels  24.3 us (14%)
  starting transfers between devices  18.1 us (10%)
  other arithmetic  8.59 us (5%)
  matrix products  6.26 us (4%)
  local copies, waits for them, and re-layouts  4.36 us (2%)
    all_to_all x1, blocking collectives, per_device(): lax.all_to_all(outgoing.reshape(owners, CAP * width, lanes), ('dp', 'expe...  54.6 us
    all_to_all x1, waiting for transfers between devices, per_device(): lax.all_to_all(expert_out.reshape(owners, CAP * width, lanes), ('dp', 'ex...  41.3 us
    pallas_call x1, Pallas kernels, expert_ffn(): pl.pallas_call(expert_kernel, grid_spec=pltpu.PrefetchScalarGridSpec(num_...  12.2 us
    pallas_call x1, Pallas kernels, attend_kernel(): pl.pallas_call(attention_kernel, grid=(kv_here,), in_specs=[pl.BlockSpec(...  12.1 us
    all_to_all x1, starting transfers between devices, per_device(): lax.all_to_all(expert_out.reshape(owners, CAP * width, lanes), ('dp', 'ex...  7.66 us
    ppermute x3, waiting for transfers between devices, swap_pair(): return lax.ppermute(x, 'tensor', [(0, 1), (1, 0)])  6.69 us
    ppermute x3, waiting for transfers between devices, per_device(): blocks.append(lax.ppermute(product, 'dp', backward))  6.45 us
    ppermute x3, waiting for transfers between devices, per_device(): arrived = lax.ppermute(attended, 'dp', onward)  5.87 us
  transfers between devices with their start and end apart: 10, of which 8 were waited for; matrix products, arithmetic and copies ran while one was open for 3% of the time, Pallas kernels for 0%

profile of v4, /device:TPU:32, one launch (start us, length us, event | category | flops | bytes accessed | tf_op | source)
XLA Modules:
  0.0 176.8 jit_solution(17306157002103751653)
XLA Ops:
  0.0 0.0 copy-start
  0.0 12.1 %shard_map.127 = bf16[64,2048]{1,0:T(8,128)(2,1)} custom-call(bf16[64,2048]{1,0:T(8,128)(2,1)} %q_ref.1, bf16[64,256]{1,0:T(8,128)(2,1)} %kn_ref.1, bf16[64,256]{1,0:T(8,128)(2,1)} %vn_ref.1, bf16[1,2048,256]{2,1,0:T(8,128)(2,1)} %kr_ref.1, bf16[1,2048,256]{2,1,0:T(8,128)(2,1)} %vr_ref.1), custom_call_target="tpu_custom_call" | custom-call | tf_op jit(solution)/shard_map/pallas_call | solution.py:77
  12.1 1.5 collective-permute-start
  13.6 2.7 %collective-permute-start.2 = (bf16[64,2048]{1,0:T(8,128)(2,1)}, bf16[64,2048]{1,0:T(8,128)(2,1)S(1)}, u32[]{:S(2)}, u32[]{:S(2)}) collective-permute-start(bf16[64,2048]{1,0:T(8,128)(2,1)} %shard_map.127), channel_id=1, source_target_pairs={{0,128},{64,192},{128,0},{192,64},{1,129},{65,193},{129,1},{193,65... | collective-permute-start | bytes 786440 | tf_op jit(solution)/shard_map/ppermute | solution.py:174
  16.3 1.4 collective-permute-start.4
  17.7 0.0 copy-done
  17.7 1.4 convolution_bitcast_fusion
  19.2 2.5 %collective-permute-done = bf16[64,2048]{1,0:T(8,128)(2,1)S(1)} collective-permute-done((bf16[64,2048]{1,0:T(8,128)(2,1)}, bf16[64,2048]{1,0:T(8,128)(2,1)S(1)}, u32[]{:S(2)}, u32[]{:S(2)}) %collective-permute-start) | collective-permute-done | bytes 262176 | tf_op jit(solution)/shard_map/ppermute | solution.py:174
  21.7 0.5 fusion.14
  22.2 0.0 copy-start.5
  22.2 2.6 %collective-permute-start.1 = (f32[64,512]{1,0:T(8,128)S(1)}, f32[64,512]{1,0:T(8,128)}, u32[]{:S(2)}, u32[]{:S(2)}) collective-permute-start(f32[64,512]{1,0:T(8,128)S(1)} %fusion.14), channel_id=1, source_target_pairs={{0,192},{64,0},{128,64},{192,128},{1,193},{65,1},{129,65},{193,129... | collective-permute-start | bytes 393224 | tf_op jit(solution)/shard_map/ppermute | solution.py:176
  24.8 3.3 %collective-permute-done.2 = bf16[64,2048]{1,0:T(8,128)(2,1)S(1)} collective-permute-done((bf16[64,2048]{1,0:T(8,128)(2,1)}, bf16[64,2048]{1,0:T(8,128)(2,1)S(1)}, u32[]{:S(2)}, u32[]{:S(2)}) %collective-permute-start.2) | collective-permute-done | bytes 262176 | tf_op jit(solution)/shard_map/ppermute | solution.py:174
  28.1 0.5 fusion.15
  28.6 0.9 collective-permute-start.3
  29.5 0.0 collective-permute-done.4
  29.5 0.5 fusion.16
  30.0 0.0 copy-start.7
  30.0 0.0 copy-start.4
  30.0 0.8 collective-permute-start.5
  30.8 0.0 copy-done.5
  30.9 0.1 copy.34
  30.9 1.2 collective-permute-done.1
  32.1 3.9 %collective-permute-done.3 = f32[64,512]{1,0:T(8,128)S(1)} collective-permute-done((f32[64,512]{1,0:T(8,128)S(1)}, f32[64,512]{1,0:T(8,128)S(1)}, u32[]{:S(2)}, u32[]{:S(2)}) %collective-permute-start.3) | collective-permute-done | bytes 131104 | tf_op jit(solution)/shard_map/ppermute | solution.py:176
  36.0 1.4 collective-permute-done.5
  37.4 0.9 pad_maximum_fusion
  38.3 0.6 gather_fusion
  39.0 0.3 collective-permute-start.6
  39.2 0.1 convert_reduce_fusion
  39.4 0.1 reduce_window_sum.11
  39.5 1.2 select_reduce_fusion
  40.8 0.1 copy.35
  40.8 0.1 copy.36
  40.9 0.0 copy-done.7
  40.9 0.5 fusion.5
  41.5 0.0 collective-permute-done.6
  41.5 0.0 copy-done.4
  41.5 1.2 multiply_reduce_fusion.1
  42.7 0.6 convolution_convert_fusion
  43.4 1.0 copy.38
  44.4 54.6 %all_to_all.10 = bf16[128,48,128]{2,1,0:T(8,128)(2,1)S(1)} all-to-all(bf16[128,48,128]{2,1,0:T(8,128)(2,1)S(1)} %bitcast.57), channel_id=1, replica_groups=mesh['dp'=4,'expert'=32,'tensor'=2] {'dp','expert'}, dimensions={0} | all-to-all | bytes 3145728 | tf_op jit(solution)/shard_map/all_to_all | solution.py:201
  99.0 0.0 copy-start.1
  99.0 1.1 copy-done.1
  100.2 0.0 collective-permute-start.7
  100.2 3.4 %collective-permute-done.7.other_ref = bf16[6144,128]{1,0:T(8,128)(2,1)S(1)} collective-permute-done((bf16[6144,128]{1,0:T(8,128)(2,1)S(1)}, bf16[6144,128]{1,0:T(8,128)(2,1)S(1)}, u32[]{:S(2)}, u32[]{:S(2)}) %collective-permute-start.7) | collective-permute-done | bytes 1572896 | tf_op jit(solution)/shard_map/ppermute | solution.py:145
  103.6 0.0 copy-start.3
  103.6 1.2 copy-done.3
  104.8 12.2 %shard_map.128 = (f32[6144,128]{1,0:T(8,128)}, f32[6144,128]{1,0:T(8,128)}) custom-call(s32[1]{0:T(128)} %bitcast.8.lane_ref, bf16[6144,128]{1,0:T(8,128)(2,1)} %bitcast.56, bf16[6144,128]{1,0:T(8,128)(2,1)} %copy-done.3, bf16[2048,384]{1,0:T(8,128)(2,1)} %bitcast.49, bf16[2048,384]{1,0:T(8,128)(2,1)} %bitcast.50, bf16[2048,384]{1,0:T(8,128)(2,1)} %bitcast.51, ...), custom_call_target="tpu_custom_call" | custom-call | tf_op jit(solution)/shard_map/pallas_call | solution.py:128
  117.0 0.0 copy-start.2
  117.1 2.2 %convert_element_type.34 = bf16[6144,128]{1,0:T(8,128)(2,1)S(1)} convert(f32[6144,128]{1,0:T(8,128)} %get-tuple-element.8) | non-fusion elementwise | flops 786432 | bytes 4718592 | tf_op jit(solution)/shard_map/convert_element_type | solution.py:208
  119.2 0.2 collective-permute-start.8
  119.5 3.3 %collective-permute-done.8 = bf16[6144,128]{1,0:T(8,128)(2,1)S(1)} collective-permute-done((bf16[6144,128]{1,0:T(8,128)(2,1)S(1)}, bf16[6144,128]{1,0:T(8,128)(2,1)S(1)}, u32[]{:S(2)}, u32[]{:S(2)}) %collective-permute-start.8) | collective-permute-done | bytes 1572896 | tf_op jit(solution)/shard_map/ppermute | solution.py:145
  122.7 0.0 copy-done.2
  122.7 1.5 add_convert_fusion
  124.2 0.0 copy-start.6
  124.2 7.7 %all-to-all-start.1 = ((bf16[128,48,128]{2,1,0:T(8,128)(2,1)}), bf16[128,48,128]{2,1,0:T(8,128)(2,1)}, u32[]{:S(2)}, u32[]{:S(2)}) async-start(bf16[128,48,128]{2,1,0:T(8,128)(2,1)} %bitcast.58), calls=%async_computation.1 | async-start | bytes 3145728 | tf_op jit(solution)/shard_map/all_to_all | solution.py:210
  131.9 0.0 copy-done.6
  131.9 0.1 copy.33
  132.0 41.3 %all-to-all-done.1 = bf16[128,48,128]{2,1,0:T(8,128)(2,1)} async-done(((bf16[128,48,128]{2,1,0:T(8,128)(2,1)}), bf16[128,48,128]{2,1,0:T(8,128)(2,1)}, u32[]{:S(2)}, u32[]{:S(2)}) %all-to-all-start.1) | async-done | bytes 1572896 | tf_op jit(solution)/shard_map/all_to_all | solution.py:210
  173.2 2.8 %multiply_reduce_fusion = f32[64,8,128]{2,1,0:T(8,128)S(1)} fusion(bf16[768,8,128]{2,1,0:T(8,128)(2,1)} %bitcast.16, f32[64,8]{1,0:T(8,128)S(1)} %copy.33, s32[64,8]{1,0:T(8,128)S(1)} %copy.36), kind=kOutput, calls=%fused_computation.2 | convolution fusion | flops 806682624 | bytes 1839104 | tf_op jit(solution)/shard_map/tkr,rjl->tkjl/dot_general | solution.py:213
  176.0 0.7 fusion.7
  (7 shorter events, 0.1 us)
Async XLA Ops:
  0.0 17.7 %copy-start = (bf16[2048,512]{1,0:T(8,128)(2,1)S(1)}, bf16[2048,512]{1,0:T(8,128)(2,1)}, u32[]{:S(2)}) copy-start(bf16[2048,512]{1,0:T(8,128)(2,1)} %param.18) | copy-start | bytes 6291460
  12.1 9.6 %collective-permute-start = (bf16[64,2048]{1,0:T(8,128)(2,1)}, bf16[64,2048]{1,0:T(8,128)(2,1)S(1)}, u32[]{:S(2)}, u32[]{:S(2)}) collective-permute-start(bf16[64,2048]{1,0:T(8,128)(2,1)} %shard_map.127), channel_id=1, source_target_pairs={{0,64},{64,128},{128,192},{192,0},{1,65},{65,129},{129,193},{193,1... | collective-permute-start | bytes 786440 | tf_op jit(solution)/shard_map/ppermute | solution.py:174
  13.6 14.6 %collective-permute-start.2 = (bf16[64,2048]{1,0:T(8,128)(2,1)}, bf16[64,2048]{1,0:T(8,128)(2,1)S(1)}, u32[]{:S(2)}, u32[]{:S(2)}) collective-permute-start(bf16[64,2048]{1,0:T(8,128)(2,1)} %shard_map.127), channel_id=1, source_target_pairs={{0,128},{64,192},{128,0},{192,64},{1,129},{65,193},{129,1},{193,65... | collective-permute-start | bytes 786440 | tf_op jit(solution)/shard_map/ppermute | solution.py:174
  16.3 13.2 %collective-permute-start.4 = (bf16[64,2048]{1,0:T(8,128)(2,1)}, bf16[64,2048]{1,0:T(8,128)(2,1)S(1)}, u32[]{:S(2)}, u32[]{:S(2)}) collective-permute-start(bf16[64,2048]{1,0:T(8,128)(2,1)} %shard_map.127), channel_id=1, source_target_pairs={{0,192},{64,0},{128,64},{192,128},{1,193},{65,1},{129,65},{193,129... | collective-permute-start | bytes 786440 | tf_op jit(solution)/shard_map/ppermute | solution.py:174
  22.2 8.7 %copy-start.5 = (s32[64,8]{0,1:T(8,128)S(1)}, s32[64,8]{0,1:T(8,128)}, u32[]{:S(2)}) copy-start(s32[64,8]{0,1:T(8,128)} %param.21) | copy-start | bytes 6148
  22.2 9.9 %collective-permute-start.1 = (f32[64,512]{1,0:T(8,128)S(1)}, f32[64,512]{1,0:T(8,128)}, u32[]{:S(2)}, u32[]{:S(2)}) collective-permute-start(f32[64,512]{1,0:T(8,128)S(1)} %fusion.14), channel_id=1, source_target_pairs={{0,192},{64,0},{128,64},{192,128},{1,193},{65,1},{129,65},{193,129... | collective-permute-start | bytes 393224 | tf_op jit(solution)/shard_map/ppermute | solution.py:176
  28.6 7.4 %collective-permute-start.3 = (f32[64,512]{1,0:T(8,128)S(1)}, f32[64,512]{1,0:T(8,128)S(1)}, u32[]{:S(2)}, u32[]{:S(2)}) collective-permute-start(f32[64,512]{1,0:T(8,128)S(1)} %fusion.15), channel_id=1, source_target_pairs={{0,128},{64,192},{128,0},{192,64},{1,129},{65,193},{129,1},{193,65... | collective-permute-start | bytes 393224 | tf_op jit(solution)/shard_map/ppermute | solution.py:176
  30.0 10.9 %copy-start.7 = (f32[2048]{0:T(1024)S(1)}, f32[2048]{0:T(1024)}, u32[]{:S(2)}) copy-start(f32[2048]{0:T(1024)} %param.20) | copy-start | bytes 24580
  30.0 11.5 %copy-start.4 = (bf16[64,2048]{1,0:T(8,128)(2,1)S(1)}, bf16[64,2048]{1,0:T(8,128)(2,1)}, u32[]{:S(2)}) copy-start(bf16[64,2048]{1,0:T(8,128)(2,1)} %param.19) | copy-start | bytes 786436
  30.0 7.3 %collective-permute-start.5 = (f32[64,512]{1,0:T(8,128)S(1)}, f32[64,512]{1,0:T(8,128)S(1)}, u32[]{:S(2)}, u32[]{:S(2)}) collective-permute-start(f32[64,512]{1,0:T(8,128)S(1)} %fusion.16), channel_id=1, source_target_pairs={{0,64},{64,128},{128,192},{192,0},{1,65},{65,129},{129,193},{193,1... | collective-permute-start | bytes 393224 | tf_op jit(solution)/shard_map/ppermute | solution.py:176
  39.0 2.5 %collective-permute-start.6 = (f32[64,2048]{1,0:T(8,128)S(1)}, f32[64,2048]{1,0:T(8,128)}, u32[]{:S(2)}, u32[]{:S(2)}) collective-permute-start(f32[64,2048]{1,0:T(8,128)S(1)} %bitcast.60), channel_id=1, source_target_pairs={{0,1},{1,0},{2,3},{3,2},{4,5},{5,4},{6,7},{7,6},{8,9},{9,8},{10,11... | collective-permute-start | bytes 1572872 | tf_op jit(solution)/shard_map/ppermute | solution.py:145
  99.0 1.1 copy-start.1
  100.2 3.4 %collective-permute-start.7 = (bf16[6144,128]{1,0:T(8,128)(2,1)S(1)}, bf16[6144,128]{1,0:T(8,128)(2,1)S(1)}, u32[]{:S(2)}, u32[]{:S(2)}) collective-permute-start(bf16[6144,128]{1,0:T(8,128)(2,1)S(1)} %bitcast.55), channel_id=1, source_target_pairs={{0,1},{1,0},{2,3},{3,2},{4,5},{5,4},{6,7},{7,6},{8,9},{9,8},{10,11... | collective-permute-start | bytes 4718600 | tf_op jit(solution)/shard_map/ppermute | solution.py:145
  103.6 1.2 copy-start.3
  117.0 5.7 %copy-start.2 = (f32[6144,128]{1,0:T(8,128)S(1)}, f32[6144,128]{1,0:T(8,128)}, u32[]{:S(2)}) copy-start(f32[6144,128]{1,0:T(8,128)} %get-tuple-element.7) | copy-start | bytes 9437188
  119.2 3.5 %collective-permute-start.8 = (bf16[6144,128]{1,0:T(8,128)(2,1)S(1)}, bf16[6144,128]{1,0:T(8,128)(2,1)S(1)}, u32[]{:S(2)}, u32[]{:S(2)}) collective-permute-start(bf16[6144,128]{1,0:T(8,128)(2,1)S(1)} %convert_element_type.34), channel_id=1, source_target_pairs={{0,1},{1,0},{2,3},{3,2},{4,5},{5,4},{6,7},{7,6},{8,9},{9,8},{10,11... | collective-permute-start | bytes 4718600 | tf_op jit(solution)/shard_map/ppermute | solution.py:145
  124.2 7.7 %copy-start.6 = (f32[64,8]{0,1:T(8,128)S(1)}, f32[64,8]{0,1:T(8,128)}, u32[]{:S(2)}) copy-start(f32[64,8]{0,1:T(8,128)} %param.22) | copy-start | bytes 6148
  124.2 49.0 %all-to-all-start.1 = ((bf16[128,48,128]{2,1,0:T(8,128)(2,1)}), bf16[128,48,128]{2,1,0:T(8,128)(2,1)}, u32[]{:S(2)}, u32[]{:S(2)}) async-start(bf16[128,48,128]{2,1,0:T(8,128)(2,1)} %bitcast.58), calls=%async_computation.1 | async-start | bytes 3145728 | tf_op jit(solution)/shard_map/all_to_all | solution.py:210

commit v5 on v3

--- a/solution.py
+++ b/solution.py
@@ -2,6 +2,7 @@
 import jax.numpy as jnp
 from jax import lax
 from jax.experimental import pallas as pl
+from jax.experimental.pallas import tpu as pltpu
 from jax.sharding import PartitionSpec as P
 
 D = 2048
@@ -89,6 +90,78 @@
     )(queries, fresh_keys, fresh_values, resident_keys, resident_values)
 
 
+def gate_up_kernel(lane_ref, mine_ref, other_ref, g_own, g_other, u_own, u_other, act_ref):
+    fold = g_own.shape[0] // HEAD_WIDTH
+    rows = act_ref.shape[0]
+    x_mine = jnp.concatenate(
+        [mine_ref[pl.ds(j, rows, stride=fold), :] for j in range(fold)], axis=1
+    )
+    x_other = jnp.concatenate(
+        [other_ref[pl.ds(j, rows, stride=fold), :] for j in range(fold)], axis=1
+    )
+    gate = jnp.dot(x_mine, g_own[...], preferred_element_type=jnp.float32) + jnp.dot(
+        x_other, g_other[...], preferred_element_type=jnp.float32
+    )
+    up = jnp.dot(x_mine, u_own[...], preferred_element_type=jnp.float32) + jnp.dot(
+        x_other, u_other[...], preferred_element_type=jnp.float32
+    )
+    act_ref[...] = (gate / (1.0 + jnp.exp(-gate)) * up).astype(act_ref.dtype)
+
+
+def down_kernel(lane_ref, act_mine, act_other, d_own, d_other, out_ref):
+    fold = d_own.shape[1] // HEAD_WIDTH
+    rows = act_mine.shape[0]
+    out = jnp.dot(act_mine[...], d_own[...], preferred_element_type=jnp.float32) + jnp.dot(
+        act_other[...], d_other[...], preferred_element_type=jnp.float32
+    )
+    for j in range(fold):
+        out_ref[pl.ds(j, rows, stride=fold), :] = out[:, j * HEAD_WIDTH:(j + 1) * HEAD_WIDTH]
+
+
+def gate_up(lane, mine, other, gate_mat, up_mat, block_rows=256, interpret=False):
+    folded, lanes = mine.shape
+    half, hidden = gate_mat.shape[0] // 2, gate_mat.shape[1]
+    fold = half // lanes
+    rows = folded // fold
+    act_spec = pl.BlockSpec((block_rows * fold, lanes), lambda i, lane_ref: (i, 0))
+    own_rows = pl.BlockSpec((half, hidden), lambda i, lane_ref: (lane_ref[0], 0))
+    other_rows = pl.BlockSpec((half, hidden), lambda i, lane_ref: (1 - lane_ref[0], 0))
+    return pl.pallas_call(
+        gate_up_kernel,
+        grid_spec=pltpu.PrefetchScalarGridSpec(
+            num_scalar_prefetch=1,
+            grid=(rows // block_rows,),
+            in_specs=[act_spec, act_spec, own_rows, other_rows, own_rows, other_rows],
+            out_specs=pl.BlockSpec((block_rows, hidden), lambda i, lane_ref: (i, 0)),
+        ),
+        out_shape=jax.ShapeDtypeStruct((rows, hidden), jnp.bfloat16),
+        interpret=interpret,
+    )(lane, mine, other, gate_mat, gate_mat, up_mat, up_mat)
+
+
+def down(lane, act_mine, act_other, down_mat, down_other, block_rows=256, interpret=False):
+    rows, hidden = act_mine.shape
+    half = down_other.shape[1]
+    fold = half // HEAD_WIDTH
+    act_spec = pl.BlockSpec((block_rows, hidden), lambda i, lane_ref: (i, 0))
+    return pl.pallas_call(
+        down_kernel,
+        grid_spec=pltpu.PrefetchScalarGridSpec(
+            num_scalar_prefetch=1,
+            grid=(rows // block_rows,),
+            in_specs=[
+                act_spec,
+                act_spec,
+                pl.BlockSpec((hidden, half), lambda i, lane_ref: (0, lane_ref[0])),
+                pl.BlockSpec((hidden, half), lambda i, lane_ref: (0, 0)),
+            ],
+            out_specs=pl.BlockSpec((block_rows * fold, HEAD_WIDTH), lambda i, lane_ref: (i, 0)),
+        ),
+        out_shape=jax.ShapeDtypeStruct((rows * fold, HEAD_WIDTH), jnp.float32),
+        interpret=interpret,
+    )(lane, act_mine, act_other, down_mat, down_other)
+
+
 def swap_pair(x):
     return lax.ppermute(x, "tensor", [(0, 1), (1, 0)])
 
@@ -148,25 +221,12 @@
     ).astype(jnp.bfloat16)
     received = lax.all_to_all(
         outgoing.reshape(owners, CAP * width, lanes), ("dp", "expert"), split_axis=0, concat_axis=0, tiled=True
-    ).reshape(owners * CAP, width, lanes)
+    ).reshape(owners * CAP * width, lanes)
     other = swap_pair(received)
-    first = jnp.where(lane == 0, received, other)
-    second = jnp.where(lane == 0, other, received)
-    flat = jnp.concatenate([first, second], axis=1)
-
-    gate_part = jnp.einsum(
-        "rjl,jlh->rh", flat, w_gate[0].reshape(2 * width, lanes, -1), preferred_element_type=jnp.float32
-    )
-    up_part = jnp.einsum(
-        "rjl,jlh->rh", flat, w_up[0].reshape(2 * width, lanes, -1), preferred_element_type=jnp.float32
-    )
-    act = (jax.nn.silu(gate_part) * up_part).astype(jnp.bfloat16)
-    result = jnp.einsum(
-        "rh,hjl->rjl", act, w_down[0].reshape(act.shape[1], 2 * width, lanes), preferred_element_type=jnp.float32
-    )
-    own = lax.dynamic_slice_in_dim(result, lane * width, width, 1)
-    theirs = lax.dynamic_slice_in_dim(result, (1 - lane) * width, width, 1)
-    expert_out = (own + swap_pair(theirs)).astype(jnp.bfloat16)
+    lane_id = lane.astype(jnp.int32).reshape(1)
+    down_other = swap_pair(lax.dynamic_slice_in_dim(w_down[0], (1 - lane) * half, half, 1))
+    act = gate_up(lane_id, received, other, w_gate[0], w_up[0])
+    expert_out = down(lane_id, act, swap_pair(act), w_down[0], down_other).astype(jnp.bfloat16)
 
     returned = lax.all_to_all(
         expert_out.reshape(owners, CAP * width, lanes), ("dp", "expert"), split_axis=0, concat_axis=0, tiled=True

time: 179 us -> 174 us (0.972)
  Pallas kernels: 12.1 us -> 24.2 us
  local copies, waits for them, and re-layouts: 12.4 us -> 3.82 us
  matrix products: 11.7 us -> 6.26 us
  waiting for transfers between devices: 60.2 us -> 57.8 us
    pallas_call x0 -> x2, Pallas kernels: none -> 12.1 us  [the longest x1 6.68 us: gate_up(): pl.pallas_call(gate_up_kernel, grid_spec=pltpu.PrefetchScalarGridSpec(num...]
    dot_general x3 -> x0, matrix products: 5.41 us -> none  [the longest x1 1.84 us: per_device(): jnp.einsum('rh,hjl->rjl', act, w_down[0].reshape(act.shape[1], 2 * width,...]
    unnamed x21 -> x14, local copies, waits for them, and re-layouts: 4.79 us -> 0.85 us
    select_n x1 -> x0, other arithmetic: 2.36 us -> none  [per_device(): first = jnp.where(lane == 0, received, other)]
    ppermute x3 -> x4, waiting for transfers between devices: 6.53 us -> 4.18 us  [swap_pair(): return lax.ppermute(x, 'tensor', [(0, 1), (1, 0)])]
    convert_element_type x1 -> x0, local copies, waits for them, and re-layouts: 2.18 us -> none  [per_device(): expert_out = (own + swap_pair(theirs)).astype(jnp.bfloat16)]
  transfers between devices with their start and end apart: 10 -> 11, of which waited for: 8 -> 8; matrix products, arithmetic and copies ran while one was open for 5% -> 4% of each run, Pallas kernels for 0% -> 4%
where the time goes in v5:
time: 174 us
  waiting for transfers between devices  57.8 us (33%)
  blocking collectives  54.7 us (31%)
  Pallas kernels  24.2 us (14%)
  starting transfers between devices  18.6 us (11%)
  other arithmetic  8.13 us (5%)
  matrix products  6.26 us (4%)
  local copies, waits for them, and re-layouts  3.82 us (2%)
    all_to_all x1, blocking collectives, per_device(): lax.all_to_all(outgoing.reshape(owners, CAP * width, lanes), ('dp', 'expe...  54.7 us
    all_to_all x1, waiting for transfers between devices, per_device(): lax.all_to_all(expert_out.reshape(owners, CAP * width, lanes), ('dp', 'ex...  41.3 us
    pallas_call x1, Pallas kernels, attend_kernel(): pl.pallas_call(attention_kernel, grid=(kv_here,), in_specs=[pl.BlockSpec(...  12.1 us
    all_to_all x1, starting transfers between devices, per_device(): lax.all_to_all(expert_out.reshape(owners, CAP * width, lanes), ('dp', 'ex...  7.66 us
    pallas_call x1, Pallas kernels, gate_up(): pl.pallas_call(gate_up_kernel, grid_spec=pltpu.PrefetchScalarGridSpec(num...  6.68 us
    ppermute x3, waiting for transfers between devices, per_device(): blocks.append(lax.ppermute(product, 'dp', backward))  6.48 us
    ppermute x3, waiting for transfers between devices, per_device(): arrived = lax.ppermute(attended, 'dp', onward)  5.88 us
    ppermute x3, starting transfers between devices, per_device(): arrived = lax.ppermute(attended, 'dp', onward)  5.65 us
  transfers between devices with their start and end apart: 11, of which 8 were waited for; matrix products, arithmetic and copies ran while one was open for 4% of the time, Pallas kernels for 4%

profile of v5, /device:TPU:32, one launch (start us, length us, event | category | flops | bytes accessed | tf_op | source)
XLA Modules:
  0.0 173.7 jit_solution(8450408305913602318)
XLA Ops:
  0.0 0.0 copy-start
  0.0 12.1 %shard_map.127 = bf16[64,2048]{1,0:T(8,128)(2,1)} custom-call(bf16[64,2048]{1,0:T(8,128)(2,1)} %q_ref.1, bf16[64,256]{1,0:T(8,128)(2,1)} %kn_ref.1, bf16[64,256]{1,0:T(8,128)(2,1)} %vn_ref.1, bf16[1,2048,256]{2,1,0:T(8,128)(2,1)} %kr_ref.1, bf16[1,2048,256]{2,1,0:T(8,128)(2,1)} %vr_ref.1), custom_call_target="tpu_custom_call" | custom-call | tf_op jit(solution)/shard_map/pallas_call | solution.py:77
  12.1 1.5 collective-permute-start
  13.6 2.7 %collective-permute-start.2 = (bf16[64,2048]{1,0:T(8,128)(2,1)}, bf16[64,2048]{1,0:T(8,128)(2,1)S(1)}, u32[]{:S(2)}, u32[]{:S(2)}) collective-permute-start(bf16[64,2048]{1,0:T(8,128)(2,1)} %shard_map.127), channel_id=1, source_target_pairs={{0,128},{64,192},{128,0},{192,64},{1,129},{65,193},{129,1},{193,65... | collective-permute-start | bytes 786440 | tf_op jit(solution)/shard_map/ppermute | solution.py:195
  16.3 1.4 collective-permute-start.4
  17.7 0.0 copy-done
  17.7 1.4 convolution_bitcast_fusion
  19.2 2.5 %collective-permute-done = bf16[64,2048]{1,0:T(8,128)(2,1)S(1)} collective-permute-done((bf16[64,2048]{1,0:T(8,128)(2,1)}, bf16[64,2048]{1,0:T(8,128)(2,1)S(1)}, u32[]{:S(2)}, u32[]{:S(2)}) %collective-permute-start) | collective-permute-done | bytes 262176 | tf_op jit(solution)/shard_map/ppermute | solution.py:195
  21.7 0.5 fusion.14
  22.2 2.6 %collective-permute-start.1 = (f32[64,512]{1,0:T(8,128)S(1)}, f32[64,512]{1,0:T(8,128)S(1)}, u32[]{:S(2)}, u32[]{:S(2)}) collective-permute-start(f32[64,512]{1,0:T(8,128)S(1)} %fusion.14), channel_id=1, source_target_pairs={{0,192},{64,0},{128,64},{192,128},{1,193},{65,1},{129,65},{193,129... | collective-permute-start | bytes 393224 | tf_op jit(solution)/shard_map/ppermute | solution.py:197
  24.8 3.4 %collective-permute-done.2 = bf16[64,2048]{1,0:T(8,128)(2,1)S(1)} collective-permute-done((bf16[64,2048]{1,0:T(8,128)(2,1)}, bf16[64,2048]{1,0:T(8,128)(2,1)S(1)}, u32[]{:S(2)}, u32[]{:S(2)}) %collective-permute-start.2) | collective-permute-done | bytes 262176 | tf_op jit(solution)/shard_map/ppermute | solution.py:195
  28.1 0.5 fusion.15
  28.6 0.0 copy-start.4
  28.6 0.9 collective-permute-start.3
  29.5 0.0 collective-permute-done.4
  29.6 0.5 fusion.16
  30.0 0.8 collective-permute-start.5
  30.8 0.0 copy-done.4
  30.8 0.1 copy.34
  30.9 1.1 collective-permute-done.1
  32.0 4.0 %collective-permute-done.3 = f32[64,512]{1,0:T(8,128)S(1)} collective-permute-done((f32[64,512]{1,0:T(8,128)S(1)}, f32[64,512]{1,0:T(8,128)S(1)}, u32[]{:S(2)}, u32[]{:S(2)}) %collective-permute-start.3) | collective-permute-done | bytes 131104 | tf_op jit(solution)/shard_map/ppermute | solution.py:197
  36.0 1.4 collective-permute-done.5
  37.4 0.0 copy-start.3
  37.4 0.7 copy-done.3
  38.1 0.9 pad_maximum_fusion
  39.0 0.0 copy-start.2
  39.0 0.6 gather_fusion
  39.6 0.0 copy-start.1
  39.7 0.3 collective-permute-start.6
  39.9 0.1 convert_reduce_fusion
  40.1 0.1 reduce_window_sum.11
  40.2 1.2 select_reduce_fusion
  41.4 0.1 copy.35
  41.5 0.1 copy.36
  41.6 0.0 dynamic-slice-start
  41.6 0.5 fusion.5
  42.1 0.0 copy-done.1
  42.2 0.0 collective-permute-done.6
  42.2 0.0 copy-done.2
  42.2 1.2 multiply_reduce_fusion.1
  43.4 0.0 dynamic-slice-done
  43.4 0.6 convolution_convert_fusion
  44.1 1.0 copy.38
  45.1 54.7 %all_to_all.10 = bf16[128,48,128]{2,1,0:T(8,128)(2,1)} all-to-all(bf16[128,48,128]{2,1,0:T(8,128)(2,1)S(1)} %bitcast.55), channel_id=1, replica_groups=mesh['dp'=4,'expert'=32,'tensor'=2] {'dp','expert'}, dimensions={0} | all-to-all | bytes 3145728 | tf_op jit(solution)/shard_map/all_to_all | solution.py:222
  99.8 0.0 collective-permute-start.7
  99.8 1.2 dynamic-slice_bitcast_fusion
  101.0 0.6 collective-permute-start.9
  101.6 2.0 %collective-permute-done.7.other_ref = bf16[6144,128]{1,0:T(8,128)(2,1)} collective-permute-done((bf16[6144,128]{1,0:T(8,128)(2,1)}, bf16[6144,128]{1,0:T(8,128)(2,1)}, u32[]{:S(2)}, u32[]{:S(2)}) %collective-permute-start.7) | collective-permute-done | bytes 1572896 | tf_op jit(solution)/shard_map/ppermute | solution.py:166
  103.6 6.7 %shard_map.128.act_mine = bf16[768,384]{1,0:T(8,128)(2,1)} custom-call(s32[1]{0:T(128)} %bitcast.8.lane_ref, bf16[6144,128]{1,0:T(8,128)(2,1)} %bitcast.11.mine_ref, bf16[6144,128]{1,0:T(8,128)(2,1)} %collective-permute-done.7.other_ref, bf16[2048,384]{1,0:T(8,128)(2,1)} %bitcast.51, bf16[2048,384]{1,0:T(8,128)(2,1)} %bitcast.52, ...), custom_call_target="tpu_custom_call" | custom-call | tf_op jit(solution)/shard_map/pallas_call | solution.py:129
  110.2 0.1 collective-permute-start.8
  110.4 0.0 collective-permute-done.9.d_other
  110.4 2.2 %collective-permute-done.8.act_other = bf16[768,384]{1,0:T(8,128)(2,1)} collective-permute-done((bf16[768,384]{1,0:T(8,128)(2,1)}, bf16[768,384]{1,0:T(8,128)(2,1)}, u32[]{:S(2)}, u32[]{:S(2)}) %collective-permute-start.8) | collective-permute-done | bytes 589856 | tf_op jit(solution)/shard_map/ppermute | solution.py:166
  112.6 5.4 %shard_map.129 = f32[6144,128]{1,0:T(8,128)} custom-call(s32[1]{0:T(128)} %bitcast.8.lane_ref, bf16[768,384]{1,0:T(8,128)(2,1)} %shard_map.128.act_mine, bf16[768,384]{1,0:T(8,128)(2,1)} %collective-permute-done.8.act_other, bf16[384,2048]{1,0:T(8,128)(2,1)} %bitcast.57, bf16[384,1024]{1,0:T(8,128)(2,1)} %collective-permute-done.9.d_other), custom_call_target="tpu_custom_call" | custom-call | tf_op jit(solution)/shard_map/pallas_call | solution.py:147
  118.0 3.2 %convert_element_type.28 = bf16[6144,128]{1,0:T(8,128)(2,1)} convert(f32[6144,128]{1,0:T(8,128)} %shard_map.129) | non-fusion elementwise | flops 786432 | bytes 4718592 | tf_op jit(solution)/shard_map/convert_element_type | solution.py:229
  121.2 0.0 copy-start.5
  121.2 7.7 %all-to-all-start.1 = ((bf16[128,48,128]{2,1,0:T(8,128)(2,1)}), bf16[128,48,128]{2,1,0:T(8,128)(2,1)}, u32[]{:S(2)}, u32[]{:S(2)}) async-start(bf16[128,48,128]{2,1,0:T(8,128)(2,1)} %bitcast.56), calls=%async_computation.1 | async-start | bytes 3145728 | tf_op jit(solution)/shard_map/all_to_all | solution.py:231
  128.9 0.0 copy-done.5
  128.9 0.1 copy.33
  129.0 41.3 %all-to-all-done.1 = bf16[128,48,128]{2,1,0:T(8,128)(2,1)} async-done(((bf16[128,48,128]{2,1,0:T(8,128)(2,1)}), bf16[128,48,128]{2,1,0:T(8,128)(2,1)}, u32[]{:S(2)}, u32[]{:S(2)}) %all-to-all-start.1) | async-done | bytes 1572896 | tf_op jit(solution)/shard_map/all_to_all | solution.py:231
  170.2 2.8 %multiply_reduce_fusion = f32[64,8,128]{2,1,0:T(8,128)S(1)} fusion(bf16[768,8,128]{2,1,0:T(8,128)(2,1)} %bitcast.17, f32[64,8]{1,0:T(8,128)S(1)} %copy.33, s32[64,8]{1,0:T(8,128)S(1)} %copy.36), kind=kOutput, calls=%fused_computation.1 | convolution fusion | flops 806682624 | bytes 1839104 | tf_op jit(solution)/shard_map/tkr,rjl->tkjl/dot_general | solution.py:234
  173.0 0.7 fusion.7
  (6 shorter events, 0.1 us)
Async XLA Ops:
  0.0 17.7 %copy-start = (bf16[2048,512]{1,0:T(8,128)(2,1)S(1)}, bf16[2048,512]{1,0:T(8,128)(2,1)}, u32[]{:S(2)}) copy-start(bf16[2048,512]{1,0:T(8,128)(2,1)} %param.18) | copy-start | bytes 6291460
  12.1 9.6 %collective-permute-start = (bf16[64,2048]{1,0:T(8,128)(2,1)}, bf16[64,2048]{1,0:T(8,128)(2,1)S(1)}, u32[]{:S(2)}, u32[]{:S(2)}) collective-permute-start(bf16[64,2048]{1,0:T(8,128)(2,1)} %shard_map.127), channel_id=1, source_target_pairs={{0,64},{64,128},{128,192},{192,0},{1,65},{65,129},{129,193},{193,1... | collective-permute-start | bytes 786440 | tf_op jit(solution)/shard_map/ppermute | solution.py:195
  13.6 14.6 %collective-permute-start.2 = (bf16[64,2048]{1,0:T(8,128)(2,1)}, bf16[64,2048]{1,0:T(8,128)(2,1)S(1)}, u32[]{:S(2)}, u32[]{:S(2)}) collective-permute-start(bf16[64,2048]{1,0:T(8,128)(2,1)} %shard_map.127), channel_id=1, source_target_pairs={{0,128},{64,192},{128,0},{192,64},{1,129},{65,193},{129,1},{193,65... | collective-permute-start | bytes 786440 | tf_op jit(solution)/shard_map/ppermute | solution.py:195
  16.3 13.3 %collective-permute-start.4 = (bf16[64,2048]{1,0:T(8,128)(2,1)}, bf16[64,2048]{1,0:T(8,128)(2,1)S(1)}, u32[]{:S(2)}, u32[]{:S(2)}) collective-permute-start(bf16[64,2048]{1,0:T(8,128)(2,1)} %shard_map.127), channel_id=1, source_target_pairs={{0,192},{64,0},{128,64},{192,128},{1,193},{65,1},{129,65},{193,129... | collective-permute-start | bytes 786440 | tf_op jit(solution)/shard_map/ppermute | solution.py:195
  22.2 9.8 %collective-permute-start.1 = (f32[64,512]{1,0:T(8,128)S(1)}, f32[64,512]{1,0:T(8,128)S(1)}, u32[]{:S(2)}, u32[]{:S(2)}) collective-permute-start(f32[64,512]{1,0:T(8,128)S(1)} %fusion.14), channel_id=1, source_target_pairs={{0,192},{64,0},{128,64},{192,128},{1,193},{65,1},{129,65},{193,129... | collective-permute-start | bytes 393224 | tf_op jit(solution)/shard_map/ppermute | solution.py:197
  28.6 2.2 %copy-start.4 = (s32[64,8]{0,1:T(8,128)S(1)}, s32[64,8]{0,1:T(8,128)}, u32[]{:S(2)}) copy-start(s32[64,8]{0,1:T(8,128)} %param.21) | copy-start | bytes 6148
  28.6 7.4 %collective-permute-start.3 = (f32[64,512]{1,0:T(8,128)S(1)}, f32[64,512]{1,0:T(8,128)S(1)}, u32[]{:S(2)}, u32[]{:S(2)}) collective-permute-start(f32[64,512]{1,0:T(8,128)S(1)} %fusion.15), channel_id=1, source_target_pairs={{0,128},{64,192},{128,0},{192,64},{1,129},{65,193},{129,1},{193,65... | collective-permute-start | bytes 393224 | tf_op jit(solution)/shard_map/ppermute | solution.py:197
  30.0 7.4 %collective-permute-start.5 = (f32[64,512]{1,0:T(8,128)S(1)}, f32[64,512]{1,0:T(8,128)S(1)}, u32[]{:S(2)}, u32[]{:S(2)}) collective-permute-start(f32[64,512]{1,0:T(8,128)S(1)} %fusion.16), channel_id=1, source_target_pairs={{0,64},{64,128},{128,192},{192,0},{1,65},{65,129},{129,193},{193,1... | collective-permute-start | bytes 393224 | tf_op jit(solution)/shard_map/ppermute | solution.py:197
  37.4 0.7 copy-start.3
  39.0 3.2 %copy-start.2 = (bf16[64,2048]{1,0:T(8,128)(2,1)S(1)}, bf16[64,2048]{1,0:T(8,128)(2,1)}, u32[]{:S(2)}) copy-start(bf16[64,2048]{1,0:T(8,128)(2,1)} %param.19) | copy-start | bytes 786436
  39.6 2.5 %copy-start.1 = (f32[4,8,8,512]{3,2,0,1:T(8,128)}, f32[4,8,8,512]{3,2,0,1:T(8,128)S(1)}, u32[]{:S(2)}) copy-start(f32[4,8,8,512]{3,2,0,1:T(8,128)S(1)} %copy.42) | copy-start | bytes 1572868
  39.7 2.5 %collective-permute-start.6 = (f32[64,2048]{1,0:T(8,128)S(1)}, f32[64,2048]{1,0:T(8,128)S(1)}, u32[]{:S(2)}, u32[]{:S(2)}) collective-permute-start(f32[64,2048]{1,0:T(8,128)S(1)} %bitcast.59), channel_id=1, source_target_pairs={{0,1},{1,0},{2,3},{3,2},{4,5},{5,4},{6,7},{7,6},{8,9},{9,8},{10,11... | collective-permute-start | bytes 1572872 | tf_op jit(solution)/shard_map/ppermute | solution.py:166
  41.6 1.8 %dynamic-slice-start = ((f32[2048]{0:T(1024)}, s32[]{:T(128)}), f32[1024]{0:T(1024)S(1)}, s32[]{:S(2)}) async-start(f32[2048]{0:T(1024)} %param.20, s32[]{:T(128)} %select_n.33), calls=%async_computation.2 | async-start | bytes 8704 | tf_op jit(solution)/shard_map/dynamic_slice | solution.py:206
  99.8 3.8 %collective-permute-start.7 = (bf16[6144,128]{1,0:T(8,128)(2,1)}, bf16[6144,128]{1,0:T(8,128)(2,1)}, u32[]{:S(2)}, u32[]{:S(2)}) collective-permute-start(bf16[6144,128]{1,0:T(8,128)(2,1)} %bitcast.11.mine_ref), channel_id=1, source_target_pairs={{0,1},{1,0},{2,3},{3,2},{4,5},{5,4},{6,7},{7,6},{8,9},{9,8},{10,11... | collective-permute-start | bytes 4718600 | tf_op jit(solution)/shard_map/ppermute | solution.py:166
  101.0 9.4 %collective-permute-start.9 = (bf16[384,1024]{1,0:T(8,128)(2,1)S(1)}, bf16[384,1024]{1,0:T(8,128)(2,1)}, u32[]{:S(2)}, u32[]{:S(2)}) collective-permute-start(bf16[384,1024]{1,0:T(8,128)(2,1)S(1)} %dynamic-slice_bitcast_fusion), channel_id=1, source_target_pairs={{0,1},{1,0},{2,3},{3,2},{4,5},{5,4},{6,7},{7,6},{8,9},{9,8},{10,11... | collective-permute-start | bytes 2359304 | tf_op jit(solution)/shard_map/ppermute | solution.py:166
  110.2 2.3 %collective-permute-start.8 = (bf16[768,384]{1,0:T(8,128)(2,1)}, bf16[768,384]{1,0:T(8,128)(2,1)}, u32[]{:S(2)}, u32[]{:S(2)}) collective-permute-start(bf16[768,384]{1,0:T(8,128)(2,1)} %shard_map.128.act_mine), channel_id=1, source_target_pairs={{0,1},{1,0},{2,3},{3,2},{4,5},{5,4},{6,7},{7,6},{8,9},{9,8},{10,11... | collective-permute-start | bytes 1769480 | tf_op jit(solution)/shard_map/ppermute | solution.py:166
  121.2 7.7 %copy-start.5 = (f32[64,8]{0,1:T(8,128)S(1)}, f32[64,8]{0,1:T(8,128)}, u32[]{:S(2)}) copy-start(f32[64,8]{0,1:T(8,128)} %param.22) | copy-start | bytes 6148
  121.2 49.0 %all-to-all-start.1 = ((bf16[128,48,128]{2,1,0:T(8,128)(2,1)}), bf16[128,48,128]{2,1,0:T(8,128)(2,1)}, u32[]{:S(2)}, u32[]{:S(2)}) async-start(bf16[128,48,128]{2,1,0:T(8,128)(2,1)} %bitcast.56), calls=%async_computation.1 | async-start | bytes 3145728 | tf_op jit(solution)/shard_map/all_to_all | solution.py:231

commit v6 on v5

--- a/solution.py
+++ b/solution.py
@@ -114,8 +114,7 @@
     out = jnp.dot(act_mine[...], d_own[...], preferred_element_type=jnp.float32) + jnp.dot(
         act_other[...], d_other[...], preferred_element_type=jnp.float32
     )
-    for j in range(fold):
-        out_ref[pl.ds(j, rows, stride=fold), :] = out[:, j * HEAD_WIDTH:(j + 1) * HEAD_WIDTH]
+    out_ref[...] = out.astype(out_ref.dtype)
 
 
 def gate_up(lane, mine, other, gate_mat, up_mat, block_rows=256, interpret=False):
@@ -155,9 +154,9 @@
                 pl.BlockSpec((hidden, half), lambda i, lane_ref: (0, lane_ref[0])),
                 pl.BlockSpec((hidden, half), lambda i, lane_ref: (0, 0)),
             ],
-            out_specs=pl.BlockSpec((block_rows * fold, HEAD_WIDTH), lambda i, lane_ref: (i, 0)),
+            out_specs=pl.BlockSpec((block_rows, half), lambda i, lane_ref: (i, 0)),
         ),
-        out_shape=jax.ShapeDtypeStruct((rows * fold, HEAD_WIDTH), jnp.float32),
+        out_shape=jax.ShapeDtypeStruct((rows, half), jnp.bfloat16),
         interpret=interpret,
     )(lane, act_mine, act_other, down_mat, down_other)
 
@@ -186,6 +185,8 @@
     half = D // lax.axis_size("tensor")
     groups = lax.axis_size("dp")
     attended = attend_kernel(queries, fresh_keys, fresh_values, resident_keys, resident_values)
+    down_other = swap_pair(lax.dynamic_slice_in_dim(w_down[0], (1 - lane) * half, half, 1))
+    attended, down_other = lax.optimization_barrier((attended, down_other))
 
     here = lax.axis_index("dp")
     blocks = [jnp.dot(attended, out_weight, preferred_element_type=jnp.float32)]
@@ -224,9 +225,8 @@
     ).reshape(owners * CAP * width, lanes)
     other = swap_pair(received)
     lane_id = lane.astype(jnp.int32).reshape(1)
-    down_other = swap_pair(lax.dynamic_slice_in_dim(w_down[0], (1 - lane) * half, half, 1))
     act = gate_up(lane_id, received, other, w_gate[0], w_up[0])
-    expert_out = down(lane_id, act, swap_pair(act), w_down[0], down_other).astype(jnp.bfloat16)
+    expert_out = down(lane_id, act, swap_pair(act), w_down[0], down_other)
 
     returned = lax.all_to_all(
         expert_out.reshape(owners, CAP * width, lanes), ("dp", "expert"), split_axis=0, concat_axis=0, tiled=True

time: 174 us -> 178 us (1.023)
  local copies, waits for them, and re-layouts: 3.82 us -> 10.1 us
  other arithmetic: 8.13 us -> 4.04 us
  waiting for transfers between devices: 57.8 us -> 61.6 us
    reshape x0 -> x1, local copies, waits for them, and re-layouts: none -> 3.7 us  [per_device(): expert_out.reshape(owners, CAP * width, lanes)]
    convert_element_type x1 -> x0, other arithmetic: 3.19 us -> none  [per_device(): down(lane_id, act, swap_pair(act), w_down[0], down_other)]
    unnamed x14 -> x20, local copies, waits for them, and re-layouts: 0.85 us -> 3.33 us
    ppermute x3, waiting for transfers between devices: 5.88 us -> 8.27 us  [per_device(): arrived = lax.ppermute(attended, 'dp', onward)]
  transfers between devices with their start and end apart: 11 -> 11, of which waited for: 8 -> 8; matrix products, arithmetic and copies ran while one was open for 4% -> 2% of each run, Pallas kernels for 4% -> 7%
where the time goes in v6:
time: 178 us; the launch traced here: 177 us
  waiting for transfers between devices  61.6 us (35%)
  blocking collectives  54.5 us (31%)
  Pallas kernels  23.6 us (13%)
  starting transfers between devices  17.9 us (10%)
  local copies, waits for them, and re-layouts  10.1 us (6%)
  matrix products  5.28 us (3%)
  other arithmetic  4.04 us (2%)
    all_to_all x1, blocking collectives, per_device(): lax.all_to_all(outgoing.reshape(owners, CAP * width, lanes), ('dp', 'expe...  54.5 us
    all_to_all x1, waiting for transfers between devices, per_device(): lax.all_to_all(expert_out.reshape(owners, CAP * width, lanes), ('dp', 'ex...  41.3 us
    pallas_call x1, Pallas kernels, attend_kernel(): pl.pallas_call(attention_kernel, grid=(kv_here,), in_specs=[pl.BlockSpec(...  11.9 us
    ppermute x3, waiting for transfers between devices, per_device(): arrived = lax.ppermute(attended, 'dp', onward)  8.27 us
    all_to_all x1, starting transfers between devices, per_device(): lax.all_to_all(expert_out.reshape(owners, CAP * width, lanes), ('dp', 'ex...  7.66 us
    pallas_call x1, Pallas kernels, gate_up(): pl.pallas_call(gate_up_kernel, grid_spec=pltpu.PrefetchScalarGridSpec(num...  6.68 us
    ppermute x3, waiting for transfers between devices, per_device(): blocks.append(lax.ppermute(product, 'dp', backward))  6.57 us
    ppermute x3, starting transfers between devices, per_device(): arrived = lax.ppermute(attended, 'dp', onward)  5.74 us
  transfers between devices with their start and end apart: 11, of which 8 were waited for; matrix products, arithmetic and copies ran while one was open for 2% of the time, Pallas kernels for 7%

profile of v6, /device:TPU:32, one launch (start us, length us, event | category | flops | bytes accessed | tf_op | source)
XLA Modules:
  0.0 177.4 jit_solution(14325004717091178715)
XLA Ops:
  0.0 0.0 copy-start
  0.0 1.3 dynamic-slice_bitcast_fusion
  1.3 0.0 copy-start.7
  1.4 0.1 collective-permute-start
  1.5 11.9 %shard_map.127 = bf16[64,2048]{1,0:T(8,128)(2,1)} custom-call(bf16[64,2048]{1,0:T(8,128)(2,1)} %q_ref.1, bf16[64,256]{1,0:T(8,128)(2,1)} %kn_ref.1, bf16[64,256]{1,0:T(8,128)(2,1)} %vn_ref.1, bf16[1,2048,256]{2,1,0:T(8,128)(2,1)} %kr_ref.1, bf16[1,2048,256]{2,1,0:T(8,128)(2,1)} %vr_ref.1), custom_call_target="tpu_custom_call" | custom-call | tf_op jit(solution)/shard_map/pallas_call | solution.py:77
  13.4 0.0 collective-permute-done.d_other
  13.4 1.5 collective-permute-start.1
  14.9 0.0 copy-done.7
  14.9 0.1 copy.34
  15.0 2.8 %collective-permute-start.3 = (bf16[64,2048]{1,0:T(8,128)(2,1)}, bf16[64,2048]{1,0:T(8,128)(2,1)S(1)}, u32[]{:S(2)}, u32[]{:S(2)}) collective-permute-start(bf16[64,2048]{1,0:T(8,128)(2,1)} %shard_map.127), channel_id=1, source_target_pairs={{0,128},{64,192},{128,0},{192,64},{1,129},{65,193},{129,1},{193,65... | collective-permute-start | bytes 786440 | tf_op jit(solution)/shard_map/ppermute | solution.py:196
  17.8 1.4 collective-permute-start.5
  19.2 4.3 %collective-permute-done.1 = bf16[64,2048]{1,0:T(8,128)(2,1)S(1)} collective-permute-done((bf16[64,2048]{1,0:T(8,128)(2,1)}, bf16[64,2048]{1,0:T(8,128)(2,1)S(1)}, u32[]{:S(2)}, u32[]{:S(2)}) %collective-permute-start.1) | collective-permute-done | bytes 262176 | tf_op jit(solution)/shard_map/ppermute | solution.py:196
  23.5 0.0 copy-done
  23.5 0.5 fusion.14
  24.0 2.1 %collective-permute-start.2 = (f32[64,512]{1,0:T(8,128)S(1)}, f32[64,512]{1,0:T(8,128)S(1)}, u32[]{:S(2)}, u32[]{:S(2)}) collective-permute-start(f32[64,512]{1,0:T(8,128)S(1)} %fusion.14), channel_id=1, source_target_pairs={{0,192},{64,0},{128,64},{192,128},{1,193},{65,1},{129,65},{193,129... | collective-permute-start | bytes 393224 | tf_op jit(solution)/shard_map/ppermute | solution.py:198
  26.1 4.0 %collective-permute-done.3 = bf16[64,2048]{1,0:T(8,128)(2,1)S(1)} collective-permute-done((bf16[64,2048]{1,0:T(8,128)(2,1)}, bf16[64,2048]{1,0:T(8,128)(2,1)S(1)}, u32[]{:S(2)}, u32[]{:S(2)}) %collective-permute-start.3) | collective-permute-done | bytes 262176 | tf_op jit(solution)/shard_map/ppermute | solution.py:196
  30.1 0.5 fusion.15
  30.6 0.0 copy-start.4
  30.6 0.9 collective-permute-start.4
  31.5 0.0 collective-permute-done.5
  31.5 0.5 fusion.16
  32.0 1.0 collective-permute-start.6
  33.0 0.0 copy-done.4
  33.0 0.5 convolution_bitcast_fusion
  33.4 0.1 collective-permute-done.2
  33.5 5.0 %collective-permute-done.4 = f32[64,512]{1,0:T(8,128)S(1)} collective-permute-done((f32[64,512]{1,0:T(8,128)S(1)}, f32[64,512]{1,0:T(8,128)S(1)}, u32[]{:S(2)}, u32[]{:S(2)}) %collective-permute-start.4) | collective-permute-done | bytes 131104 | tf_op jit(solution)/shard_map/ppermute | solution.py:198
  38.6 1.5 collective-permute-done.6
  40.1 0.0 copy-start.6
  40.1 0.6 gather_fusion
  40.7 0.0 copy-start.2
  40.7 0.3 collective-permute-start.7
  41.0 0.1 convert_reduce_fusion
  41.2 0.1 reduce_window_sum.11
  41.3 1.2 select_reduce_fusion
  42.5 0.1 copy.35
  42.6 0.1 copy.36
  42.7 0.0 dynamic-slice-start
  42.7 0.5 fusion.5
  43.2 0.0 copy-done.2
  43.2 0.0 collective-permute-done.7
  43.2 0.0 copy-done.6
  43.2 1.2 multiply_reduce_fusion.1
  44.5 0.0 dynamic-slice-done
  44.5 0.6 convolution_convert_fusion
  45.1 1.0 copy.38
  46.1 54.5 %all_to_all.10 = bf16[128,48,128]{2,1,0:T(8,128)(2,1)S(1)} all-to-all(bf16[128,48,128]{2,1,0:T(8,128)(2,1)S(1)} %bitcast.56), channel_id=1, replica_groups=mesh['dp'=4,'expert'=32,'tensor'=2] {'dp','expert'}, dimensions={0} | all-to-all | bytes 3145728 | tf_op jit(solution)/shard_map/all_to_all | solution.py:223
  100.7 0.0 copy-start.1
  100.7 1.2 copy-done.1
  101.8 0.0 collective-permute-start.8
  101.8 3.4 %collective-permute-done.8.other_ref = bf16[6144,128]{1,0:T(8,128)(2,1)S(1)} collective-permute-done((bf16[6144,128]{1,0:T(8,128)(2,1)S(1)}, bf16[6144,128]{1,0:T(8,128)(2,1)S(1)}, u32[]{:S(2)}, u32[]{:S(2)}) %collective-permute-start.8) | collective-permute-done | bytes 1572896 | tf_op jit(solution)/shard_map/ppermute | solution.py:165
  105.2 0.0 copy-start.3
  105.2 1.2 copy-done.3
  106.4 6.7 %shard_map.128.act_mine = bf16[768,384]{1,0:T(8,128)(2,1)} custom-call(s32[1]{0:T(128)} %bitcast.9.lane_ref, bf16[6144,128]{1,0:T(8,128)(2,1)} %bitcast.55, bf16[6144,128]{1,0:T(8,128)(2,1)} %copy-done.3, bf16[2048,384]{1,0:T(8,128)(2,1)} %bitcast.50, bf16[2048,384]{1,0:T(8,128)(2,1)} %bitcast.51, bf16[2048,384]{1,0:T(8,128)(2,1)} %bitcast.52, ...), custom_call_target="tpu_custom_call" | custom-call | tf_op jit(solution)/shard_map/pallas_call | solution.py:128
  113.1 0.1 collective-permute-start.9
  113.2 2.1 %collective-permute-done.9.act_other = bf16[768,384]{1,0:T(8,128)(2,1)S(1)} collective-permute-done((bf16[768,384]{1,0:T(8,128)(2,1)}, bf16[768,384]{1,0:T(8,128)(2,1)S(1)}, u32[]{:S(2)}, u32[]{:S(2)}) %collective-permute-start.9) | collective-permute-done | bytes 589856 | tf_op jit(solution)/shard_map/ppermute | solution.py:165
  115.3 0.8 copy-done.5
  116.1 5.0 %shard_map.129 = bf16[768,1024]{1,0:T(8,128)(2,1)} custom-call(s32[1]{0:T(128)} %bitcast.9.lane_ref, bf16[768,384]{1,0:T(8,128)(2,1)} %shard_map.128.act_mine, bf16[768,384]{1,0:T(8,128)(2,1)} %copy-done.5, bf16[384,2048]{1,0:T(8,128)(2,1)} %bitcast.57, bf16[384,1024]{1,0:T(8,128)(2,1)} %collective-permute-done.d_other), custom_call_target="tpu_custom_call" | custom-call | tf_op jit(solution)/shard_map/pallas_call | solution.py:146
  121.1 3.7 %reshape.100 = bf16[128,48,128]{2,1,0:T(8,128)(2,1)} reshape(bf16[768,1024]{1,0:T(8,128)(2,1)} %shard_map.129) | data formatting | bytes 3145728 | tf_op jit(solution)/shard_map/reshape | solution.py:232
  124.8 7.7 %all-to-all-start.1 = ((bf16[128,48,128]{2,1,0:T(8,128)(2,1)}), bf16[128,48,128]{2,1,0:T(8,128)(2,1)}, u32[]{:S(2)}, u32[]{:S(2)}) async-start(bf16[128,48,128]{2,1,0:T(8,128)(2,1)} %reshape.100), calls=%async_computation.1 | async-start | bytes 3145728 | tf_op jit(solution)/shard_map/all_to_all | solution.py:231
  132.5 0.0 copy-done.8
  132.5 0.1 copy.33
  132.6 41.3 %all-to-all-done.1 = bf16[128,48,128]{2,1,0:T(8,128)(2,1)} async-done(((bf16[128,48,128]{2,1,0:T(8,128)(2,1)}), bf16[128,48,128]{2,1,0:T(8,128)(2,1)}, u32[]{:S(2)}, u32[]{:S(2)}) %all-to-all-start.1) | async-done | bytes 1572896 | tf_op jit(solution)/shard_map/all_to_all | solution.py:231
  173.9 2.8 %multiply_reduce_fusion = f32[64,8,128]{2,1,0:T(8,128)S(1)} fusion(bf16[768,8,128]{2,1,0:T(8,128)(2,1)} %bitcast.16, f32[64,8]{1,0:T(8,128)S(1)} %copy.33, s32[64,8]{1,0:T(8,128)S(1)} %copy.36), kind=kOutput, calls=%fused_computation.1 | convolution fusion | flops 806682624 | bytes 1839104 | tf_op jit(solution)/shard_map/tkr,rjl->tkjl/dot_general | solution.py:234
  176.6 0.7 fusion.7
  (9 shorter events, 0.1 us)
Async XLA Ops:
  0.0 23.5 %copy-start = (bf16[2048,512]{1,0:T(8,128)(2,1)S(1)}, bf16[2048,512]{1,0:T(8,128)(2,1)}, u32[]{:S(2)}) copy-start(bf16[2048,512]{1,0:T(8,128)(2,1)} %param.18) | copy-start | bytes 6291460
  1.3 13.5 %copy-start.7 = (s32[64,8]{0,1:T(8,128)S(1)}, s32[64,8]{0,1:T(8,128)}, u32[]{:S(2)}) copy-start(s32[64,8]{0,1:T(8,128)} %param.21) | copy-start | bytes 6148
  1.4 12.0 %collective-permute-start = (bf16[384,1024]{1,0:T(8,128)(2,1)S(1)}, bf16[384,1024]{1,0:T(8,128)(2,1)}, u32[]{:S(2)}, u32[]{:S(2)}) collective-permute-start(bf16[384,1024]{1,0:T(8,128)(2,1)S(1)} %dynamic-slice_bitcast_fusion), channel_id=1, source_target_pairs={{0,1},{1,0},{2,3},{3,2},{4,5},{5,4},{6,7},{7,6},{8,9},{9,8},{10,11... | collective-permute-start | bytes 2359304 | tf_op jit(solution)/shard_map/ppermute | solution.py:165
  13.4 10.1 %collective-permute-start.1 = (bf16[64,2048]{1,0:T(8,128)(2,1)}, bf16[64,2048]{1,0:T(8,128)(2,1)S(1)}, u32[]{:S(2)}, u32[]{:S(2)}) collective-permute-start(bf16[64,2048]{1,0:T(8,128)(2,1)} %shard_map.127), channel_id=1, source_target_pairs={{0,64},{64,128},{128,192},{192,0},{1,65},{65,129},{129,193},{193,1... | collective-permute-start | bytes 786440 | tf_op jit(solution)/shard_map/ppermute | solution.py:196
  15.0 15.1 %collective-permute-start.3 = (bf16[64,2048]{1,0:T(8,128)(2,1)}, bf16[64,2048]{1,0:T(8,128)(2,1)S(1)}, u32[]{:S(2)}, u32[]{:S(2)}) collective-permute-start(bf16[64,2048]{1,0:T(8,128)(2,1)} %shard_map.127), channel_id=1, source_target_pairs={{0,128},{64,192},{128,0},{192,64},{1,129},{65,193},{129,1},{193,65... | collective-permute-start | bytes 786440 | tf_op jit(solution)/shard_map/ppermute | solution.py:196
  17.8 13.7 %collective-permute-start.5 = (bf16[64,2048]{1,0:T(8,128)(2,1)}, bf16[64,2048]{1,0:T(8,128)(2,1)S(1)}, u32[]{:S(2)}, u32[]{:S(2)}) collective-permute-start(bf16[64,2048]{1,0:T(8,128)(2,1)} %shard_map.127), channel_id=1, source_target_pairs={{0,192},{64,0},{128,64},{192,128},{1,193},{65,1},{129,65},{193,129... | collective-permute-start | bytes 786440 | tf_op jit(solution)/shard_map/ppermute | solution.py:196
  24.0 9.5 %collective-permute-start.2 = (f32[64,512]{1,0:T(8,128)S(1)}, f32[64,512]{1,0:T(8,128)S(1)}, u32[]{:S(2)}, u32[]{:S(2)}) collective-permute-start(f32[64,512]{1,0:T(8,128)S(1)} %fusion.14), channel_id=1, source_target_pairs={{0,192},{64,0},{128,64},{192,128},{1,193},{65,1},{129,65},{193,129... | collective-permute-start | bytes 393224 | tf_op jit(solution)/shard_map/ppermute | solution.py:198
  30.6 2.4 %copy-start.4 = (bf16[64,2048]{1,0:T(8,128)(2,1)S(1)}, bf16[64,2048]{1,0:T(8,128)(2,1)}, u32[]{:S(2)}) copy-start(bf16[64,2048]{1,0:T(8,128)(2,1)} %shard_map.127) | copy-start | bytes 786436
  30.6 8.0 %collective-permute-start.4 = (f32[64,512]{1,0:T(8,128)S(1)}, f32[64,512]{1,0:T(8,128)S(1)}, u32[]{:S(2)}, u32[]{:S(2)}) collective-permute-start(f32[64,512]{1,0:T(8,128)S(1)} %fusion.15), channel_id=1, source_target_pairs={{0,128},{64,192},{128,0},{192,64},{1,129},{65,193},{129,1},{193,65... | collective-permute-start | bytes 393224 | tf_op jit(solution)/shard_map/ppermute | solution.py:198
  32.0 8.0 %collective-permute-start.6 = (f32[64,512]{1,0:T(8,128)S(1)}, f32[64,512]{1,0:T(8,128)S(1)}, u32[]{:S(2)}, u32[]{:S(2)}) collective-permute-start(f32[64,512]{1,0:T(8,128)S(1)} %fusion.16), channel_id=1, source_target_pairs={{0,64},{64,128},{128,192},{192,0},{1,65},{65,129},{129,193},{193,1... | collective-permute-start | bytes 393224 | tf_op jit(solution)/shard_map/ppermute | solution.py:198
  40.1 3.2 %copy-start.6 = (bf16[64,2048]{1,0:T(8,128)(2,1)S(1)}, bf16[64,2048]{1,0:T(8,128)(2,1)}, u32[]{:S(2)}) copy-start(bf16[64,2048]{1,0:T(8,128)(2,1)} %param.19) | copy-start | bytes 786436
  40.7 2.5 %copy-start.2 = (f32[4,8,8,512]{3,2,0,1:T(8,128)}, f32[4,8,8,512]{3,2,0,1:T(8,128)S(1)}, u32[]{:S(2)}) copy-start(f32[4,8,8,512]{3,2,0,1:T(8,128)S(1)} %copy.42) | copy-start | bytes 1572868
  40.7 2.5 %collective-permute-start.7 = (f32[64,2048]{1,0:T(8,128)S(1)}, f32[64,2048]{1,0:T(8,128)S(1)}, u32[]{:S(2)}, u32[]{:S(2)}) collective-permute-start(f32[64,2048]{1,0:T(8,128)S(1)} %bitcast.59), channel_id=1, source_target_pairs={{0,1},{1,0},{2,3},{3,2},{4,5},{5,4},{6,7},{7,6},{8,9},{9,8},{10,11... | collective-permute-start | bytes 1572872 | tf_op jit(solution)/shard_map/ppermute | solution.py:165
  42.7 1.8 %dynamic-slice-start = ((f32[2048]{0:T(1024)}, s32[]{:T(128)}), f32[1024]{0:T(1024)S(1)}, s32[]{:S(2)}) async-start(f32[2048]{0:T(1024)} %param.20, s32[]{:T(128)} %select_n.34), calls=%async_computation.2 | async-start | bytes 8704 | tf_op jit(solution)/shard_map/dynamic_slice | solution.py:207
  100.7 1.2 copy-start.1
  101.8 3.4 %collective-permute-start.8 = (bf16[6144,128]{1,0:T(8,128)(2,1)S(1)}, bf16[6144,128]{1,0:T(8,128)(2,1)S(1)}, u32[]{:S(2)}, u32[]{:S(2)}) collective-permute-start(bf16[6144,128]{1,0:T(8,128)(2,1)S(1)} %bitcast.54), channel_id=1, source_target_pairs={{0,1},{1,0},{2,3},{3,2},{4,5},{5,4},{6,7},{7,6},{8,9},{9,8},{10,11... | collective-permute-start | bytes 4718600 | tf_op jit(solution)/shard_map/ppermute | solution.py:165
  105.2 1.2 copy-start.3
  113.1 2.2 %collective-permute-start.9 = (bf16[768,384]{1,0:T(8,128)(2,1)}, bf16[768,384]{1,0:T(8,128)(2,1)S(1)}, u32[]{:S(2)}, u32[]{:S(2)}) collective-permute-start(bf16[768,384]{1,0:T(8,128)(2,1)} %shard_map.128.act_mine), channel_id=1, source_target_pairs={{0,1},{1,0},{2,3},{3,2},{4,5},{5,4},{6,7},{7,6},{8,9},{9,8},{10,11... | collective-permute-start | bytes 1769480 | tf_op jit(solution)/shard_map/ppermute | solution.py:165
  115.3 0.8 copy-start.5
  124.8 7.7 %copy-start.8 = (f32[64,8]{0,1:T(8,128)S(1)}, f32[64,8]{0,1:T(8,128)}, u32[]{:S(2)}) copy-start(f32[64,8]{0,1:T(8,128)} %param.22) | copy-start | bytes 6148
  124.8 49.0 %all-to-all-start.1 = ((bf16[128,48,128]{2,1,0:T(8,128)(2,1)}), bf16[128,48,128]{2,1,0:T(8,128)(2,1)}, u32[]{:S(2)}, u32[]{:S(2)}) async-start(bf16[128,48,128]{2,1,0:T(8,128)(2,1)} %reshape.100), calls=%async_computation.1 | async-start | bytes 3145728 | tf_op jit(solution)/shard_map/all_to_all | solution.py:231

commit v7 on v5

--- a/solution.py
+++ b/solution.py
@@ -45,28 +45,31 @@
     v_res = vr_ref[0]
     k_new = kn_ref[...]
     v_new = vn_ref[...]
-    rows = lax.broadcasted_iota(jnp.int32, (tokens, tokens), 0)
-    cols = lax.broadcasted_iota(jnp.int32, (tokens, tokens), 1)
+    q = jnp.concatenate(
+        [q_ref[:, g * HEAD_WIDTH:(g + 1) * HEAD_WIDTH] for g in range(group)], axis=0
+    )
+    rows = lax.broadcasted_iota(jnp.int32, (group * tokens, tokens), 0) % tokens
+    cols = lax.broadcasted_iota(jnp.int32, (group * tokens, tokens), 1)
     visible = cols <= rows
     scale = HEAD_WIDTH ** (-0.5)
     dims = (((1,), (1,)), ((), ()))
+    s_res = lax.dot_general(q, k_res, dims, preferred_element_type=jnp.float32) * scale
+    s_new = lax.dot_general(q, k_new, dims, preferred_element_type=jnp.float32) * scale
+    s_new = jnp.where(visible, s_new, jnp.float32(-1e30))
+    top = jnp.maximum(
+        jnp.max(s_res, axis=1, keepdims=True), jnp.max(s_new, axis=1, keepdims=True)
+    )
+    w_res = jnp.exp(s_res - top)
+    w_new = jnp.exp(s_new - top)
+    total = jnp.sum(w_res, axis=1, keepdims=True) + jnp.sum(w_new, axis=1, keepdims=True)
+    p_res = (w_res / total).astype(jnp.bfloat16)
+    p_new = (w_new / total).astype(jnp.bfloat16)
+    out = jnp.dot(p_res, v_res, preferred_element_type=jnp.float32) + jnp.dot(
+        p_new, v_new, preferred_element_type=jnp.float32
+    )
+    out = out.astype(o_ref.dtype)
     for g in range(group):
-        q = q_ref[:, g * HEAD_WIDTH:(g + 1) * HEAD_WIDTH]
-        s_res = lax.dot_general(q, k_res, dims, preferred_element_type=jnp.float32) * scale
-        s_new = lax.dot_general(q, k_new, dims, preferred_element_type=jnp.float32) * scale
-        s_new = jnp.where(visible, s_new, jnp.float32(-1e30))
-        top = jnp.maximum(
-            jnp.max(s_res, axis=1, keepdims=True), jnp.max(s_new, axis=1, keepdims=True)
-        )
-        w_res = jnp.exp(s_res - top)
-        w_new = jnp.exp(s_new - top)
-        total = jnp.sum(w_res, axis=1, keepdims=True) + jnp.sum(w_new, axis=1, keepdims=True)
-        p_res = (w_res / total).astype(jnp.bfloat16)
-        p_new = (w_new / total).astype(jnp.bfloat16)
-        out = jnp.dot(p_res, v_res, preferred_element_type=jnp.float32) + jnp.dot(
-            p_new, v_new, preferred_element_type=jnp.float32
-        )
-        o_ref[:, g * HEAD_WIDTH:(g + 1) * HEAD_WIDTH] = out.astype(o_ref.dtype)
+        o_ref[:, g * HEAD_WIDTH:(g + 1) * HEAD_WIDTH] = out[g * tokens:(g + 1) * tokens]
 
 
 def attend_kernel(queries, fresh_keys, fresh_values, resident_keys, resident_values, interpret=False):

time: 174 us -> 171 us (0.983)
  Pallas kernels: 24.2 us -> 20.6 us
    pallas_call x1, Pallas kernels: 12.1 us -> 8.49 us  [attend_kernel(): pl.pallas_call(attention_kernel, grid=(kv_here,), in_specs=[pl.BlockSpec(...]
where the time goes in v7:
time: 171 us; the launch traced here: 170 us
  waiting for transfers between devices  57.8 us (34%)
  blocking collectives  54.7 us (32%)
  Pallas kernels  20.6 us (12%)
  starting transfers between devices  18.6 us (11%)
  other arithmetic  8.13 us (5%)
  matrix products  6.26 us (4%)
  local copies, waits for them, and re-layouts  3.82 us (2%)
    all_to_all x1, blocking collectives, per_device(): lax.all_to_all(outgoing.reshape(owners, CAP * width, lanes), ('dp', 'expe...  54.7 us
    all_to_all x1, waiting for transfers between devices, per_device(): lax.all_to_all(expert_out.reshape(owners, CAP * width, lanes), ('dp', 'ex...  41.3 us
    pallas_call x1, Pallas kernels, attend_kernel(): pl.pallas_call(attention_kernel, grid=(kv_here,), in_specs=[pl.BlockSpec(...  8.49 us
    all_to_all x1, starting transfers between devices, per_device(): lax.all_to_all(expert_out.reshape(owners, CAP * width, lanes), ('dp', 'ex...  7.66 us
    pallas_call x1, Pallas kernels, gate_up(): pl.pallas_call(gate_up_kernel, grid_spec=pltpu.PrefetchScalarGridSpec(num...  6.68 us
    ppermute x3, waiting for transfers between devices, per_device(): blocks.append(lax.ppermute(product, 'dp', backward))  6.49 us
    ppermute x3, waiting for transfers between devices, per_device(): arrived = lax.ppermute(attended, 'dp', onward)  5.87 us
    ppermute x3, starting transfers between devices, per_device(): arrived = lax.ppermute(attended, 'dp', onward)  5.66 us
  transfers between devices with their start and end apart: 11, of which 8 were waited for; matrix products, arithmetic and copies ran while one was open for 4% of the time, Pallas kernels for 4%

profile of v7, /device:TPU:32, one launch (start us, length us, event | category | flops | bytes accessed | tf_op | source)
XLA Modules:
  0.0 170.2 jit_solution(11014760588266892442)
XLA Ops:
  0.0 0.0 copy-start
  0.0 8.5 %shard_map.127 = bf16[64,2048]{1,0:T(8,128)(2,1)} custom-call(bf16[64,2048]{1,0:T(8,128)(2,1)} %q_ref.1, bf16[64,256]{1,0:T(8,128)(2,1)} %kn_ref.1, bf16[64,256]{1,0:T(8,128)(2,1)} %vn_ref.1, bf16[1,2048,256]{2,1,0:T(8,128)(2,1)} %kr_ref.1, bf16[1,2048,256]{2,1,0:T(8,128)(2,1)} %vr_ref.1), custom_call_target="tpu_custom_call" | custom-call | tf_op jit(solution)/shard_map/pallas_call | solution.py:80
  8.5 1.5 collective-permute-start
  10.0 2.7 %collective-permute-start.2 = (bf16[64,2048]{1,0:T(8,128)(2,1)}, bf16[64,2048]{1,0:T(8,128)(2,1)S(1)}, u32[]{:S(2)}, u32[]{:S(2)}) collective-permute-start(bf16[64,2048]{1,0:T(8,128)(2,1)} %shard_map.127), channel_id=1, source_target_pairs={{0,128},{64,192},{128,0},{192,64},{1,129},{65,193},{129,1},{193,65... | collective-permute-start | bytes 786440 | tf_op jit(solution)/shard_map/ppermute | solution.py:198
  12.7 1.4 collective-permute-start.4
  14.1 0.0 copy-done
  14.2 1.4 convolution_bitcast_fusion
  15.6 2.5 %collective-permute-done = bf16[64,2048]{1,0:T(8,128)(2,1)S(1)} collective-permute-done((bf16[64,2048]{1,0:T(8,128)(2,1)}, bf16[64,2048]{1,0:T(8,128)(2,1)S(1)}, u32[]{:S(2)}, u32[]{:S(2)}) %collective-permute-start) | collective-permute-done | bytes 262176 | tf_op jit(solution)/shard_map/ppermute | solution.py:198
  18.1 0.5 fusion.14
  18.6 2.6 %collective-permute-start.1 = (f32[64,512]{1,0:T(8,128)S(1)}, f32[64,512]{1,0:T(8,128)S(1)}, u32[]{:S(2)}, u32[]{:S(2)}) collective-permute-start(f32[64,512]{1,0:T(8,128)S(1)} %fusion.14), channel_id=1, source_target_pairs={{0,192},{64,0},{128,64},{192,128},{1,193},{65,1},{129,65},{193,129... | collective-permute-start | bytes 393224 | tf_op jit(solution)/shard_map/ppermute | solution.py:200
  21.2 3.4 %collective-permute-done.2 = bf16[64,2048]{1,0:T(8,128)(2,1)S(1)} collective-permute-done((bf16[64,2048]{1,0:T(8,128)(2,1)}, bf16[64,2048]{1,0:T(8,128)(2,1)S(1)}, u32[]{:S(2)}, u32[]{:S(2)}) %collective-permute-start.2) | collective-permute-done | bytes 262176 | tf_op jit(solution)/shard_map/ppermute | solution.py:198
  24.6 0.5 fusion.15
  25.0 0.0 copy-start.4
  25.0 0.9 collective-permute-start.3
  26.0 0.0 collective-permute-done.4
  26.0 0.5 fusion.16
  26.4 0.8 collective-permute-start.5
  27.2 0.0 copy-done.4
  27.2 0.1 copy.34
  27.3 1.1 collective-permute-done.1
  28.4 4.0 %collective-permute-done.3 = f32[64,512]{1,0:T(8,128)S(1)} collective-permute-done((f32[64,512]{1,0:T(8,128)S(1)}, f32[64,512]{1,0:T(8,128)S(1)}, u32[]{:S(2)}, u32[]{:S(2)}) %collective-permute-start.3) | collective-permute-done | bytes 131104 | tf_op jit(solution)/shard_map/ppermute | solution.py:200
  32.4 1.4 collective-permute-done.5
  33.8 0.0 copy-start.3
  33.8 0.7 copy-done.3
  34.5 0.9 pad_maximum_fusion
  35.4 0.0 copy-start.2
  35.4 0.6 gather_fusion
  36.1 0.0 copy-start.1
  36.1 0.3 collective-permute-start.6
  36.4 0.1 convert_reduce_fusion
  36.5 0.1 reduce_window_sum.11
  36.6 1.2 select_reduce_fusion
  37.9 0.1 copy.35
  37.9 0.1 copy.36
  38.0 0.0 dynamic-slice-start
  38.0 0.5 fusion.5
  38.6 0.0 copy-done.1
  38.6 0.0 collective-permute-done.6
  38.6 0.0 copy-done.2
  38.6 1.2 multiply_reduce_fusion.1
  39.9 0.0 dynamic-slice-done
  39.9 0.6 convolution_convert_fusion
  40.5 1.0 copy.38
  41.5 54.7 %all_to_all.10 = bf16[128,48,128]{2,1,0:T(8,128)(2,1)} all-to-all(bf16[128,48,128]{2,1,0:T(8,128)(2,1)S(1)} %bitcast.55), channel_id=1, replica_groups=mesh['dp'=4,'expert'=32,'tensor'=2] {'dp','expert'}, dimensions={0} | all-to-all | bytes 3145728 | tf_op jit(solution)/shard_map/all_to_all | solution.py:225
  96.2 0.0 collective-permute-start.7
  96.2 1.2 dynamic-slice_bitcast_fusion
  97.4 0.6 collective-permute-start.9
  98.0 2.0 %collective-permute-done.7.other_ref = bf16[6144,128]{1,0:T(8,128)(2,1)} collective-permute-done((bf16[6144,128]{1,0:T(8,128)(2,1)}, bf16[6144,128]{1,0:T(8,128)(2,1)}, u32[]{:S(2)}, u32[]{:S(2)}) %collective-permute-start.7) | collective-permute-done | bytes 1572896 | tf_op jit(solution)/shard_map/ppermute | solution.py:169
  100.0 6.7 %shard_map.128.act_mine = bf16[768,384]{1,0:T(8,128)(2,1)} custom-call(s32[1]{0:T(128)} %bitcast.8.lane_ref, bf16[6144,128]{1,0:T(8,128)(2,1)} %bitcast.11.mine_ref, bf16[6144,128]{1,0:T(8,128)(2,1)} %collective-permute-done.7.other_ref, bf16[2048,384]{1,0:T(8,128)(2,1)} %bitcast.51, bf16[2048,384]{1,0:T(8,128)(2,1)} %bitcast.52, ...), custom_call_target="tpu_custom_call" | custom-call | tf_op jit(solution)/shard_map/pallas_call | solution.py:132
  106.7 0.1 collective-permute-start.8
  106.8 0.0 collective-permute-done.9.d_other
  106.8 2.2 %collective-permute-done.8.act_other = bf16[768,384]{1,0:T(8,128)(2,1)} collective-permute-done((bf16[768,384]{1,0:T(8,128)(2,1)}, bf16[768,384]{1,0:T(8,128)(2,1)}, u32[]{:S(2)}, u32[]{:S(2)}) %collective-permute-start.8) | collective-permute-done | bytes 589856 | tf_op jit(solution)/shard_map/ppermute | solution.py:169
  109.0 5.4 %shard_map.129 = f32[6144,128]{1,0:T(8,128)} custom-call(s32[1]{0:T(128)} %bitcast.8.lane_ref, bf16[768,384]{1,0:T(8,128)(2,1)} %shard_map.128.act_mine, bf16[768,384]{1,0:T(8,128)(2,1)} %collective-permute-done.8.act_other, bf16[384,2048]{1,0:T(8,128)(2,1)} %bitcast.57, bf16[384,1024]{1,0:T(8,128)(2,1)} %collective-permute-done.9.d_other), custom_call_target="tpu_custom_call" | custom-call | tf_op jit(solution)/shard_map/pallas_call | solution.py:150
  114.4 3.2 %convert_element_type.28 = bf16[6144,128]{1,0:T(8,128)(2,1)} convert(f32[6144,128]{1,0:T(8,128)} %shard_map.129) | non-fusion elementwise | flops 786432 | bytes 4718592 | tf_op jit(solution)/shard_map/convert_element_type | solution.py:232
  117.6 0.0 copy-start.5
  117.6 7.7 %all-to-all-start.1 = ((bf16[128,48,128]{2,1,0:T(8,128)(2,1)}), bf16[128,48,128]{2,1,0:T(8,128)(2,1)}, u32[]{:S(2)}, u32[]{:S(2)}) async-start(bf16[128,48,128]{2,1,0:T(8,128)(2,1)} %bitcast.56), calls=%async_computation.1 | async-start | bytes 3145728 | tf_op jit(solution)/shard_map/all_to_all | solution.py:234
  125.3 0.0 copy-done.5
  125.3 0.1 copy.33
  125.4 41.3 %all-to-all-done.1 = bf16[128,48,128]{2,1,0:T(8,128)(2,1)} async-done(((bf16[128,48,128]{2,1,0:T(8,128)(2,1)}), bf16[128,48,128]{2,1,0:T(8,128)(2,1)}, u32[]{:S(2)}, u32[]{:S(2)}) %all-to-all-start.1) | async-done | bytes 1572896 | tf_op jit(solution)/shard_map/all_to_all | solution.py:234
  166.7 2.8 %multiply_reduce_fusion = f32[64,8,128]{2,1,0:T(8,128)S(1)} fusion(bf16[768,8,128]{2,1,0:T(8,128)(2,1)} %bitcast.17, f32[64,8]{1,0:T(8,128)S(1)} %copy.33, s32[64,8]{1,0:T(8,128)S(1)} %copy.36), kind=kOutput, calls=%fused_computation.1 | convolution fusion | flops 806682624 | bytes 1839104 | tf_op jit(solution)/shard_map/tkr,rjl->tkjl/dot_general | solution.py:237
  169.4 0.7 fusion.7
  (6 shorter events, 0.1 us)
Async XLA Ops:
  0.0 14.1 %copy-start = (bf16[2048,512]{1,0:T(8,128)(2,1)S(1)}, bf16[2048,512]{1,0:T(8,128)(2,1)}, u32[]{:S(2)}) copy-start(bf16[2048,512]{1,0:T(8,128)(2,1)} %param.18) | copy-start | bytes 6291460
  8.5 9.6 %collective-permute-start = (bf16[64,2048]{1,0:T(8,128)(2,1)}, bf16[64,2048]{1,0:T(8,128)(2,1)S(1)}, u32[]{:S(2)}, u32[]{:S(2)}) collective-permute-start(bf16[64,2048]{1,0:T(8,128)(2,1)} %shard_map.127), channel_id=1, source_target_pairs={{0,64},{64,128},{128,192},{192,0},{1,65},{65,129},{129,193},{193,1... | collective-permute-start | bytes 786440 | tf_op jit(solution)/shard_map/ppermute | solution.py:198
  10.0 14.6 %collective-permute-start.2 = (bf16[64,2048]{1,0:T(8,128)(2,1)}, bf16[64,2048]{1,0:T(8,128)(2,1)S(1)}, u32[]{:S(2)}, u32[]{:S(2)}) collective-permute-start(bf16[64,2048]{1,0:T(8,128)(2,1)} %shard_map.127), channel_id=1, source_target_pairs={{0,128},{64,192},{128,0},{192,64},{1,129},{65,193},{129,1},{193,65... | collective-permute-start | bytes 786440 | tf_op jit(solution)/shard_map/ppermute | solution.py:198
  12.7 13.3 %collective-permute-start.4 = (bf16[64,2048]{1,0:T(8,128)(2,1)}, bf16[64,2048]{1,0:T(8,128)(2,1)S(1)}, u32[]{:S(2)}, u32[]{:S(2)}) collective-permute-start(bf16[64,2048]{1,0:T(8,128)(2,1)} %shard_map.127), channel_id=1, source_target_pairs={{0,192},{64,0},{128,64},{192,128},{1,193},{65,1},{129,65},{193,129... | collective-permute-start | bytes 786440 | tf_op jit(solution)/shard_map/ppermute | solution.py:198
  18.6 9.8 %collective-permute-start.1 = (f32[64,512]{1,0:T(8,128)S(1)}, f32[64,512]{1,0:T(8,128)S(1)}, u32[]{:S(2)}, u32[]{:S(2)}) collective-permute-start(f32[64,512]{1,0:T(8,128)S(1)} %fusion.14), channel_id=1, source_target_pairs={{0,192},{64,0},{128,64},{192,128},{1,193},{65,1},{129,65},{193,129... | collective-permute-start | bytes 393224 | tf_op jit(solution)/shard_map/ppermute | solution.py:200
  25.0 2.2 %copy-start.4 = (s32[64,8]{0,1:T(8,128)S(1)}, s32[64,8]{0,1:T(8,128)}, u32[]{:S(2)}) copy-start(s32[64,8]{0,1:T(8,128)} %param.21) | copy-start | bytes 6148
  25.0 7.4 %collective-permute-start.3 = (f32[64,512]{1,0:T(8,128)S(1)}, f32[64,512]{1,0:T(8,128)S(1)}, u32[]{:S(2)}, u32[]{:S(2)}) collective-permute-start(f32[64,512]{1,0:T(8,128)S(1)} %fusion.15), channel_id=1, source_target_pairs={{0,128},{64,192},{128,0},{192,64},{1,129},{65,193},{129,1},{193,65... | collective-permute-start | bytes 393224 | tf_op jit(solution)/shard_map/ppermute | solution.py:200
  26.4 7.4 %collective-permute-start.5 = (f32[64,512]{1,0:T(8,128)S(1)}, f32[64,512]{1,0:T(8,128)S(1)}, u32[]{:S(2)}, u32[]{:S(2)}) collective-permute-start(f32[64,512]{1,0:T(8,128)S(1)} %fusion.16), channel_id=1, source_target_pairs={{0,64},{64,128},{128,192},{192,0},{1,65},{65,129},{129,193},{193,1... | collective-permute-start | bytes 393224 | tf_op jit(solution)/shard_map/ppermute | solution.py:200
  33.8 0.7 copy-start.3
  35.4 3.2 %copy-start.2 = (bf16[64,2048]{1,0:T(8,128)(2,1)S(1)}, bf16[64,2048]{1,0:T(8,128)(2,1)}, u32[]{:S(2)}) copy-start(bf16[64,2048]{1,0:T(8,128)(2,1)} %param.19) | copy-start | bytes 786436
  36.1 2.5 %copy-start.1 = (f32[4,8,8,512]{3,2,0,1:T(8,128)}, f32[4,8,8,512]{3,2,0,1:T(8,128)S(1)}, u32[]{:S(2)}) copy-start(f32[4,8,8,512]{3,2,0,1:T(8,128)S(1)} %copy.42) | copy-start | bytes 1572868
  36.1 2.5 %collective-permute-start.6 = (f32[64,2048]{1,0:T(8,128)S(1)}, f32[64,2048]{1,0:T(8,128)S(1)}, u32[]{:S(2)}, u32[]{:S(2)}) collective-permute-start(f32[64,2048]{1,0:T(8,128)S(1)} %bitcast.59), channel_id=1, source_target_pairs={{0,1},{1,0},{2,3},{3,2},{4,5},{5,4},{6,7},{7,6},{8,9},{9,8},{10,11... | collective-permute-start | bytes 1572872 | tf_op jit(solution)/shard_map/ppermute | solution.py:169
  38.0 1.8 %dynamic-slice-start = ((f32[2048]{0:T(1024)}, s32[]{:T(128)}), f32[1024]{0:T(1024)S(1)}, s32[]{:S(2)}) async-start(f32[2048]{0:T(1024)} %param.20, s32[]{:T(128)} %select_n.33), calls=%async_computation.2 | async-start | bytes 8704 | tf_op jit(solution)/shard_map/dynamic_slice | solution.py:209
  96.2 3.8 %collective-permute-start.7 = (bf16[6144,128]{1,0:T(8,128)(2,1)}, bf16[6144,128]{1,0:T(8,128)(2,1)}, u32[]{:S(2)}, u32[]{:S(2)}) collective-permute-start(bf16[6144,128]{1,0:T(8,128)(2,1)} %bitcast.11.mine_ref), channel_id=1, source_target_pairs={{0,1},{1,0},{2,3},{3,2},{4,5},{5,4},{6,7},{7,6},{8,9},{9,8},{10,11... | collective-permute-start | bytes 4718600 | tf_op jit(solution)/shard_map/ppermute | solution.py:169
  97.4 9.4 %collective-permute-start.9 = (bf16[384,1024]{1,0:T(8,128)(2,1)S(1)}, bf16[384,1024]{1,0:T(8,128)(2,1)}, u32[]{:S(2)}, u32[]{:S(2)}) collective-permute-start(bf16[384,1024]{1,0:T(8,128)(2,1)S(1)} %dynamic-slice_bitcast_fusion), channel_id=1, source_target_pairs={{0,1},{1,0},{2,3},{3,2},{4,5},{5,4},{6,7},{7,6},{8,9},{9,8},{10,11... | collective-permute-start | bytes 2359304 | tf_op jit(solution)/shard_map/ppermute | solution.py:169
  106.7 2.3 %collective-permute-start.8 = (bf16[768,384]{1,0:T(8,128)(2,1)}, bf16[768,384]{1,0:T(8,128)(2,1)}, u32[]{:S(2)}, u32[]{:S(2)}) collective-permute-start(bf16[768,384]{1,0:T(8,128)(2,1)} %shard_map.128.act_mine), channel_id=1, source_target_pairs={{0,1},{1,0},{2,3},{3,2},{4,5},{5,4},{6,7},{7,6},{8,9},{9,8},{10,11... | collective-permute-start | bytes 1769480 | tf_op jit(solution)/shard_map/ppermute | solution.py:169
  117.6 7.7 %copy-start.5 = (f32[64,8]{0,1:T(8,128)S(1)}, f32[64,8]{0,1:T(8,128)}, u32[]{:S(2)}) copy-start(f32[64,8]{0,1:T(8,128)} %param.22) | copy-start | bytes 6148
  117.6 49.0 %all-to-all-start.1 = ((bf16[128,48,128]{2,1,0:T(8,128)(2,1)}), bf16[128,48,128]{2,1,0:T(8,128)(2,1)}, u32[]{:S(2)}, u32[]{:S(2)}) async-start(bf16[128,48,128]{2,1,0:T(8,128)(2,1)} %bitcast.56), calls=%async_computation.1 | async-start | bytes 3145728 | tf_op jit(solution)/shard_map/all_to_all | solution.py:234

commit v8 on v7

--- a/solution.py
+++ b/solution.py
@@ -111,14 +111,15 @@
     act_ref[...] = (gate / (1.0 + jnp.exp(-gate)) * up).astype(act_ref.dtype)
 
 
-def down_kernel(lane_ref, act_mine, act_other, d_own, d_other, out_ref):
+def down_kernel(lane_ref, act_mine, act_other, d_own, d_other, out_ref, fold_ref):
     fold = d_own.shape[1] // HEAD_WIDTH
     rows = act_mine.shape[0]
     out = jnp.dot(act_mine[...], d_own[...], preferred_element_type=jnp.float32) + jnp.dot(
         act_other[...], d_other[...], preferred_element_type=jnp.float32
     )
     for j in range(fold):
-        out_ref[pl.ds(j, rows, stride=fold), :] = out[:, j * HEAD_WIDTH:(j + 1) * HEAD_WIDTH]
+        fold_ref[pl.ds(j, rows, stride=fold), :] = out[:, j * HEAD_WIDTH:(j + 1) * HEAD_WIDTH]
+    out_ref[...] = fold_ref[...].astype(out_ref.dtype)
 
 
 def gate_up(lane, mine, other, gate_mat, up_mat, block_rows=256, interpret=False):
@@ -159,8 +160,9 @@
                 pl.BlockSpec((hidden, half), lambda i, lane_ref: (0, 0)),
             ],
             out_specs=pl.BlockSpec((block_rows * fold, HEAD_WIDTH), lambda i, lane_ref: (i, 0)),
+            scratch_shapes=[pltpu.VMEM((block_rows * fold, HEAD_WIDTH), jnp.float32)],
         ),
-        out_shape=jax.ShapeDtypeStruct((rows * fold, HEAD_WIDTH), jnp.float32),
+        out_shape=jax.ShapeDtypeStruct((rows * fold, HEAD_WIDTH), jnp.bfloat16),
         interpret=interpret,
     )(lane, act_mine, act_other, down_mat, down_other)
 
@@ -229,7 +231,7 @@
     lane_id = lane.astype(jnp.int32).reshape(1)
     down_other = swap_pair(lax.dynamic_slice_in_dim(w_down[0], (1 - lane) * half, half, 1))
     act = gate_up(lane_id, received, other, w_gate[0], w_up[0])
-    expert_out = down(lane_id, act, swap_pair(act), w_down[0], down_other).astype(jnp.bfloat16)
+    expert_out = down(lane_id, act, swap_pair(act), w_down[0], down_other)
 
     returned = lax.all_to_all(
         expert_out.reshape(owners, CAP * width, lanes), ("dp", "expert"), split_axis=0, concat_axis=0, tiled=True

time: 171 us -> 166 us (0.971)
  other arithmetic: 8.13 us -> 4.04 us
    convert_element_type x1 -> x0, other arithmetic: 3.19 us -> none  [per_device(): down(lane_id, act, swap_pair(act), w_down[0], down_other)]
where the time goes in v8:
time: 166 us; the launch traced here: 165 us
  waiting for transfers between devices  57.8 us (35%)
  blocking collectives  54.7 us (33%)
  Pallas kernels  20.3 us (12%)
  starting transfers between devices  18.6 us (11%)
  matrix products  6.26 us (4%)
  other arithmetic  4.04 us (2%)
  local copies, waits for them, and re-layouts  3.16 us (2%)
    all_to_all x1, blocking collectives, per_device(): lax.all_to_all(outgoing.reshape(owners, CAP * width, lanes), ('dp', 'expe...  54.7 us
    all_to_all x1, waiting for transfers between devices, per_device(): lax.all_to_all(expert_out.reshape(owners, CAP * width, lanes), ('dp', 'ex...  41.3 us
    pallas_call x1, Pallas kernels, attend_kernel(): pl.pallas_call(attention_kernel, grid=(kv_here,), in_specs=[pl.BlockSpec(...  8.47 us
    all_to_all x1, starting transfers between devices, per_device(): lax.all_to_all(expert_out.reshape(owners, CAP * width, lanes), ('dp', 'ex...  7.66 us
    pallas_call x1, Pallas kernels, gate_up(): pl.pallas_call(gate_up_kernel, grid_spec=pltpu.PrefetchScalarGridSpec(num...  6.68 us
    ppermute x3, waiting for transfers between devices, per_device(): blocks.append(lax.ppermute(product, 'dp', backward))  6.49 us
    ppermute x3, waiting for transfers between devices, per_device(): arrived = lax.ppermute(attended, 'dp', onward)  5.87 us
    ppermute x3, starting transfers between devices, per_device(): arrived = lax.ppermute(attended, 'dp', onward)  5.66 us
  transfers between devices with their start and end apart: 11, of which 8 were waited for; matrix products, arithmetic and copies ran while one was open for 4% of the time, Pallas kernels for 4%

profile of v8, /device:TPU:32, one launch (start us, length us, event | category | flops | bytes accessed | tf_op | source)
XLA Modules:
  0.0 165.1 jit_solution(2392637434476256801)
XLA Ops:
  0.0 0.0 copy-start
  0.0 8.5 %shard_map.127 = bf16[64,2048]{1,0:T(8,128)(2,1)} custom-call(bf16[64,2048]{1,0:T(8,128)(2,1)} %q_ref.1, bf16[64,256]{1,0:T(8,128)(2,1)} %kn_ref.1, bf16[64,256]{1,0:T(8,128)(2,1)} %vn_ref.1, bf16[1,2048,256]{2,1,0:T(8,128)(2,1)} %kr_ref.1, bf16[1,2048,256]{2,1,0:T(8,128)(2,1)} %vr_ref.1), custom_call_target="tpu_custom_call" | custom-call | tf_op jit(solution)/shard_map/pallas_call | solution.py:80
  8.5 1.5 collective-permute-start
  10.0 2.7 %collective-permute-start.2 = (bf16[64,2048]{1,0:T(8,128)(2,1)}, bf16[64,2048]{1,0:T(8,128)(2,1)S(1)}, u32[]{:S(2)}, u32[]{:S(2)}) collective-permute-start(bf16[64,2048]{1,0:T(8,128)(2,1)} %shard_map.127), channel_id=1, source_target_pairs={{0,128},{64,192},{128,0},{192,64},{1,129},{65,193},{129,1},{193,65... | collective-permute-start | bytes 786440 | tf_op jit(solution)/shard_map/ppermute | solution.py:200
  12.7 1.4 collective-permute-start.4
  14.1 0.0 copy-done
  14.1 1.4 convolution_bitcast_fusion
  15.6 2.5 %collective-permute-done = bf16[64,2048]{1,0:T(8,128)(2,1)S(1)} collective-permute-done((bf16[64,2048]{1,0:T(8,128)(2,1)}, bf16[64,2048]{1,0:T(8,128)(2,1)S(1)}, u32[]{:S(2)}, u32[]{:S(2)}) %collective-permute-start) | collective-permute-done | bytes 262176 | tf_op jit(solution)/shard_map/ppermute | solution.py:200
  18.1 0.5 fusion.14
  18.6 2.6 %collective-permute-start.1 = (f32[64,512]{1,0:T(8,128)S(1)}, f32[64,512]{1,0:T(8,128)S(1)}, u32[]{:S(2)}, u32[]{:S(2)}) collective-permute-start(f32[64,512]{1,0:T(8,128)S(1)} %fusion.14), channel_id=1, source_target_pairs={{0,192},{64,0},{128,64},{192,128},{1,193},{65,1},{129,65},{193,129... | collective-permute-start | bytes 393224 | tf_op jit(solution)/shard_map/ppermute | solution.py:202
  21.2 3.4 %collective-permute-done.2 = bf16[64,2048]{1,0:T(8,128)(2,1)S(1)} collective-permute-done((bf16[64,2048]{1,0:T(8,128)(2,1)}, bf16[64,2048]{1,0:T(8,128)(2,1)S(1)}, u32[]{:S(2)}, u32[]{:S(2)}) %collective-permute-start.2) | collective-permute-done | bytes 262176 | tf_op jit(solution)/shard_map/ppermute | solution.py:200
  24.5 0.5 fusion.15
  25.0 0.0 copy-start.2
  25.0 0.9 collective-permute-start.3
  25.9 0.0 collective-permute-done.4
  25.9 0.5 fusion.16
  26.4 0.8 collective-permute-start.5
  27.2 0.0 copy-done.2
  27.2 0.1 copy.34
  27.3 1.1 collective-permute-done.1
  28.4 4.0 %collective-permute-done.3 = f32[64,512]{1,0:T(8,128)S(1)} collective-permute-done((f32[64,512]{1,0:T(8,128)S(1)}, f32[64,512]{1,0:T(8,128)S(1)}, u32[]{:S(2)}, u32[]{:S(2)}) %collective-permute-start.3) | collective-permute-done | bytes 131104 | tf_op jit(solution)/shard_map/ppermute | solution.py:202
  32.4 1.4 collective-permute-done.5
  33.9 0.0 copy-start.1
  33.9 0.6 gather_fusion
  34.5 0.3 collective-permute-start.6
  34.8 0.1 convert_reduce_fusion
  34.9 0.1 reduce_window_sum.11
  35.0 1.2 select_reduce_fusion
  36.3 0.1 copy.35
  36.4 0.1 copy.36
  36.4 0.0 dynamic-slice-start
  36.5 0.5 fusion.5
  37.0 0.0 collective-permute-done.6
  37.0 0.0 copy-done.1
  37.0 1.2 multiply_reduce_fusion.1
  38.3 0.0 dynamic-slice-done
  38.3 0.6 convolution_convert_fusion
  38.9 1.0 copy.38
  39.9 54.7 %all_to_all.10 = bf16[128,48,128]{2,1,0:T(8,128)(2,1)} all-to-all(bf16[128,48,128]{2,1,0:T(8,128)(2,1)S(1)} %bitcast.55), channel_id=1, replica_groups=mesh['dp'=4,'expert'=32,'tensor'=2] {'dp','expert'}, dimensions={0} | all-to-all | bytes 3145728 | tf_op jit(solution)/shard_map/all_to_all | solution.py:227
  94.6 0.0 collective-permute-start.7
  94.6 1.2 dynamic-slice_bitcast_fusion
  95.8 0.6 collective-permute-start.9
  96.4 2.0 %collective-permute-done.7.other_ref = bf16[6144,128]{1,0:T(8,128)(2,1)} collective-permute-done((bf16[6144,128]{1,0:T(8,128)(2,1)}, bf16[6144,128]{1,0:T(8,128)(2,1)}, u32[]{:S(2)}, u32[]{:S(2)}) %collective-permute-start.7) | collective-permute-done | bytes 1572896 | tf_op jit(solution)/shard_map/ppermute | solution.py:171
  98.4 6.7 %shard_map.128.act_mine = bf16[768,384]{1,0:T(8,128)(2,1)} custom-call(s32[1]{0:T(128)} %bitcast.8.lane_ref, bf16[6144,128]{1,0:T(8,128)(2,1)} %bitcast.11.mine_ref, bf16[6144,128]{1,0:T(8,128)(2,1)} %collective-permute-done.7.other_ref, bf16[2048,384]{1,0:T(8,128)(2,1)} %bitcast.51, bf16[2048,384]{1,0:T(8,128)(2,1)} %bitcast.52, ...), custom_call_target="tpu_custom_call" | custom-call | tf_op jit(solution)/shard_map/pallas_call | solution.py:133
  105.1 0.1 collective-permute-start.8
  105.2 0.0 collective-permute-done.9.d_other
  105.2 2.2 %collective-permute-done.8.act_other = bf16[768,384]{1,0:T(8,128)(2,1)} collective-permute-done((bf16[768,384]{1,0:T(8,128)(2,1)}, bf16[768,384]{1,0:T(8,128)(2,1)}, u32[]{:S(2)}, u32[]{:S(2)}) %collective-permute-start.8) | collective-permute-done | bytes 589856 | tf_op jit(solution)/shard_map/ppermute | solution.py:171
  107.4 5.1 %shard_map.129 = bf16[6144,128]{1,0:T(8,128)(2,1)} custom-call(s32[1]{0:T(128)} %bitcast.8.lane_ref, bf16[768,384]{1,0:T(8,128)(2,1)} %shard_map.128.act_mine, bf16[768,384]{1,0:T(8,128)(2,1)} %collective-permute-done.8.act_other, bf16[384,2048]{1,0:T(8,128)(2,1)} %bitcast.57, bf16[384,1024]{1,0:T(8,128)(2,1)} %collective-permute-done.9.d_other), custom_call_target="tpu_custom_call" | custom-call | tf_op jit(solution)/shard_map/pallas_call | solution.py:151
  112.6 0.0 copy-start.3
  112.6 7.7 %all-to-all-start.1 = ((bf16[128,48,128]{2,1,0:T(8,128)(2,1)}), bf16[128,48,128]{2,1,0:T(8,128)(2,1)}, u32[]{:S(2)}, u32[]{:S(2)}) async-start(bf16[128,48,128]{2,1,0:T(8,128)(2,1)} %bitcast.56), calls=%async_computation.1 | async-start | bytes 3145728 | tf_op jit(solution)/shard_map/all_to_all | solution.py:236
  120.2 0.0 copy-done.3
  120.2 0.1 copy.33
  120.3 41.3 %all-to-all-done.1 = bf16[128,48,128]{2,1,0:T(8,128)(2,1)} async-done(((bf16[128,48,128]{2,1,0:T(8,128)(2,1)}), bf16[128,48,128]{2,1,0:T(8,128)(2,1)}, u32[]{:S(2)}, u32[]{:S(2)}) %all-to-all-start.1) | async-done | bytes 1572896 | tf_op jit(solution)/shard_map/all_to_all | solution.py:236
  161.6 2.8 %multiply_reduce_fusion = f32[64,8,128]{2,1,0:T(8,128)S(1)} fusion(bf16[768,8,128]{2,1,0:T(8,128)(2,1)} %bitcast.17, f32[64,8]{1,0:T(8,128)S(1)} %copy.33, s32[64,8]{1,0:T(8,128)S(1)} %copy.36), kind=kOutput, calls=%fused_computation.1 | convolution fusion | flops 806682624 | bytes 1839104 | tf_op jit(solution)/shard_map/tkr,rjl->tkjl/dot_general | solution.py:239
  164.4 0.7 fusion.7
  (7 shorter events, 0.1 us)
Async XLA Ops:
  0.0 14.1 %copy-start = (bf16[2048,512]{1,0:T(8,128)(2,1)S(1)}, bf16[2048,512]{1,0:T(8,128)(2,1)}, u32[]{:S(2)}) copy-start(bf16[2048,512]{1,0:T(8,128)(2,1)} %param.18) | copy-start | bytes 6291460
  8.5 9.6 %collective-permute-start = (bf16[64,2048]{1,0:T(8,128)(2,1)}, bf16[64,2048]{1,0:T(8,128)(2,1)S(1)}, u32[]{:S(2)}, u32[]{:S(2)}) collective-permute-start(bf16[64,2048]{1,0:T(8,128)(2,1)} %shard_map.127), channel_id=1, source_target_pairs={{0,64},{64,128},{128,192},{192,0},{1,65},{65,129},{129,193},{193,1... | collective-permute-start | bytes 786440 | tf_op jit(solution)/shard_map/ppermute | solution.py:200
  10.0 14.6 %collective-permute-start.2 = (bf16[64,2048]{1,0:T(8,128)(2,1)}, bf16[64,2048]{1,0:T(8,128)(2,1)S(1)}, u32[]{:S(2)}, u32[]{:S(2)}) collective-permute-start(bf16[64,2048]{1,0:T(8,128)(2,1)} %shard_map.127), channel_id=1, source_target_pairs={{0,128},{64,192},{128,0},{192,64},{1,129},{65,193},{129,1},{193,65... | collective-permute-start | bytes 786440 | tf_op jit(solution)/shard_map/ppermute | solution.py:200
  12.7 13.3 %collective-permute-start.4 = (bf16[64,2048]{1,0:T(8,128)(2,1)}, bf16[64,2048]{1,0:T(8,128)(2,1)S(1)}, u32[]{:S(2)}, u32[]{:S(2)}) collective-permute-start(bf16[64,2048]{1,0:T(8,128)(2,1)} %shard_map.127), channel_id=1, source_target_pairs={{0,192},{64,0},{128,64},{192,128},{1,193},{65,1},{129,65},{193,129... | collective-permute-start | bytes 786440 | tf_op jit(solution)/shard_map/ppermute | solution.py:200
  18.6 9.8 %collective-permute-start.1 = (f32[64,512]{1,0:T(8,128)S(1)}, f32[64,512]{1,0:T(8,128)S(1)}, u32[]{:S(2)}, u32[]{:S(2)}) collective-permute-start(f32[64,512]{1,0:T(8,128)S(1)} %fusion.14), channel_id=1, source_target_pairs={{0,192},{64,0},{128,64},{192,128},{1,193},{65,1},{129,65},{193,129... | collective-permute-start | bytes 393224 | tf_op jit(solution)/shard_map/ppermute | solution.py:202
  25.0 2.2 %copy-start.2 = (s32[64,8]{0,1:T(8,128)S(1)}, s32[64,8]{0,1:T(8,128)}, u32[]{:S(2)}) copy-start(s32[64,8]{0,1:T(8,128)} %param.21) | copy-start | bytes 6148
  25.0 7.4 %collective-permute-start.3 = (f32[64,512]{1,0:T(8,128)S(1)}, f32[64,512]{1,0:T(8,128)S(1)}, u32[]{:S(2)}, u32[]{:S(2)}) collective-permute-start(f32[64,512]{1,0:T(8,128)S(1)} %fusion.15), channel_id=1, source_target_pairs={{0,128},{64,192},{128,0},{192,64},{1,129},{65,193},{129,1},{193,65... | collective-permute-start | bytes 393224 | tf_op jit(solution)/shard_map/ppermute | solution.py:202
  26.4 7.4 %collective-permute-start.5 = (f32[64,512]{1,0:T(8,128)S(1)}, f32[64,512]{1,0:T(8,128)S(1)}, u32[]{:S(2)}, u32[]{:S(2)}) collective-permute-start(f32[64,512]{1,0:T(8,128)S(1)} %fusion.16), channel_id=1, source_target_pairs={{0,64},{64,128},{128,192},{192,0},{1,65},{65,129},{129,193},{193,1... | collective-permute-start | bytes 393224 | tf_op jit(solution)/shard_map/ppermute | solution.py:202
  33.9 3.2 %copy-start.1 = (bf16[64,2048]{1,0:T(8,128)(2,1)S(1)}, bf16[64,2048]{1,0:T(8,128)(2,1)}, u32[]{:S(2)}) copy-start(bf16[64,2048]{1,0:T(8,128)(2,1)} %param.19) | copy-start | bytes 786436
  34.5 2.5 %collective-permute-start.6 = (f32[64,2048]{1,0:T(8,128)S(1)}, f32[64,2048]{1,0:T(8,128)}, u32[]{:S(2)}, u32[]{:S(2)}) collective-permute-start(f32[64,2048]{1,0:T(8,128)S(1)} %bitcast.59), channel_id=1, source_target_pairs={{0,1},{1,0},{2,3},{3,2},{4,5},{5,4},{6,7},{7,6},{8,9},{9,8},{10,11... | collective-permute-start | bytes 1572872 | tf_op jit(solution)/shard_map/ppermute | solution.py:171
  36.4 1.8 %dynamic-slice-start = ((f32[2048]{0:T(1024)}, s32[]{:T(128)}), f32[1024]{0:T(1024)S(1)}, s32[]{:S(2)}) async-start(f32[2048]{0:T(1024)} %param.20, s32[]{:T(128)} %select_n.33), calls=%async_computation.2 | async-start | bytes 8704 | tf_op jit(solution)/shard_map/dynamic_slice | solution.py:211
  94.6 3.8 %collective-permute-start.7 = (bf16[6144,128]{1,0:T(8,128)(2,1)}, bf16[6144,128]{1,0:T(8,128)(2,1)}, u32[]{:S(2)}, u32[]{:S(2)}) collective-permute-start(bf16[6144,128]{1,0:T(8,128)(2,1)} %bitcast.11.mine_ref), channel_id=1, source_target_pairs={{0,1},{1,0},{2,3},{3,2},{4,5},{5,4},{6,7},{7,6},{8,9},{9,8},{10,11... | collective-permute-start | bytes 4718600 | tf_op jit(solution)/shard_map/ppermute | solution.py:171
  95.8 9.4 %collective-permute-start.9 = (bf16[384,1024]{1,0:T(8,128)(2,1)S(1)}, bf16[384,1024]{1,0:T(8,128)(2,1)}, u32[]{:S(2)}, u32[]{:S(2)}) collective-permute-start(bf16[384,1024]{1,0:T(8,128)(2,1)S(1)} %dynamic-slice_bitcast_fusion), channel_id=1, source_target_pairs={{0,1},{1,0},{2,3},{3,2},{4,5},{5,4},{6,7},{7,6},{8,9},{9,8},{10,11... | collective-permute-start | bytes 2359304 | tf_op jit(solution)/shard_map/ppermute | solution.py:171
  105.1 2.3 %collective-permute-start.8 = (bf16[768,384]{1,0:T(8,128)(2,1)}, bf16[768,384]{1,0:T(8,128)(2,1)}, u32[]{:S(2)}, u32[]{:S(2)}) collective-permute-start(bf16[768,384]{1,0:T(8,128)(2,1)} %shard_map.128.act_mine), channel_id=1, source_target_pairs={{0,1},{1,0},{2,3},{3,2},{4,5},{5,4},{6,7},{7,6},{8,9},{9,8},{10,11... | collective-permute-start | bytes 1769480 | tf_op jit(solution)/shard_map/ppermute | solution.py:171
  112.6 7.7 %copy-start.3 = (f32[64,8]{0,1:T(8,128)S(1)}, f32[64,8]{0,1:T(8,128)}, u32[]{:S(2)}) copy-start(f32[64,8]{0,1:T(8,128)} %param.22) | copy-start | bytes 6148
  112.6 49.0 %all-to-all-start.1 = ((bf16[128,48,128]{2,1,0:T(8,128)(2,1)}), bf16[128,48,128]{2,1,0:T(8,128)(2,1)}, u32[]{:S(2)}, u32[]{:S(2)}) async-start(bf16[128,48,128]{2,1,0:T(8,128)(2,1)} %bitcast.56), calls=%async_computation.1 | async-start | bytes 3145728 | tf_op jit(solution)/shard_map/all_to_all | solution.py:236

commit v9 on v8

--- a/solution.py
+++ b/solution.py
@@ -145,7 +145,7 @@
 
 def down(lane, act_mine, act_other, down_mat, down_other, block_rows=256, interpret=False):
     rows, hidden = act_mine.shape
-    half = down_other.shape[1]
+    half = down_other.shape[1] // 2
     fold = half // HEAD_WIDTH
     act_spec = pl.BlockSpec((block_rows, hidden), lambda i, lane_ref: (i, 0))
     return pl.pallas_call(
@@ -157,7 +157,7 @@
                 act_spec,
                 act_spec,
                 pl.BlockSpec((hidden, half), lambda i, lane_ref: (0, lane_ref[0])),
-                pl.BlockSpec((hidden, half), lambda i, lane_ref: (0, 0)),
+                pl.BlockSpec((hidden, half), lambda i, lane_ref: (0, lane_ref[0])),
             ],
             out_specs=pl.BlockSpec((block_rows * fold, HEAD_WIDTH), lambda i, lane_ref: (i, 0)),
             scratch_shapes=[pltpu.VMEM((block_rows * fold, HEAD_WIDTH), jnp.float32)],
@@ -229,15 +229,21 @@
     ).reshape(owners * CAP * width, lanes)
     other = swap_pair(received)
     lane_id = lane.astype(jnp.int32).reshape(1)
-    down_other = swap_pair(lax.dynamic_slice_in_dim(w_down[0], (1 - lane) * half, half, 1))
+    down_other = swap_pair(w_down[0])
     act = gate_up(lane_id, received, other, w_gate[0], w_up[0])
     expert_out = down(lane_id, act, swap_pair(act), w_down[0], down_other)
 
     returned = lax.all_to_all(
         expert_out.reshape(owners, CAP * width, lanes), ("dp", "expert"), split_axis=0, concat_axis=0, tiled=True
     ).reshape(owners * CAP, width, lanes)
-    picked = jnp.einsum("tkr,rjl->tkjl", pick, returned, preferred_element_type=jnp.float32)
-    moe = jnp.sum(gates[:, :, None, None] * picked, axis=1).reshape(tokens_here, half)
+    spread_gates = jnp.sum(gates[:, :, None] * pick.astype(jnp.float32), axis=1)
+    first_part = spread_gates.astype(jnp.bfloat16)
+    rest = spread_gates - first_part.astype(jnp.float32)
+    second_part = rest.astype(jnp.bfloat16)
+    third_part = (rest - second_part.astype(jnp.float32)).astype(jnp.bfloat16)
+    parts = jnp.concatenate([first_part, second_part, third_part], axis=0)
+    combined = jnp.einsum("sr,rjl->sjl", parts, returned, preferred_element_type=jnp.float32)
+    moe = jnp.sum(combined.reshape(3, tokens_here, width, lanes), axis=0).reshape(tokens_here, half)
     return (hidden_half + moe).astype(jnp.bfloat16)
 
 

time: 166 us -> 167 us (level)
  local copies, waits for them, and re-layouts: 3.16 us -> 5.1 us
    unnamed x10 -> x16, local copies, waits for them, and re-layouts: 0.19 us -> 3.31 us
where the time goes in v9:
time: 167 us
  waiting for transfers between devices  57.9 us (35%)
  blocking collectives  54.6 us (33%)
  Pallas kernels  20.3 us (12%)
  starting transfers between devices  18.5 us (11%)
  matrix products  5.39 us (3%)
  local copies, waits for them, and re-layouts  5.1 us (3%)
  other arithmetic  4.66 us (3%)
    all_to_all x1, blocking collectives, per_device(): lax.all_to_all(outgoing.reshape(owners, CAP * width, lanes), ('dp', 'expe...  54.6 us
    all_to_all x1, waiting for transfers between devices, per_device(): lax.all_to_all(expert_out.reshape(owners, CAP * width, lanes), ('dp', 'ex...  40.6 us
    pallas_call x1, Pallas kernels, attend_kernel(): pl.pallas_call(attention_kernel, grid=(kv_here,), in_specs=[pl.BlockSpec(...  8.48 us
    all_to_all x1, starting transfers between devices, per_device(): lax.all_to_all(expert_out.reshape(owners, CAP * width, lanes), ('dp', 'ex...  7.65 us
    pallas_call x1, Pallas kernels, gate_up(): pl.pallas_call(gate_up_kernel, grid_spec=pltpu.PrefetchScalarGridSpec(num...  6.69 us
    ppermute x3, waiting for transfers between devices, per_device(): blocks.append(lax.ppermute(product, 'dp', backward))  6.49 us
    ppermute x3, waiting for transfers between devices, per_device(): arrived = lax.ppermute(attended, 'dp', onward)  5.87 us
    ppermute x3, starting transfers between devices, per_device(): arrived = lax.ppermute(attended, 'dp', onward)  5.66 us
  transfers between devices with their start and end apart: 11, of which 8 were waited for; matrix products, arithmetic and copies ran while one was open for 4% of the time, Pallas kernels for 4%

profile of v9, /device:TPU:32, one launch (start us, length us, event | category | flops | bytes accessed | tf_op | source)
XLA Modules:
  0.0 166.8 jit_solution(826627065887117323)
XLA Ops:
  0.0 0.0 copy-start
  0.0 8.5 %shard_map.127 = bf16[64,2048]{1,0:T(8,128)(2,1)} custom-call(bf16[64,2048]{1,0:T(8,128)(2,1)} %q_ref.1, bf16[64,256]{1,0:T(8,128)(2,1)} %kn_ref.1, bf16[64,256]{1,0:T(8,128)(2,1)} %vn_ref.1, bf16[1,2048,256]{2,1,0:T(8,128)(2,1)} %kr_ref.1, bf16[1,2048,256]{2,1,0:T(8,128)(2,1)} %vr_ref.1), custom_call_target="tpu_custom_call" | custom-call | tf_op jit(solution)/shard_map/pallas_call | solution.py:80
  8.5 1.5 collective-permute-start
  10.0 2.7 %collective-permute-start.2 = (bf16[64,2048]{1,0:T(8,128)(2,1)}, bf16[64,2048]{1,0:T(8,128)(2,1)S(1)}, u32[]{:S(2)}, u32[]{:S(2)}) collective-permute-start(bf16[64,2048]{1,0:T(8,128)(2,1)} %shard_map.127), channel_id=1, source_target_pairs={{0,128},{64,192},{128,0},{192,64},{1,129},{65,193},{129,1},{193,65... | collective-permute-start | bytes 786440 | tf_op jit(solution)/shard_map/ppermute | solution.py:200
  12.7 1.4 collective-permute-start.4
  14.1 0.0 copy-done
  14.1 1.4 convolution_bitcast_fusion
  15.6 2.5 %collective-permute-done = bf16[64,2048]{1,0:T(8,128)(2,1)S(1)} collective-permute-done((bf16[64,2048]{1,0:T(8,128)(2,1)}, bf16[64,2048]{1,0:T(8,128)(2,1)S(1)}, u32[]{:S(2)}, u32[]{:S(2)}) %collective-permute-start) | collective-permute-done | bytes 262176 | tf_op jit(solution)/shard_map/ppermute | solution.py:200
  18.1 0.5 fusion.17
  18.6 2.6 %collective-permute-start.1 = (f32[64,512]{1,0:T(8,128)S(1)}, f32[64,512]{1,0:T(8,128)S(1)}, u32[]{:S(2)}, u32[]{:S(2)}) collective-permute-start(f32[64,512]{1,0:T(8,128)S(1)} %fusion.17), channel_id=1, source_target_pairs={{0,192},{64,0},{128,64},{192,128},{1,193},{65,1},{129,65},{193,129... | collective-permute-start | bytes 393224 | tf_op jit(solution)/shard_map/ppermute | solution.py:202
  21.2 3.4 %collective-permute-done.2 = bf16[64,2048]{1,0:T(8,128)(2,1)S(1)} collective-permute-done((bf16[64,2048]{1,0:T(8,128)(2,1)}, bf16[64,2048]{1,0:T(8,128)(2,1)S(1)}, u32[]{:S(2)}, u32[]{:S(2)}) %collective-permute-start.2) | collective-permute-done | bytes 262176 | tf_op jit(solution)/shard_map/ppermute | solution.py:200
  24.6 0.5 fusion.18
  25.0 0.0 copy-start.5
  25.0 0.9 collective-permute-start.3
  26.0 0.0 collective-permute-done.4
  26.0 0.5 fusion.19
  26.4 0.8 collective-permute-start.5
  27.2 0.0 copy-done.5
  27.2 0.1 copy.50
  27.3 1.1 collective-permute-done.1
  28.4 4.0 %collective-permute-done.3 = f32[64,512]{1,0:T(8,128)S(1)} collective-permute-done((f32[64,512]{1,0:T(8,128)S(1)}, f32[64,512]{1,0:T(8,128)S(1)}, u32[]{:S(2)}, u32[]{:S(2)}) %collective-permute-start.3) | collective-permute-done | bytes 131104 | tf_op jit(solution)/shard_map/ppermute | solution.py:202
  32.4 1.4 collective-permute-done.5
  33.9 0.0 copy-start.4
  33.9 0.6 gather_fusion
  34.5 0.3 collective-permute-start.6
  34.8 0.1 convert_reduce_fusion
  35.0 0.1 reduce_window_sum.11
  35.1 1.2 select_reduce_fusion
  36.3 0.1 copy.51
  36.4 0.1 copy.52
  36.5 0.0 dynamic-slice-start
  36.5 0.5 fusion.7
  37.0 0.0 collective-permute-done.6
  37.0 0.0 copy-done.4
  37.0 1.2 multiply_reduce_fusion.1
  38.3 0.0 dynamic-slice-done
  38.3 0.6 convolution_convert_fusion
  38.9 1.0 copy.54
  39.9 54.6 %all_to_all.10 = bf16[128,48,128]{2,1,0:T(8,128)(2,1)S(1)} all-to-all(bf16[128,48,128]{2,1,0:T(8,128)(2,1)S(1)} %bitcast.60), channel_id=1, replica_groups=mesh['dp'=4,'expert'=32,'tensor'=2] {'dp','expert'}, dimensions={0} | all-to-all | bytes 3145728 | tf_op jit(solution)/shard_map/all_to_all | solution.py:227
  94.5 0.0 copy-start.1
  94.5 1.2 copy-done.1
  95.7 0.0 collective-permute-start.7
  95.7 0.5 collective-permute-start.9
  96.2 2.9 %collective-permute-done.7.other_ref = bf16[6144,128]{1,0:T(8,128)(2,1)S(1)} collective-permute-done((bf16[6144,128]{1,0:T(8,128)(2,1)S(1)}, bf16[6144,128]{1,0:T(8,128)(2,1)S(1)}, u32[]{:S(2)}, u32[]{:S(2)}) %collective-permute-start.7) | collective-permute-done | bytes 1572896 | tf_op jit(solution)/shard_map/ppermute | solution.py:171
  99.1 0.0 copy-start.2
  99.1 1.1 copy-done.2
  100.3 6.7 %shard_map.128.act_mine = bf16[768,384]{1,0:T(8,128)(2,1)} custom-call(s32[1]{0:T(128)} %bitcast.9.lane_ref, bf16[6144,128]{1,0:T(8,128)(2,1)} %bitcast.59, bf16[6144,128]{1,0:T(8,128)(2,1)} %copy-done.2, bf16[2048,384]{1,0:T(8,128)(2,1)} %bitcast.54, bf16[2048,384]{1,0:T(8,128)(2,1)} %bitcast.55, bf16[2048,384]{1,0:T(8,128)(2,1)} %bitcast.56, ...), custom_call_target="tpu_custom_call" | custom-call | tf_op jit(solution)/shard_map/pallas_call | solution.py:133
  106.9 0.1 collective-permute-start.8
  107.1 0.0 collective-permute-done.9.d_other
  107.1 2.1 %collective-permute-done.8.act_other = bf16[768,384]{1,0:T(8,128)(2,1)S(1)} collective-permute-done((bf16[768,384]{1,0:T(8,128)(2,1)}, bf16[768,384]{1,0:T(8,128)(2,1)S(1)}, u32[]{:S(2)}, u32[]{:S(2)}) %collective-permute-start.8) | collective-permute-done | bytes 589856 | tf_op jit(solution)/shard_map/ppermute | solution.py:171
  109.2 0.0 copy-start.3
  109.2 0.8 copy-done.3
  110.0 5.1 %shard_map.129 = bf16[6144,128]{1,0:T(8,128)(2,1)} custom-call(s32[1]{0:T(128)} %bitcast.9.lane_ref, bf16[768,384]{1,0:T(8,128)(2,1)} %shard_map.128.act_mine, bf16[768,384]{1,0:T(8,128)(2,1)} %copy-done.3, bf16[384,2048]{1,0:T(8,128)(2,1)} %bitcast.15.d_own, bf16[384,2048]{1,0:T(8,128)(2,1)} %collective-permute-done.9.d_other), custom_call_target="tpu_custom_call" | custom-call | tf_op jit(solution)/shard_map/pallas_call | solution.py:151
  115.1 0.0 copy-start.6
  115.1 7.7 %all-to-all-start.1 = ((bf16[128,48,128]{2,1,0:T(8,128)(2,1)}), bf16[128,48,128]{2,1,0:T(8,128)(2,1)}, u32[]{:S(2)}, u32[]{:S(2)}) async-start(bf16[128,48,128]{2,1,0:T(8,128)(2,1)} %bitcast.61), calls=%async_computation.1 | async-start | bytes 3145728 | tf_op jit(solution)/shard_map/all_to_all | solution.py:236
  122.8 0.0 copy-done.6
  122.8 0.1 copy.49
  122.9 0.6 multiply_reduce_fusion
  123.6 40.6 %all-to-all-done.1 = bf16[128,48,128]{2,1,0:T(8,128)(2,1)} async-done(((bf16[128,48,128]{2,1,0:T(8,128)(2,1)}), bf16[128,48,128]{2,1,0:T(8,128)(2,1)}, u32[]{:S(2)}, u32[]{:S(2)}) %all-to-all-start.1) | async-done | bytes 1572896 | tf_op jit(solution)/shard_map/all_to_all | solution.py:236
  164.1 1.9 %fusion.4 = f32[64,8,128]{2,0,1:T(8,128)S(1)} fusion(bf16[3,64,768,1]{2,1,3,0:T(8,128)(2,1)S(1)} %bitcast.65, bf16[768,8,128]{2,1,0:T(8,128)(2,1)} %bitcast.17), kind=kOutput, calls=%fused_computation.8 | convolution fusion | flops 302120960 | bytes 2129920 | tf_op jit(solution)/shard_map/sr,rjl->sjl/dot_general | solution.py:245
  166.1 0.7 fusion.8
  (9 shorter events, 0.2 us)
Async XLA Ops:
  0.0 14.1 %copy-start = (bf16[2048,512]{1,0:T(8,128)(2,1)S(1)}, bf16[2048,512]{1,0:T(8,128)(2,1)}, u32[]{:S(2)}) copy-start(bf16[2048,512]{1,0:T(8,128)(2,1)} %param.18) | copy-start | bytes 6291460
  8.5 9.6 %collective-permute-start = (bf16[64,2048]{1,0:T(8,128)(2,1)}, bf16[64,2048]{1,0:T(8,128)(2,1)S(1)}, u32[]{:S(2)}, u32[]{:S(2)}) collective-permute-start(bf16[64,2048]{1,0:T(8,128)(2,1)} %shard_map.127), channel_id=1, source_target_pairs={{0,64},{64,128},{128,192},{192,0},{1,65},{65,129},{129,193},{193,1... | collective-permute-start | bytes 786440 | tf_op jit(solution)/shard_map/ppermute | solution.py:200
  10.0 14.6 %collective-permute-start.2 = (bf16[64,2048]{1,0:T(8,128)(2,1)}, bf16[64,2048]{1,0:T(8,128)(2,1)S(1)}, u32[]{:S(2)}, u32[]{:S(2)}) collective-permute-start(bf16[64,2048]{1,0:T(8,128)(2,1)} %shard_map.127), channel_id=1, source_target_pairs={{0,128},{64,192},{128,0},{192,64},{1,129},{65,193},{129,1},{193,65... | collective-permute-start | bytes 786440 | tf_op jit(solution)/shard_map/ppermute | solution.py:200
  12.7 13.3 %collective-permute-start.4 = (bf16[64,2048]{1,0:T(8,128)(2,1)}, bf16[64,2048]{1,0:T(8,128)(2,1)S(1)}, u32[]{:S(2)}, u32[]{:S(2)}) collective-permute-start(bf16[64,2048]{1,0:T(8,128)(2,1)} %shard_map.127), channel_id=1, source_target_pairs={{0,192},{64,0},{128,64},{192,128},{1,193},{65,1},{129,65},{193,129... | collective-permute-start | bytes 786440 | tf_op jit(solution)/shard_map/ppermute | solution.py:200
  18.6 9.8 %collective-permute-start.1 = (f32[64,512]{1,0:T(8,128)S(1)}, f32[64,512]{1,0:T(8,128)S(1)}, u32[]{:S(2)}, u32[]{:S(2)}) collective-permute-start(f32[64,512]{1,0:T(8,128)S(1)} %fusion.17), channel_id=1, source_target_pairs={{0,192},{64,0},{128,64},{192,128},{1,193},{65,1},{129,65},{193,129... | collective-permute-start | bytes 393224 | tf_op jit(solution)/shard_map/ppermute | solution.py:202
  25.0 2.2 %copy-start.5 = (s32[64,8]{0,1:T(8,128)S(1)}, s32[64,8]{0,1:T(8,128)}, u32[]{:S(2)}) copy-start(s32[64,8]{0,1:T(8,128)} %param.21) | copy-start | bytes 6148
  25.0 7.4 %collective-permute-start.3 = (f32[64,512]{1,0:T(8,128)S(1)}, f32[64,512]{1,0:T(8,128)S(1)}, u32[]{:S(2)}, u32[]{:S(2)}) collective-permute-start(f32[64,512]{1,0:T(8,128)S(1)} %fusion.18), channel_id=1, source_target_pairs={{0,128},{64,192},{128,0},{192,64},{1,129},{65,193},{129,1},{193,65... | collective-permute-start | bytes 393224 | tf_op jit(solution)/shard_map/ppermute | solution.py:202
  26.4 7.4 %collective-permute-start.5 = (f32[64,512]{1,0:T(8,128)S(1)}, f32[64,512]{1,0:T(8,128)S(1)}, u32[]{:S(2)}, u32[]{:S(2)}) collective-permute-start(f32[64,512]{1,0:T(8,128)S(1)} %fusion.19), channel_id=1, source_target_pairs={{0,64},{64,128},{128,192},{192,0},{1,65},{65,129},{129,193},{193,1... | collective-permute-start | bytes 393224 | tf_op jit(solution)/shard_map/ppermute | solution.py:202
  33.9 3.2 %copy-start.4 = (bf16[64,2048]{1,0:T(8,128)(2,1)S(1)}, bf16[64,2048]{1,0:T(8,128)(2,1)}, u32[]{:S(2)}) copy-start(bf16[64,2048]{1,0:T(8,128)(2,1)} %param.19) | copy-start | bytes 786436
  34.5 2.5 %collective-permute-start.6 = (f32[64,2048]{1,0:T(8,128)S(1)}, f32[64,2048]{1,0:T(8,128)}, u32[]{:S(2)}, u32[]{:S(2)}) collective-permute-start(f32[64,2048]{1,0:T(8,128)S(1)} %bitcast.63), channel_id=1, source_target_pairs={{0,1},{1,0},{2,3},{3,2},{4,5},{5,4},{6,7},{7,6},{8,9},{9,8},{10,11... | collective-permute-start | bytes 1572872 | tf_op jit(solution)/shard_map/ppermute | solution.py:171
  36.5 1.8 %dynamic-slice-start = ((f32[2048]{0:T(1024)}, s32[]{:T(128)}), f32[1024]{0:T(1024)S(1)}, s32[]{:S(2)}) async-start(f32[2048]{0:T(1024)} %param.20, s32[]{:T(128)} %select_n.30), calls=%async_computation.2 | async-start | bytes 8704 | tf_op jit(solution)/shard_map/dynamic_slice | solution.py:211
  94.5 1.2 copy-start.1
  95.7 3.4 %collective-permute-start.7 = (bf16[6144,128]{1,0:T(8,128)(2,1)S(1)}, bf16[6144,128]{1,0:T(8,128)(2,1)S(1)}, u32[]{:S(2)}, u32[]{:S(2)}) collective-permute-start(bf16[6144,128]{1,0:T(8,128)(2,1)S(1)} %bitcast.58), channel_id=1, source_target_pairs={{0,1},{1,0},{2,3},{3,2},{4,5},{5,4},{6,7},{7,6},{8,9},{9,8},{10,11... | collective-permute-start | bytes 4718600 | tf_op jit(solution)/shard_map/ppermute | solution.py:171
  95.7 11.4 %collective-permute-start.9 = (bf16[384,2048]{1,0:T(8,128)(2,1)}, bf16[384,2048]{1,0:T(8,128)(2,1)}, u32[]{:S(2)}, u32[]{:S(2)}) collective-permute-start(bf16[384,2048]{1,0:T(8,128)(2,1)} %bitcast.15.d_own), channel_id=1, source_target_pairs={{0,1},{1,0},{2,3},{3,2},{4,5},{5,4},{6,7},{7,6},{8,9},{9,8},{10,11... | collective-permute-start | bytes 4718600 | tf_op jit(solution)/shard_map/ppermute | solution.py:171
  99.1 1.2 copy-start.2
  106.9 2.2 %collective-permute-start.8 = (bf16[768,384]{1,0:T(8,128)(2,1)}, bf16[768,384]{1,0:T(8,128)(2,1)S(1)}, u32[]{:S(2)}, u32[]{:S(2)}) collective-permute-start(bf16[768,384]{1,0:T(8,128)(2,1)} %shard_map.128.act_mine), channel_id=1, source_target_pairs={{0,1},{1,0},{2,3},{3,2},{4,5},{5,4},{6,7},{7,6},{8,9},{9,8},{10,11... | collective-permute-start | bytes 1769480 | tf_op jit(solution)/shard_map/ppermute | solution.py:171
  109.2 0.8 copy-start.3
  115.1 7.7 %copy-start.6 = (f32[64,8]{0,1:T(8,128)S(1)}, f32[64,8]{0,1:T(8,128)}, u32[]{:S(2)}) copy-start(f32[64,8]{0,1:T(8,128)} %param.22) | copy-start | bytes 6148
  115.1 49.0 %all-to-all-start.1 = ((bf16[128,48,128]{2,1,0:T(8,128)(2,1)}), bf16[128,48,128]{2,1,0:T(8,128)(2,1)}, u32[]{:S(2)}, u32[]{:S(2)}) async-start(bf16[128,48,128]{2,1,0:T(8,128)(2,1)} %bitcast.61), calls=%async_computation.1 | async-start | bytes 3145728 | tf_op jit(solution)/shard_map/all_to_all | solution.py:236

commit v10 on v8

--- a/solution.py
+++ b/solution.py
@@ -62,8 +62,9 @@
     w_res = jnp.exp(s_res - top)
     w_new = jnp.exp(s_new - top)
     total = jnp.sum(w_res, axis=1, keepdims=True) + jnp.sum(w_new, axis=1, keepdims=True)
-    p_res = (w_res / total).astype(jnp.bfloat16)
-    p_new = (w_new / total).astype(jnp.bfloat16)
+    inverse = 1.0 / total
+    p_res = (w_res * inverse).astype(jnp.bfloat16)
+    p_new = (w_new * inverse).astype(jnp.bfloat16)
     out = jnp.dot(p_res, v_res, preferred_element_type=jnp.float32) + jnp.dot(
         p_new, v_new, preferred_element_type=jnp.float32
     )

time: 166 us -> 166 us (level)
  no operation moved by 1% of the time
where the time goes in v10:
time: 166 us; the launch traced here: 165 us
  waiting for transfers between devices  57.8 us (35%)
  blocking collectives  54.7 us (33%)
  Pallas kernels  20.3 us (12%)
  starting transfers between devices  18.6 us (11%)
  matrix products  6.26 us (4%)
  other arithmetic  4.04 us (2%)
  local copies, waits for them, and re-layouts  3.16 us (2%)
    all_to_all x1, blocking collectives, per_device(): lax.all_to_all(outgoing.reshape(owners, CAP * width, lanes), ('dp', 'expe...  54.7 us
    all_to_all x1, waiting for transfers between devices, per_device(): lax.all_to_all(expert_out.reshape(owners, CAP * width, lanes), ('dp', 'ex...  41.3 us
    pallas_call x1, Pallas kernels, attend_kernel(): pl.pallas_call(attention_kernel, grid=(kv_here,), in_specs=[pl.BlockSpec(...  8.47 us
    all_to_all x1, starting transfers between devices, per_device(): lax.all_to_all(expert_out.reshape(owners, CAP * width, lanes), ('dp', 'ex...  7.66 us
    pallas_call x1, Pallas kernels, gate_up(): pl.pallas_call(gate_up_kernel, grid_spec=pltpu.PrefetchScalarGridSpec(num...  6.68 us
    ppermute x3, waiting for transfers between devices, per_device(): blocks.append(lax.ppermute(product, 'dp', backward))  6.49 us
    ppermute x3, waiting for transfers between devices, per_device(): arrived = lax.ppermute(attended, 'dp', onward)  5.87 us
    ppermute x3, starting transfers between devices, per_device(): arrived = lax.ppermute(attended, 'dp', onward)  5.66 us
  transfers between devices with their start and end apart: 11, of which 8 were waited for; matrix products, arithmetic and copies ran while one was open for 4% of the time, Pallas kernels for 4%

profile of v10, /device:TPU:32, one launch (start us, length us, event | category | flops | bytes accessed | tf_op | source)
XLA Modules:
  0.0 165.1 jit_solution(2392637434476256801)
XLA Ops:
  0.0 0.0 copy-start
  0.0 8.5 %shard_map.127 = bf16[64,2048]{1,0:T(8,128)(2,1)} custom-call(bf16[64,2048]{1,0:T(8,128)(2,1)} %q_ref.1, bf16[64,256]{1,0:T(8,128)(2,1)} %kn_ref.1, bf16[64,256]{1,0:T(8,128)(2,1)} %vn_ref.1, bf16[1,2048,256]{2,1,0:T(8,128)(2,1)} %kr_ref.1, bf16[1,2048,256]{2,1,0:T(8,128)(2,1)} %vr_ref.1), custom_call_target="tpu_custom_call" | custom-call | tf_op jit(solution)/shard_map/pallas_call | solution.py:81
  8.5 1.5 collective-permute-start
  10.0 2.7 %collective-permute-start.2 = (bf16[64,2048]{1,0:T(8,128)(2,1)}, bf16[64,2048]{1,0:T(8,128)(2,1)S(1)}, u32[]{:S(2)}, u32[]{:S(2)}) collective-permute-start(bf16[64,2048]{1,0:T(8,128)(2,1)} %shard_map.127), channel_id=1, source_target_pairs={{0,128},{64,192},{128,0},{192,64},{1,129},{65,193},{129,1},{193,65... | collective-permute-start | bytes 786440 | tf_op jit(solution)/shard_map/ppermute | solution.py:201
  12.7 1.4 collective-permute-start.4
  14.1 0.0 copy-done
  14.1 1.4 convolution_bitcast_fusion
  15.6 2.5 %collective-permute-done = bf16[64,2048]{1,0:T(8,128)(2,1)S(1)} collective-permute-done((bf16[64,2048]{1,0:T(8,128)(2,1)}, bf16[64,2048]{1,0:T(8,128)(2,1)S(1)}, u32[]{:S(2)}, u32[]{:S(2)}) %collective-permute-start) | collective-permute-done | bytes 262176 | tf_op jit(solution)/shard_map/ppermute | solution.py:201
  18.1 0.5 fusion.14
  18.6 2.6 %collective-permute-start.1 = (f32[64,512]{1,0:T(8,128)S(1)}, f32[64,512]{1,0:T(8,128)S(1)}, u32[]{:S(2)}, u32[]{:S(2)}) collective-permute-start(f32[64,512]{1,0:T(8,128)S(1)} %fusion.14), channel_id=1, source_target_pairs={{0,192},{64,0},{128,64},{192,128},{1,193},{65,1},{129,65},{193,129... | collective-permute-start | bytes 393224 | tf_op jit(solution)/shard_map/ppermute | solution.py:203
  21.2 3.4 %collective-permute-done.2 = bf16[64,2048]{1,0:T(8,128)(2,1)S(1)} collective-permute-done((bf16[64,2048]{1,0:T(8,128)(2,1)}, bf16[64,2048]{1,0:T(8,128)(2,1)S(1)}, u32[]{:S(2)}, u32[]{:S(2)}) %collective-permute-start.2) | collective-permute-done | bytes 262176 | tf_op jit(solution)/shard_map/ppermute | solution.py:201
  24.5 0.5 fusion.15
  25.0 0.0 copy-start.2
  25.0 0.9 collective-permute-start.3
  25.9 0.0 collective-permute-done.4
  25.9 0.5 fusion.16
  26.4 0.8 collective-permute-start.5
  27.2 0.0 copy-done.2
  27.2 0.1 copy.34
  27.3 1.1 collective-permute-done.1
  28.4 4.0 %collective-permute-done.3 = f32[64,512]{1,0:T(8,128)S(1)} collective-permute-done((f32[64,512]{1,0:T(8,128)S(1)}, f32[64,512]{1,0:T(8,128)S(1)}, u32[]{:S(2)}, u32[]{:S(2)}) %collective-permute-start.3) | collective-permute-done | bytes 131104 | tf_op jit(solution)/shard_map/ppermute | solution.py:203
  32.4 1.4 collective-permute-done.5
  33.9 0.0 copy-start.1
  33.9 0.6 gather_fusion
  34.5 0.3 collective-permute-start.6
  34.8 0.1 convert_reduce_fusion
  34.9 0.1 reduce_window_sum.11
  35.0 1.2 select_reduce_fusion
  36.3 0.1 copy.35
  36.4 0.1 copy.36
  36.4 0.0 dynamic-slice-start
  36.5 0.5 fusion.5
  37.0 0.0 collective-permute-done.6
  37.0 0.0 copy-done.1
  37.0 1.2 multiply_reduce_fusion.1
  38.3 0.0 dynamic-slice-done
  38.3 0.6 convolution_convert_fusion
  38.9 1.0 copy.38
  39.9 54.7 %all_to_all.10 = bf16[128,48,128]{2,1,0:T(8,128)(2,1)} all-to-all(bf16[128,48,128]{2,1,0:T(8,128)(2,1)S(1)} %bitcast.55), channel_id=1, replica_groups=mesh['dp'=4,'expert'=32,'tensor'=2] {'dp','expert'}, dimensions={0} | all-to-all | bytes 3145728 | tf_op jit(solution)/shard_map/all_to_all | solution.py:228
  94.6 0.0 collective-permute-start.7
  94.6 1.2 dynamic-slice_bitcast_fusion
  95.8 0.6 collective-permute-start.9
  96.4 2.0 %collective-permute-done.7.other_ref = bf16[6144,128]{1,0:T(8,128)(2,1)} collective-permute-done((bf16[6144,128]{1,0:T(8,128)(2,1)}, bf16[6144,128]{1,0:T(8,128)(2,1)}, u32[]{:S(2)}, u32[]{:S(2)}) %collective-permute-start.7) | collective-permute-done | bytes 1572896 | tf_op jit(solution)/shard_map/ppermute | solution.py:172
  98.4 6.7 %shard_map.128.act_mine = bf16[768,384]{1,0:T(8,128)(2,1)} custom-call(s32[1]{0:T(128)} %bitcast.8.lane_ref, bf16[6144,128]{1,0:T(8,128)(2,1)} %bitcast.11.mine_ref, bf16[6144,128]{1,0:T(8,128)(2,1)} %collective-permute-done.7.other_ref, bf16[2048,384]{1,0:T(8,128)(2,1)} %bitcast.51, bf16[2048,384]{1,0:T(8,128)(2,1)} %bitcast.52, ...), custom_call_target="tpu_custom_call" | custom-call | tf_op jit(solution)/shard_map/pallas_call | solution.py:134
  105.1 0.1 collective-permute-start.8
  105.2 0.0 collective-permute-done.9.d_other
  105.2 2.2 %collective-permute-done.8.act_other = bf16[768,384]{1,0:T(8,128)(2,1)} collective-permute-done((bf16[768,384]{1,0:T(8,128)(2,1)}, bf16[768,384]{1,0:T(8,128)(2,1)}, u32[]{:S(2)}, u32[]{:S(2)}) %collective-permute-start.8) | collective-permute-done | bytes 589856 | tf_op jit(solution)/shard_map/ppermute | solution.py:172
  107.4 5.1 %shard_map.129 = bf16[6144,128]{1,0:T(8,128)(2,1)} custom-call(s32[1]{0:T(128)} %bitcast.8.lane_ref, bf16[768,384]{1,0:T(8,128)(2,1)} %shard_map.128.act_mine, bf16[768,384]{1,0:T(8,128)(2,1)} %collective-permute-done.8.act_other, bf16[384,2048]{1,0:T(8,128)(2,1)} %bitcast.57, bf16[384,1024]{1,0:T(8,128)(2,1)} %collective-permute-done.9.d_other), custom_call_target="tpu_custom_call" | custom-call | tf_op jit(solution)/shard_map/pallas_call | solution.py:152
  112.6 0.0 copy-start.3
  112.6 7.7 %all-to-all-start.1 = ((bf16[128,48,128]{2,1,0:T(8,128)(2,1)}), bf16[128,48,128]{2,1,0:T(8,128)(2,1)}, u32[]{:S(2)}, u32[]{:S(2)}) async-start(bf16[128,48,128]{2,1,0:T(8,128)(2,1)} %bitcast.56), calls=%async_computation.1 | async-start | bytes 3145728 | tf_op jit(solution)/shard_map/all_to_all | solution.py:237
  120.2 0.0 copy-done.3
  120.2 0.1 copy.33
  120.3 41.3 %all-to-all-done.1 = bf16[128,48,128]{2,1,0:T(8,128)(2,1)} async-done(((bf16[128,48,128]{2,1,0:T(8,128)(2,1)}), bf16[128,48,128]{2,1,0:T(8,128)(2,1)}, u32[]{:S(2)}, u32[]{:S(2)}) %all-to-all-start.1) | async-done | bytes 1572896 | tf_op jit(solution)/shard_map/all_to_all | solution.py:237
  161.6 2.8 %multiply_reduce_fusion = f32[64,8,128]{2,1,0:T(8,128)S(1)} fusion(bf16[768,8,128]{2,1,0:T(8,128)(2,1)} %bitcast.17, f32[64,8]{1,0:T(8,128)S(1)} %copy.33, s32[64,8]{1,0:T(8,128)S(1)} %copy.36), kind=kOutput, calls=%fused_computation.1 | convolution fusion | flops 806682624 | bytes 1839104 | tf_op jit(solution)/shard_map/tkr,rjl->tkjl/dot_general | solution.py:240
  164.4 0.7 fusion.7
  (7 shorter events, 0.1 us)
Async XLA Ops:
  0.0 14.1 %copy-start = (bf16[2048,512]{1,0:T(8,128)(2,1)S(1)}, bf16[2048,512]{1,0:T(8,128)(2,1)}, u32[]{:S(2)}) copy-start(bf16[2048,512]{1,0:T(8,128)(2,1)} %param.18) | copy-start | bytes 6291460
  8.5 9.6 %collective-permute-start = (bf16[64,2048]{1,0:T(8,128)(2,1)}, bf16[64,2048]{1,0:T(8,128)(2,1)S(1)}, u32[]{:S(2)}, u32[]{:S(2)}) collective-permute-start(bf16[64,2048]{1,0:T(8,128)(2,1)} %shard_map.127), channel_id=1, source_target_pairs={{0,64},{64,128},{128,192},{192,0},{1,65},{65,129},{129,193},{193,1... | collective-permute-start | bytes 786440 | tf_op jit(solution)/shard_map/ppermute | solution.py:201
  10.0 14.6 %collective-permute-start.2 = (bf16[64,2048]{1,0:T(8,128)(2,1)}, bf16[64,2048]{1,0:T(8,128)(2,1)S(1)}, u32[]{:S(2)}, u32[]{:S(2)}) collective-permute-start(bf16[64,2048]{1,0:T(8,128)(2,1)} %shard_map.127), channel_id=1, source_target_pairs={{0,128},{64,192},{128,0},{192,64},{1,129},{65,193},{129,1},{193,65... | collective-permute-start | bytes 786440 | tf_op jit(solution)/shard_map/ppermute | solution.py:201
  12.7 13.3 %collective-permute-start.4 = (bf16[64,2048]{1,0:T(8,128)(2,1)}, bf16[64,2048]{1,0:T(8,128)(2,1)S(1)}, u32[]{:S(2)}, u32[]{:S(2)}) collective-permute-start(bf16[64,2048]{1,0:T(8,128)(2,1)} %shard_map.127), channel_id=1, source_target_pairs={{0,192},{64,0},{128,64},{192,128},{1,193},{65,1},{129,65},{193,129... | collective-permute-start | bytes 786440 | tf_op jit(solution)/shard_map/ppermute | solution.py:201
  18.6 9.8 %collective-permute-start.1 = (f32[64,512]{1,0:T(8,128)S(1)}, f32[64,512]{1,0:T(8,128)S(1)}, u32[]{:S(2)}, u32[]{:S(2)}) collective-permute-start(f32[64,512]{1,0:T(8,128)S(1)} %fusion.14), channel_id=1, source_target_pairs={{0,192},{64,0},{128,64},{192,128},{1,193},{65,1},{129,65},{193,129... | collective-permute-start | bytes 393224 | tf_op jit(solution)/shard_map/ppermute | solution.py:203
  25.0 2.2 %copy-start.2 = (s32[64,8]{0,1:T(8,128)S(1)}, s32[64,8]{0,1:T(8,128)}, u32[]{:S(2)}) copy-start(s32[64,8]{0,1:T(8,128)} %param.21) | copy-start | bytes 6148
  25.0 7.4 %collective-permute-start.3 = (f32[64,512]{1,0:T(8,128)S(1)}, f32[64,512]{1,0:T(8,128)S(1)}, u32[]{:S(2)}, u32[]{:S(2)}) collective-permute-start(f32[64,512]{1,0:T(8,128)S(1)} %fusion.15), channel_id=1, source_target_pairs={{0,128},{64,192},{128,0},{192,64},{1,129},{65,193},{129,1},{193,65... | collective-permute-start | bytes 393224 | tf_op jit(solution)/shard_map/ppermute | solution.py:203
  26.4 7.4 %collective-permute-start.5 = (f32[64,512]{1,0:T(8,128)S(1)}, f32[64,512]{1,0:T(8,128)S(1)}, u32[]{:S(2)}, u32[]{:S(2)}) collective-permute-start(f32[64,512]{1,0:T(8,128)S(1)} %fusion.16), channel_id=1, source_target_pairs={{0,64},{64,128},{128,192},{192,0},{1,65},{65,129},{129,193},{193,1... | collective-permute-start | bytes 393224 | tf_op jit(solution)/shard_map/ppermute | solution.py:203
  33.9 3.2 %copy-start.1 = (bf16[64,2048]{1,0:T(8,128)(2,1)S(1)}, bf16[64,2048]{1,0:T(8,128)(2,1)}, u32[]{:S(2)}) copy-start(bf16[64,2048]{1,0:T(8,128)(2,1)} %param.19) | copy-start | bytes 786436
  34.5 2.5 %collective-permute-start.6 = (f32[64,2048]{1,0:T(8,128)S(1)}, f32[64,2048]{1,0:T(8,128)}, u32[]{:S(2)}, u32[]{:S(2)}) collective-permute-start(f32[64,2048]{1,0:T(8,128)S(1)} %bitcast.59), channel_id=1, source_target_pairs={{0,1},{1,0},{2,3},{3,2},{4,5},{5,4},{6,7},{7,6},{8,9},{9,8},{10,11... | collective-permute-start | bytes 1572872 | tf_op jit(solution)/shard_map/ppermute | solution.py:172
  36.4 1.8 %dynamic-slice-start = ((f32[2048]{0:T(1024)}, s32[]{:T(128)}), f32[1024]{0:T(1024)S(1)}, s32[]{:S(2)}) async-start(f32[2048]{0:T(1024)} %param.20, s32[]{:T(128)} %select_n.33), calls=%async_computation.2 | async-start | bytes 8704 | tf_op jit(solution)/shard_map/dynamic_slice | solution.py:212
  94.6 3.8 %collective-permute-start.7 = (bf16[6144,128]{1,0:T(8,128)(2,1)}, bf16[6144,128]{1,0:T(8,128)(2,1)}, u32[]{:S(2)}, u32[]{:S(2)}) collective-permute-start(bf16[6144,128]{1,0:T(8,128)(2,1)} %bitcast.11.mine_ref), channel_id=1, source_target_pairs={{0,1},{1,0},{2,3},{3,2},{4,5},{5,4},{6,7},{7,6},{8,9},{9,8},{10,11... | collective-permute-start | bytes 4718600 | tf_op jit(solution)/shard_map/ppermute | solution.py:172
  95.8 9.4 %collective-permute-start.9 = (bf16[384,1024]{1,0:T(8,128)(2,1)S(1)}, bf16[384,1024]{1,0:T(8,128)(2,1)}, u32[]{:S(2)}, u32[]{:S(2)}) collective-permute-start(bf16[384,1024]{1,0:T(8,128)(2,1)S(1)} %dynamic-slice_bitcast_fusion), channel_id=1, source_target_pairs={{0,1},{1,0},{2,3},{3,2},{4,5},{5,4},{6,7},{7,6},{8,9},{9,8},{10,11... | collective-permute-start | bytes 2359304 | tf_op jit(solution)/shard_map/ppermute | solution.py:172
  105.1 2.3 %collective-permute-start.8 = (bf16[768,384]{1,0:T(8,128)(2,1)}, bf16[768,384]{1,0:T(8,128)(2,1)}, u32[]{:S(2)}, u32[]{:S(2)}) collective-permute-start(bf16[768,384]{1,0:T(8,128)(2,1)} %shard_map.128.act_mine), channel_id=1, source_target_pairs={{0,1},{1,0},{2,3},{3,2},{4,5},{5,4},{6,7},{7,6},{8,9},{9,8},{10,11... | collective-permute-start | bytes 1769480 | tf_op jit(solution)/shard_map/ppermute | solution.py:172
  112.6 7.7 %copy-start.3 = (f32[64,8]{0,1:T(8,128)S(1)}, f32[64,8]{0,1:T(8,128)}, u32[]{:S(2)}) copy-start(f32[64,8]{0,1:T(8,128)} %param.22) | copy-start | bytes 6148
  112.6 49.0 %all-to-all-start.1 = ((bf16[128,48,128]{2,1,0:T(8,128)(2,1)}), bf16[128,48,128]{2,1,0:T(8,128)(2,1)}, u32[]{:S(2)}, u32[]{:S(2)}) async-start(bf16[128,48,128]{2,1,0:T(8,128)(2,1)} %bitcast.56), calls=%async_computation.1 | async-start | bytes 3145728 | tf_op jit(solution)/shard_map/all_to_all | solution.py:237

commit v11 on v10

--- a/solution.py
+++ b/solution.py
@@ -166,6 +166,37 @@
         out_shape=jax.ShapeDtypeStruct((rows * fold, HEAD_WIDTH), jnp.bfloat16),
         interpret=interpret,
     )(lane, act_mine, act_other, down_mat, down_other)
+
+
+def combine_kernel(code_ref, gates_ref, ret_ref, hid_ref, out_ref):
+    fold = hid_ref.shape[1] // HEAD_WIDTH
+    rows = ret_ref.shape[0] // fold
+    tokens, top = code_ref.shape
+    places = lax.broadcasted_iota(jnp.int32, (tokens, rows), 1)
+    code = code_ref[...]
+    gates = gates_ref[...]
+    spread = jnp.zeros((tokens, rows), jnp.float32)
+    for k in range(top):
+        spread = spread + jnp.where(places == code[:, k:k + 1], gates[:, k:k + 1], jnp.float32(0.0))
+    first = spread.astype(jnp.bfloat16)
+    rest = spread - first.astype(jnp.float32)
+    second = rest.astype(jnp.bfloat16)
+    third = (rest - second.astype(jnp.float32)).astype(jnp.bfloat16)
+    returned = jnp.concatenate(
+        [ret_ref[pl.ds(j, rows, stride=fold), :] for j in range(fold)], axis=1
+    )
+    moe = jnp.dot(first, returned, preferred_element_type=jnp.float32)
+    moe = moe + jnp.dot(second, returned, preferred_element_type=jnp.float32)
+    moe = moe + jnp.dot(third, returned, preferred_element_type=jnp.float32)
+    out_ref[...] = (hid_ref[...] + moe).astype(out_ref.dtype)
+
+
+def combine(code, gates, returned, hidden_half, interpret=False):
+    return pl.pallas_call(
+        combine_kernel,
+        out_shape=jax.ShapeDtypeStruct(hidden_half.shape, jnp.bfloat16),
+        interpret=interpret,
+    )(code, gates, returned, hidden_half)
 
 
 def swap_pair(x):
@@ -236,10 +267,8 @@
 
     returned = lax.all_to_all(
         expert_out.reshape(owners, CAP * width, lanes), ("dp", "expert"), split_axis=0, concat_axis=0, tiled=True
-    ).reshape(owners * CAP, width, lanes)
-    picked = jnp.einsum("tkr,rjl->tkjl", pick, returned, preferred_element_type=jnp.float32)
-    moe = jnp.sum(gates[:, :, None, None] * picked, axis=1).reshape(tokens_here, half)
-    return (hidden_half + moe).astype(jnp.bfloat16)
+    ).reshape(owners * CAP * width, lanes)
+    return combine(code, gates, returned, hidden_half)
 
 
 def solution(mesh):

time: 166 us -> 167 us (level)
  Pallas kernels: 20.3 us -> 23.7 us
  matrix products: 6.26 us -> 3.44 us
  local copies, waits for them, and re-layouts: 3.16 us -> 5.18 us
    pallas_call x0 -> x1, Pallas kernels: none -> 3.37 us  [combine(): pl.pallas_call(combine_kernel, out_shape=jax.ShapeDtypeStruct(hidden_half...]
    dot_general x1 -> x0, matrix products: 2.78 us -> none  [per_device(): jnp.einsum('tkr,rjl->tkjl', pick, returned, preferred_element_type=jnp.fl...]
    unnamed x10 -> x18, local copies, waits for them, and re-layouts: 0.19 us -> 2.27 us
where the time goes in v11:
time: 167 us
  waiting for transfers between devices  57 us (34%)
  blocking collectives  54.7 us (33%)
  Pallas kernels  23.7 us (14%)
  starting transfers between devices  18.6 us (11%)
  local copies, waits for them, and re-layouts  5.18 us (3%)
  other arithmetic  4.04 us (2%)
  matrix products  3.44 us (2%)
    all_to_all x1, blocking collectives, per_device(): lax.all_to_all(outgoing.reshape(owners, CAP * width, lanes), ('dp', 'expe...  54.7 us
    all_to_all x1, waiting for transfers between devices, per_device(): lax.all_to_all(expert_out.reshape(owners, CAP * width, lanes), ('dp', 'ex...  40.7 us
    pallas_call x1, Pallas kernels, attend_kernel(): pl.pallas_call(attention_kernel, grid=(kv_here,), in_specs=[pl.BlockSpec(...  8.48 us
    all_to_all x1, starting transfers between devices, per_device(): lax.all_to_all(expert_out.reshape(owners, CAP * width, lanes), ('dp', 'ex...  7.65 us
    pallas_call x1, Pallas kernels, gate_up(): pl.pallas_call(gate_up_kernel, grid_spec=pltpu.PrefetchScalarGridSpec(num...  6.68 us
    ppermute x3, waiting for transfers between devices, per_device(): blocks.append(lax.ppermute(product, 'dp', backward))  6.47 us
    ppermute x3, waiting for transfers between devices, per_device(): arrived = lax.ppermute(attended, 'dp', onward)  5.86 us
    ppermute x3, starting transfers between devices, per_device(): arrived = lax.ppermute(attended, 'dp', onward)  5.66 us
  transfers between devices with their start and end apart: 11, of which 8 were waited for; matrix products, arithmetic and copies ran while one was open for 4% of the time, Pallas kernels for 4%

profile of v11, /device:TPU:32, one launch (start us, length us, event | category | flops | bytes accessed | tf_op | source)
XLA Modules:
  0.0 166.9 jit_solution(9756431802092725681)
XLA Ops:
  0.0 0.0 copy-start
  0.0 8.5 %shard_map.127 = bf16[64,2048]{1,0:T(8,128)(2,1)} custom-call(bf16[64,2048]{1,0:T(8,128)(2,1)} %q_ref.1, bf16[64,256]{1,0:T(8,128)(2,1)} %kn_ref.1, bf16[64,256]{1,0:T(8,128)(2,1)} %vn_ref.1, bf16[1,2048,256]{2,1,0:T(8,128)(2,1)} %kr_ref.1, bf16[1,2048,256]{2,1,0:T(8,128)(2,1)} %vr_ref.1), custom_call_target="tpu_custom_call" | custom-call | tf_op jit(solution)/shard_map/pallas_call | solution.py:81
  8.5 1.5 collective-permute-start
  10.0 2.7 %collective-permute-start.2 = (bf16[64,2048]{1,0:T(8,128)(2,1)}, bf16[64,2048]{1,0:T(8,128)(2,1)S(1)}, u32[]{:S(2)}, u32[]{:S(2)}) collective-permute-start(bf16[64,2048]{1,0:T(8,128)(2,1)} %shard_map.127), channel_id=1, source_target_pairs={{0,128},{64,192},{128,0},{192,64},{1,129},{65,193},{129,1},{193,65... | collective-permute-start | bytes 786440 | tf_op jit(solution)/shard_map/ppermute | solution.py:232
  12.7 1.4 collective-permute-start.4
  14.1 0.0 copy-done
  14.1 1.4 convolution_bitcast_fusion
  15.6 2.5 %collective-permute-done = bf16[64,2048]{1,0:T(8,128)(2,1)S(1)} collective-permute-done((bf16[64,2048]{1,0:T(8,128)(2,1)}, bf16[64,2048]{1,0:T(8,128)(2,1)S(1)}, u32[]{:S(2)}, u32[]{:S(2)}) %collective-permute-start) | collective-permute-done | bytes 262176 | tf_op jit(solution)/shard_map/ppermute | solution.py:232
  18.1 0.5 fusion.8
  18.6 0.0 copy-start.6
  18.6 2.6 %collective-permute-start.1 = (f32[64,512]{1,0:T(8,128)S(1)}, f32[64,512]{1,0:T(8,128)}, u32[]{:S(2)}, u32[]{:S(2)}) collective-permute-start(f32[64,512]{1,0:T(8,128)S(1)} %fusion.8), channel_id=1, source_target_pairs={{0,192},{64,0},{128,64},{192,128},{1,193},{65,1},{129,65},{193,129... | collective-permute-start | bytes 393224 | tf_op jit(solution)/shard_map/ppermute | solution.py:234
  21.2 3.4 %collective-permute-done.2 = bf16[64,2048]{1,0:T(8,128)(2,1)S(1)} collective-permute-done((bf16[64,2048]{1,0:T(8,128)(2,1)}, bf16[64,2048]{1,0:T(8,128)(2,1)S(1)}, u32[]{:S(2)}, u32[]{:S(2)}) %collective-permute-start.2) | collective-permute-done | bytes 262176 | tf_op jit(solution)/shard_map/ppermute | solution.py:232
  24.6 0.5 fusion.9
  25.0 0.9 collective-permute-start.3
  25.9 0.0 collective-permute-done.4
  25.9 0.5 fusion.10
  26.4 0.0 copy-start.3
  26.4 0.8 collective-permute-start.5
  27.2 0.0 copy-done.6
  27.2 0.1 copy.33
  27.3 1.2 collective-permute-done.1
  28.5 3.9 %collective-permute-done.3 = f32[64,512]{1,0:T(8,128)S(1)} collective-permute-done((f32[64,512]{1,0:T(8,128)S(1)}, f32[64,512]{1,0:T(8,128)S(1)}, u32[]{:S(2)}, u32[]{:S(2)}) %collective-permute-start.3) | collective-permute-done | bytes 131104 | tf_op jit(solution)/shard_map/ppermute | solution.py:234
  32.4 0.0 copy-start.4
  32.4 1.4 collective-permute-done.5
  33.8 0.0 copy-start.5
  33.8 0.0 copy-done.4
  33.8 0.7 copy-done.5
  34.5 1.1 pad_maximum_fusion
  35.5 0.6 gather_fusion
  36.2 0.3 collective-permute-start.6
  36.5 0.1 convert_reduce_fusion
  36.6 0.1 reduce_window_sum.11
  36.7 0.1 copy.34
  36.8 0.0 dynamic-slice-start
  36.8 1.2 select_reduce_fusion
  38.1 0.0 copy-start.2
  38.1 0.5 fusion.1
  38.6 0.0 collective-permute-done.6
  38.6 0.0 copy-done.3
  38.6 0.2 multiply_reduce_fusion
  38.8 0.0 dynamic-slice-done
  38.8 0.7 fusion.2
  39.6 0.6 convolution_convert_fusion
  40.2 0.0 copy-done.2
  40.2 1.0 copy.37
  41.2 54.7 %all_to_all.10 = bf16[128,48,128]{2,1,0:T(8,128)(2,1)} all-to-all(bf16[128,48,128]{2,1,0:T(8,128)(2,1)S(1)} %bitcast.40), channel_id=1, replica_groups=mesh['dp'=4,'expert'=32,'tensor'=2] {'dp','expert'}, dimensions={0} | all-to-all | bytes 3145728 | tf_op jit(solution)/shard_map/all_to_all | solution.py:259
  95.9 0.0 collective-permute-start.7
  95.9 1.2 dynamic-slice_bitcast_fusion
  97.1 0.6 collective-permute-start.9
  97.7 2.0 %collective-permute-done.7.other_ref = bf16[6144,128]{1,0:T(8,128)(2,1)} collective-permute-done((bf16[6144,128]{1,0:T(8,128)(2,1)}, bf16[6144,128]{1,0:T(8,128)(2,1)}, u32[]{:S(2)}, u32[]{:S(2)}) %collective-permute-start.7) | collective-permute-done | bytes 1572896 | tf_op jit(solution)/shard_map/ppermute | solution.py:203
  99.7 6.7 %shard_map.128.act_mine = bf16[768,384]{1,0:T(8,128)(2,1)} custom-call(s32[1]{0:T(128)} %bitcast.lane_ref, bf16[6144,128]{1,0:T(8,128)(2,1)} %bitcast.9.mine_ref, bf16[6144,128]{1,0:T(8,128)(2,1)} %collective-permute-done.7.other_ref, bf16[2048,384]{1,0:T(8,128)(2,1)} %bitcast.36, bf16[2048,384]{1,0:T(8,128)(2,1)} %bitcast.37, bf16[2048,384]{1,0:T(8,128)(2,1)} %bitcast.38, ...), custom_call_target="tpu_custom_call" | custom-call | tf_op jit(solution)/shard_map/pallas_call | solution.py:134
  106.3 0.1 collective-permute-start.8
  106.5 0.0 collective-permute-done.9.d_other
  106.5 2.1 %collective-permute-done.8.act_other = bf16[768,384]{1,0:T(8,128)(2,1)S(1)} collective-permute-done((bf16[768,384]{1,0:T(8,128)(2,1)}, bf16[768,384]{1,0:T(8,128)(2,1)S(1)}, u32[]{:S(2)}, u32[]{:S(2)}) %collective-permute-start.8) | collective-permute-done | bytes 589856 | tf_op jit(solution)/shard_map/ppermute | solution.py:203
  108.6 0.0 copy-start.1
  108.6 0.8 copy-done.1
  109.4 5.2 %shard_map.129 = bf16[6144,128]{1,0:T(8,128)(2,1)} custom-call(s32[1]{0:T(128)} %bitcast.lane_ref, bf16[768,384]{1,0:T(8,128)(2,1)} %shard_map.128.act_mine, bf16[768,384]{1,0:T(8,128)(2,1)} %copy-done.1, bf16[384,2048]{1,0:T(8,128)(2,1)} %bitcast.42, bf16[384,1024]{1,0:T(8,128)(2,1)} %collective-permute-done.9.d_other), custom_call_target="tpu_custom_call" | custom-call | tf_op jit(solution)/shard_map/pallas_call | solution.py:152
  114.5 0.0 copy-start.7
  114.5 7.7 %all-to-all-start.1 = ((bf16[128,48,128]{2,1,0:T(8,128)(2,1)}), bf16[128,48,128]{2,1,0:T(8,128)(2,1)}, u32[]{:S(2)}, u32[]{:S(2)}) async-start(bf16[128,48,128]{2,1,0:T(8,128)(2,1)} %bitcast.41), calls=%async_computation.1 | async-start | bytes 3145728 | tf_op jit(solution)/shard_map/all_to_all | solution.py:268
  122.2 0.0 copy-done.7
  122.2 0.7 copy.38.gates_ref
  122.9 40.7 %all-to-all-done.1 = bf16[128,48,128]{2,1,0:T(8,128)(2,1)} async-done(((bf16[128,48,128]{2,1,0:T(8,128)(2,1)}), bf16[128,48,128]{2,1,0:T(8,128)(2,1)}, u32[]{:S(2)}, u32[]{:S(2)}) %all-to-all-start.1) | async-done | bytes 1572896 | tf_op jit(solution)/shard_map/all_to_all | solution.py:268
  163.6 3.4 %shard_map.130 = bf16[64,1024]{1,0:T(8,128)(2,1)} custom-call(s32[64,8]{1,0:T(8,128)} %copy-done.2, f32[64,8]{1,0:T(8,128)} %copy.38.gates_ref, bf16[6144,128]{1,0:T(8,128)(2,1)} %bitcast.15.ret_ref, f32[64,1024]{1,0:T(8,128)} %get-tuple-element.6.hid_ref), custom_call_target="tpu_custom_call" | custom-call | tf_op jit(solution)/shard_map/pallas_call | solution.py:195
  (7 shorter events, 0.1 us)
Async XLA Ops:
  0.0 14.1 %copy-start = (bf16[2048,512]{1,0:T(8,128)(2,1)S(1)}, bf16[2048,512]{1,0:T(8,128)(2,1)}, u32[]{:S(2)}) copy-start(bf16[2048,512]{1,0:T(8,128)(2,1)} %param.18) | copy-start | bytes 6291460
  8.5 9.6 %collective-permute-start = (bf16[64,2048]{1,0:T(8,128)(2,1)}, bf16[64,2048]{1,0:T(8,128)(2,1)S(1)}, u32[]{:S(2)}, u32[]{:S(2)}) collective-permute-start(bf16[64,2048]{1,0:T(8,128)(2,1)} %shard_map.127), channel_id=1, source_target_pairs={{0,64},{64,128},{128,192},{192,0},{1,65},{65,129},{129,193},{193,1... | collective-permute-start | bytes 786440 | tf_op jit(solution)/shard_map/ppermute | solution.py:232
  10.0 14.6 %collective-permute-start.2 = (bf16[64,2048]{1,0:T(8,128)(2,1)}, bf16[64,2048]{1,0:T(8,128)(2,1)S(1)}, u32[]{:S(2)}, u32[]{:S(2)}) collective-permute-start(bf16[64,2048]{1,0:T(8,128)(2,1)} %shard_map.127), channel_id=1, source_target_pairs={{0,128},{64,192},{128,0},{192,64},{1,129},{65,193},{129,1},{193,65... | collective-permute-start | bytes 786440 | tf_op jit(solution)/shard_map/ppermute | solution.py:232
  12.7 13.2 %collective-permute-start.4 = (bf16[64,2048]{1,0:T(8,128)(2,1)}, bf16[64,2048]{1,0:T(8,128)(2,1)S(1)}, u32[]{:S(2)}, u32[]{:S(2)}) collective-permute-start(bf16[64,2048]{1,0:T(8,128)(2,1)} %shard_map.127), channel_id=1, source_target_pairs={{0,192},{64,0},{128,64},{192,128},{1,193},{65,1},{129,65},{193,129... | collective-permute-start | bytes 786440 | tf_op jit(solution)/shard_map/ppermute | solution.py:232
  18.6 8.7 %copy-start.6 = (s32[64,8]{0,1:T(8,128)S(1)}, s32[64,8]{0,1:T(8,128)}, u32[]{:S(2)}) copy-start(s32[64,8]{0,1:T(8,128)} %param.21) | copy-start | bytes 6148
  18.6 9.9 %collective-permute-start.1 = (f32[64,512]{1,0:T(8,128)S(1)}, f32[64,512]{1,0:T(8,128)}, u32[]{:S(2)}, u32[]{:S(2)}) collective-permute-start(f32[64,512]{1,0:T(8,128)S(1)} %fusion.8), channel_id=1, source_target_pairs={{0,192},{64,0},{128,64},{192,128},{1,193},{65,1},{129,65},{193,129... | collective-permute-start | bytes 393224 | tf_op jit(solution)/shard_map/ppermute | solution.py:234
  25.0 7.4 %collective-permute-start.3 = (f32[64,512]{1,0:T(8,128)S(1)}, f32[64,512]{1,0:T(8,128)S(1)}, u32[]{:S(2)}, u32[]{:S(2)}) collective-permute-start(f32[64,512]{1,0:T(8,128)S(1)} %fusion.9), channel_id=1, source_target_pairs={{0,128},{64,192},{128,0},{192,64},{1,129},{65,193},{129,1},{193,65... | collective-permute-start | bytes 393224 | tf_op jit(solution)/shard_map/ppermute | solution.py:234
  26.4 12.2 %copy-start.3 = (bf16[64,2048]{1,0:T(8,128)(2,1)S(1)}, bf16[64,2048]{1,0:T(8,128)(2,1)}, u32[]{:S(2)}) copy-start(bf16[64,2048]{1,0:T(8,128)(2,1)} %param.19) | copy-start | bytes 786436
  26.4 7.4 %collective-permute-start.5 = (f32[64,512]{1,0:T(8,128)S(1)}, f32[64,512]{1,0:T(8,128)S(1)}, u32[]{:S(2)}, u32[]{:S(2)}) collective-permute-start(f32[64,512]{1,0:T(8,128)S(1)} %fusion.10), channel_id=1, source_target_pairs={{0,64},{64,128},{128,192},{192,0},{1,65},{65,129},{129,193},{193,1... | collective-permute-start | bytes 393224 | tf_op jit(solution)/shard_map/ppermute | solution.py:234
  32.4 1.4 copy-start.4
  33.8 0.7 copy-start.5
  36.2 2.4 %collective-permute-start.6 = (f32[64,2048]{1,0:T(8,128)S(1)}, f32[64,2048]{1,0:T(8,128)S(1)}, u32[]{:S(2)}, u32[]{:S(2)}) collective-permute-start(f32[64,2048]{1,0:T(8,128)S(1)} %bitcast.44), channel_id=1, source_target_pairs={{0,1},{1,0},{2,3},{3,2},{4,5},{5,4},{6,7},{7,6},{8,9},{9,8},{10,11... | collective-permute-start | bytes 1572872 | tf_op jit(solution)/shard_map/ppermute | solution.py:203
  36.8 2.0 %dynamic-slice-start = ((f32[2048]{0:T(1024)}, s32[]{:T(128)}), f32[1024]{0:T(1024)S(1)}, s32[]{:S(2)}) async-start(f32[2048]{0:T(1024)} %param.20, s32[]{:T(128)} %select_n.33), calls=%async_computation.2 | async-start | bytes 8704 | tf_op jit(solution)/shard_map/dynamic_slice | solution.py:243
  38.1 2.1 %copy-start.2 = (s32[64,8]{1,0:T(8,128)}, s32[64,8]{1,0:T(8,128)S(1)}, u32[]{:S(2)}) copy-start(s32[64,8]{1,0:T(8,128)S(1)} %add.50.code_ref) | copy-start | bytes 6148
  95.9 3.8 %collective-permute-start.7 = (bf16[6144,128]{1,0:T(8,128)(2,1)}, bf16[6144,128]{1,0:T(8,128)(2,1)}, u32[]{:S(2)}, u32[]{:S(2)}) collective-permute-start(bf16[6144,128]{1,0:T(8,128)(2,1)} %bitcast.9.mine_ref), channel_id=1, source_target_pairs={{0,1},{1,0},{2,3},{3,2},{4,5},{5,4},{6,7},{7,6},{8,9},{9,8},{10,11... | collective-permute-start | bytes 4718600 | tf_op jit(solution)/shard_map/ppermute | solution.py:203
  97.1 9.4 %collective-permute-start.9 = (bf16[384,1024]{1,0:T(8,128)(2,1)S(1)}, bf16[384,1024]{1,0:T(8,128)(2,1)}, u32[]{:S(2)}, u32[]{:S(2)}) collective-permute-start(bf16[384,1024]{1,0:T(8,128)(2,1)S(1)} %dynamic-slice_bitcast_fusion), channel_id=1, source_target_pairs={{0,1},{1,0},{2,3},{3,2},{4,5},{5,4},{6,7},{7,6},{8,9},{9,8},{10,11... | collective-permute-start | bytes 2359304 | tf_op jit(solution)/shard_map/ppermute | solution.py:203
  106.3 2.2 %collective-permute-start.8 = (bf16[768,384]{1,0:T(8,128)(2,1)}, bf16[768,384]{1,0:T(8,128)(2,1)S(1)}, u32[]{:S(2)}, u32[]{:S(2)}) collective-permute-start(bf16[768,384]{1,0:T(8,128)(2,1)} %shard_map.128.act_mine), channel_id=1, source_target_pairs={{0,1},{1,0},{2,3},{3,2},{4,5},{5,4},{6,7},{7,6},{8,9},{9,8},{10,11... | collective-permute-start | bytes 1769480 | tf_op jit(solution)/shard_map/ppermute | solution.py:203
  108.6 0.8 copy-start.1
  114.5 7.7 %copy-start.7 = (f32[64,8]{0,1:T(8,128)S(1)}, f32[64,8]{0,1:T(8,128)}, u32[]{:S(2)}) copy-start(f32[64,8]{0,1:T(8,128)} %param.22) | copy-start | bytes 6148
  114.5 49.0 %all-to-all-start.1 = ((bf16[128,48,128]{2,1,0:T(8,128)(2,1)}), bf16[128,48,128]{2,1,0:T(8,128)(2,1)}, u32[]{:S(2)}, u32[]{:S(2)}) async-start(bf16[128,48,128]{2,1,0:T(8,128)(2,1)} %bitcast.41), calls=%async_computation.1 | async-start | bytes 3145728 | tf_op jit(solution)/shard_map/all_to_all | solution.py:268

commit v12 on v11

--- a/solution.py
+++ b/solution.py
@@ -185,9 +185,9 @@
     returned = jnp.concatenate(
         [ret_ref[pl.ds(j, rows, stride=fold), :] for j in range(fold)], axis=1
     )
-    moe = jnp.dot(first, returned, preferred_element_type=jnp.float32)
-    moe = moe + jnp.dot(second, returned, preferred_element_type=jnp.float32)
-    moe = moe + jnp.dot(third, returned, preferred_element_type=jnp.float32)
+    parts = jnp.concatenate([first, second, third], axis=0)
+    summed = jnp.dot(parts, returned, preferred_element_type=jnp.float32)
+    moe = summed[:tokens] + summed[tokens:2 * tokens] + summed[2 * tokens:]
     out_ref[...] = (hid_ref[...] + moe).astype(out_ref.dtype)
 
 

time: 167 us -> 167 us (level)
  no operation moved by 1% of the time
where the time goes in v12:
time: 167 us; the launch traced here: 166 us
  waiting for transfers between devices  57 us (34%)
  blocking collectives  54.7 us (33%)
  Pallas kernels  23.2 us (14%)
  starting transfers between devices  18.6 us (11%)
  local copies, waits for them, and re-layouts  5.18 us (3%)
  other arithmetic  4.04 us (2%)
  matrix products  3.44 us (2%)
    all_to_all x1, blocking collectives, per_device(): lax.all_to_all(outgoing.reshape(owners, CAP * width, lanes), ('dp', 'expe...  54.7 us
    all_to_all x1, waiting for transfers between devices, per_device(): lax.all_to_all(expert_out.reshape(owners, CAP * width, lanes), ('dp', 'ex...  40.7 us
    pallas_call x1, Pallas kernels, attend_kernel(): pl.pallas_call(attention_kernel, grid=(kv_here,), in_specs=[pl.BlockSpec(...  8.48 us
    all_to_all x1, starting transfers between devices, per_device(): lax.all_to_all(expert_out.reshape(owners, CAP * width, lanes), ('dp', 'ex...  7.65 us
    pallas_call x1, Pallas kernels, gate_up(): pl.pallas_call(gate_up_kernel, grid_spec=pltpu.PrefetchScalarGridSpec(num...  6.68 us
    ppermute x3, waiting for transfers between devices, per_device(): blocks.append(lax.ppermute(product, 'dp', backward))  6.47 us
    ppermute x3, waiting for transfers between devices, per_device(): arrived = lax.ppermute(attended, 'dp', onward)  5.86 us
    ppermute x3, starting transfers between devices, per_device(): arrived = lax.ppermute(attended, 'dp', onward)  5.66 us
  transfers between devices with their start and end apart: 11, of which 8 were waited for; matrix products, arithmetic and copies ran while one was open for 4% of the time, Pallas kernels for 4%

profile of v12, /device:TPU:32, one launch (start us, length us, event | category | flops | bytes accessed | tf_op | source)
XLA Modules:
  0.0 166.5 jit_solution(12884490754952723066)
XLA Ops:
  0.0 0.0 copy-start
  0.0 8.5 %shard_map.127 = bf16[64,2048]{1,0:T(8,128)(2,1)} custom-call(bf16[64,2048]{1,0:T(8,128)(2,1)} %q_ref.1, bf16[64,256]{1,0:T(8,128)(2,1)} %kn_ref.1, bf16[64,256]{1,0:T(8,128)(2,1)} %vn_ref.1, bf16[1,2048,256]{2,1,0:T(8,128)(2,1)} %kr_ref.1, bf16[1,2048,256]{2,1,0:T(8,128)(2,1)} %vr_ref.1), custom_call_target="tpu_custom_call" | custom-call | tf_op jit(solution)/shard_map/pallas_call | solution.py:81
  8.5 1.5 collective-permute-start
  10.0 2.7 %collective-permute-start.2 = (bf16[64,2048]{1,0:T(8,128)(2,1)}, bf16[64,2048]{1,0:T(8,128)(2,1)S(1)}, u32[]{:S(2)}, u32[]{:S(2)}) collective-permute-start(bf16[64,2048]{1,0:T(8,128)(2,1)} %shard_map.127), channel_id=1, source_target_pairs={{0,128},{64,192},{128,0},{192,64},{1,129},{65,193},{129,1},{193,65... | collective-permute-start | bytes 786440 | tf_op jit(solution)/shard_map/ppermute | solution.py:232
  12.7 1.4 collective-permute-start.4
  14.1 0.0 copy-done
  14.1 1.4 convolution_bitcast_fusion
  15.6 2.5 %collective-permute-done = bf16[64,2048]{1,0:T(8,128)(2,1)S(1)} collective-permute-done((bf16[64,2048]{1,0:T(8,128)(2,1)}, bf16[64,2048]{1,0:T(8,128)(2,1)S(1)}, u32[]{:S(2)}, u32[]{:S(2)}) %collective-permute-start) | collective-permute-done | bytes 262176 | tf_op jit(solution)/shard_map/ppermute | solution.py:232
  18.1 0.5 fusion.8
  18.6 0.0 copy-start.6
  18.6 2.6 %collective-permute-start.1 = (f32[64,512]{1,0:T(8,128)S(1)}, f32[64,512]{1,0:T(8,128)}, u32[]{:S(2)}, u32[]{:S(2)}) collective-permute-start(f32[64,512]{1,0:T(8,128)S(1)} %fusion.8), channel_id=1, source_target_pairs={{0,192},{64,0},{128,64},{192,128},{1,193},{65,1},{129,65},{193,129... | collective-permute-start | bytes 393224 | tf_op jit(solution)/shard_map/ppermute | solution.py:234
  21.2 3.4 %collective-permute-done.2 = bf16[64,2048]{1,0:T(8,128)(2,1)S(1)} collective-permute-done((bf16[64,2048]{1,0:T(8,128)(2,1)}, bf16[64,2048]{1,0:T(8,128)(2,1)S(1)}, u32[]{:S(2)}, u32[]{:S(2)}) %collective-permute-start.2) | collective-permute-done | bytes 262176 | tf_op jit(solution)/shard_map/ppermute | solution.py:232
  24.6 0.5 fusion.9
  25.0 0.9 collective-permute-start.3
  25.9 0.0 collective-permute-done.4
  25.9 0.5 fusion.10
  26.4 0.0 copy-start.3
  26.4 0.8 collective-permute-start.5
  27.2 0.0 copy-done.6
  27.2 0.1 copy.33
  27.3 1.2 collective-permute-done.1
  28.5 3.9 %collective-permute-done.3 = f32[64,512]{1,0:T(8,128)S(1)} collective-permute-done((f32[64,512]{1,0:T(8,128)S(1)}, f32[64,512]{1,0:T(8,128)S(1)}, u32[]{:S(2)}, u32[]{:S(2)}) %collective-permute-start.3) | collective-permute-done | bytes 131104 | tf_op jit(solution)/shard_map/ppermute | solution.py:234
  32.4 0.0 copy-start.4
  32.4 1.4 collective-permute-done.5
  33.8 0.0 copy-start.5
  33.8 0.0 copy-done.4
  33.8 0.7 copy-done.5
  34.5 1.1 pad_maximum_fusion
  35.5 0.6 gather_fusion
  36.2 0.3 collective-permute-start.6
  36.5 0.1 convert_reduce_fusion
  36.6 0.1 reduce_window_sum.11
  36.7 0.1 copy.34
  36.8 0.0 dynamic-slice-start
  36.8 1.2 select_reduce_fusion
  38.1 0.0 copy-start.2
  38.1 0.5 fusion.1
  38.6 0.0 collective-permute-done.6
  38.6 0.0 copy-done.3
  38.6 0.2 multiply_reduce_fusion
  38.8 0.0 dynamic-slice-done
  38.8 0.7 fusion.2
  39.6 0.6 convolution_convert_fusion
  40.2 0.0 copy-done.2
  40.2 1.0 copy.37
  41.2 54.7 %all_to_all.10 = bf16[128,48,128]{2,1,0:T(8,128)(2,1)} all-to-all(bf16[128,48,128]{2,1,0:T(8,128)(2,1)S(1)} %bitcast.40), channel_id=1, replica_groups=mesh['dp'=4,'expert'=32,'tensor'=2] {'dp','expert'}, dimensions={0} | all-to-all | bytes 3145728 | tf_op jit(solution)/shard_map/all_to_all | solution.py:259
  95.9 0.0 collective-permute-start.7
  95.9 1.2 dynamic-slice_bitcast_fusion
  97.1 0.6 collective-permute-start.9
  97.7 2.0 %collective-permute-done.7.other_ref = bf16[6144,128]{1,0:T(8,128)(2,1)} collective-permute-done((bf16[6144,128]{1,0:T(8,128)(2,1)}, bf16[6144,128]{1,0:T(8,128)(2,1)}, u32[]{:S(2)}, u32[]{:S(2)}) %collective-permute-start.7) | collective-permute-done | bytes 1572896 | tf_op jit(solution)/shard_map/ppermute | solution.py:203
  99.7 6.7 %shard_map.128.act_mine = bf16[768,384]{1,0:T(8,128)(2,1)} custom-call(s32[1]{0:T(128)} %bitcast.lane_ref, bf16[6144,128]{1,0:T(8,128)(2,1)} %bitcast.9.mine_ref, bf16[6144,128]{1,0:T(8,128)(2,1)} %collective-permute-done.7.other_ref, bf16[2048,384]{1,0:T(8,128)(2,1)} %bitcast.36, bf16[2048,384]{1,0:T(8,128)(2,1)} %bitcast.37, bf16[2048,384]{1,0:T(8,128)(2,1)} %bitcast.38, ...), custom_call_target="tpu_custom_call" | custom-call | tf_op jit(solution)/shard_map/pallas_call | solution.py:134
  106.3 0.1 collective-permute-start.8
  106.5 0.0 collective-permute-done.9.d_other
  106.5 2.1 %collective-permute-done.8.act_other = bf16[768,384]{1,0:T(8,128)(2,1)S(1)} collective-permute-done((bf16[768,384]{1,0:T(8,128)(2,1)}, bf16[768,384]{1,0:T(8,128)(2,1)S(1)}, u32[]{:S(2)}, u32[]{:S(2)}) %collective-permute-start.8) | collective-permute-done | bytes 589856 | tf_op jit(solution)/shard_map/ppermute | solution.py:203
  108.6 0.0 copy-start.1
  108.6 0.8 copy-done.1
  109.4 5.2 %shard_map.129 = bf16[6144,128]{1,0:T(8,128)(2,1)} custom-call(s32[1]{0:T(128)} %bitcast.lane_ref, bf16[768,384]{1,0:T(8,128)(2,1)} %shard_map.128.act_mine, bf16[768,384]{1,0:T(8,128)(2,1)} %copy-done.1, bf16[384,2048]{1,0:T(8,128)(2,1)} %bitcast.42, bf16[384,1024]{1,0:T(8,128)(2,1)} %collective-permute-done.9.d_other), custom_call_target="tpu_custom_call" | custom-call | tf_op jit(solution)/shard_map/pallas_call | solution.py:152
  114.5 0.0 copy-start.7
  114.5 7.7 %all-to-all-start.1 = ((bf16[128,48,128]{2,1,0:T(8,128)(2,1)}), bf16[128,48,128]{2,1,0:T(8,128)(2,1)}, u32[]{:S(2)}, u32[]{:S(2)}) async-start(bf16[128,48,128]{2,1,0:T(8,128)(2,1)} %bitcast.41), calls=%async_computation.1 | async-start | bytes 3145728 | tf_op jit(solution)/shard_map/all_to_all | solution.py:268
  122.2 0.0 copy-done.7
  122.2 0.7 copy.38.gates_ref
  122.9 40.7 %all-to-all-done.1 = bf16[128,48,128]{2,1,0:T(8,128)(2,1)} async-done(((bf16[128,48,128]{2,1,0:T(8,128)(2,1)}), bf16[128,48,128]{2,1,0:T(8,128)(2,1)}, u32[]{:S(2)}, u32[]{:S(2)}) %all-to-all-start.1) | async-done | bytes 1572896 | tf_op jit(solution)/shard_map/all_to_all | solution.py:268
  163.6 2.9 %shard_map.130 = bf16[64,1024]{1,0:T(8,128)(2,1)} custom-call(s32[64,8]{1,0:T(8,128)} %copy-done.2, f32[64,8]{1,0:T(8,128)} %copy.38.gates_ref, bf16[6144,128]{1,0:T(8,128)(2,1)} %bitcast.15.ret_ref, f32[64,1024]{1,0:T(8,128)} %get-tuple-element.6.hid_ref), custom_call_target="tpu_custom_call" | custom-call | tf_op jit(solution)/shard_map/pallas_call | solution.py:195
  (7 shorter events, 0.1 us)
Async XLA Ops:
  0.0 14.1 %copy-start = (bf16[2048,512]{1,0:T(8,128)(2,1)S(1)}, bf16[2048,512]{1,0:T(8,128)(2,1)}, u32[]{:S(2)}) copy-start(bf16[2048,512]{1,0:T(8,128)(2,1)} %param.18) | copy-start | bytes 6291460
  8.5 9.6 %collective-permute-start = (bf16[64,2048]{1,0:T(8,128)(2,1)}, bf16[64,2048]{1,0:T(8,128)(2,1)S(1)}, u32[]{:S(2)}, u32[]{:S(2)}) collective-permute-start(bf16[64,2048]{1,0:T(8,128)(2,1)} %shard_map.127), channel_id=1, source_target_pairs={{0,64},{64,128},{128,192},{192,0},{1,65},{65,129},{129,193},{193,1... | collective-permute-start | bytes 786440 | tf_op jit(solution)/shard_map/ppermute | solution.py:232
  10.0 14.6 %collective-permute-start.2 = (bf16[64,2048]{1,0:T(8,128)(2,1)}, bf16[64,2048]{1,0:T(8,128)(2,1)S(1)}, u32[]{:S(2)}, u32[]{:S(2)}) collective-permute-start(bf16[64,2048]{1,0:T(8,128)(2,1)} %shard_map.127), channel_id=1, source_target_pairs={{0,128},{64,192},{128,0},{192,64},{1,129},{65,193},{129,1},{193,65... | collective-permute-start | bytes 786440 | tf_op jit(solution)/shard_map/ppermute | solution.py:232
  12.7 13.2 %collective-permute-start.4 = (bf16[64,2048]{1,0:T(8,128)(2,1)}, bf16[64,2048]{1,0:T(8,128)(2,1)S(1)}, u32[]{:S(2)}, u32[]{:S(2)}) collective-permute-start(bf16[64,2048]{1,0:T(8,128)(2,1)} %shard_map.127), channel_id=1, source_target_pairs={{0,192},{64,0},{128,64},{192,128},{1,193},{65,1},{129,65},{193,129... | collective-permute-start | bytes 786440 | tf_op jit(solution)/shard_map/ppermute | solution.py:232
  18.6 8.7 %copy-start.6 = (s32[64,8]{0,1:T(8,128)S(1)}, s32[64,8]{0,1:T(8,128)}, u32[]{:S(2)}) copy-start(s32[64,8]{0,1:T(8,128)} %param.21) | copy-start | bytes 6148
  18.6 9.9 %collective-permute-start.1 = (f32[64,512]{1,0:T(8,128)S(1)}, f32[64,512]{1,0:T(8,128)}, u32[]{:S(2)}, u32[]{:S(2)}) collective-permute-start(f32[64,512]{1,0:T(8,128)S(1)} %fusion.8), channel_id=1, source_target_pairs={{0,192},{64,0},{128,64},{192,128},{1,193},{65,1},{129,65},{193,129... | collective-permute-start | bytes 393224 | tf_op jit(solution)/shard_map/ppermute | solution.py:234
  25.0 7.4 %collective-permute-start.3 = (f32[64,512]{1,0:T(8,128)S(1)}, f32[64,512]{1,0:T(8,128)S(1)}, u32[]{:S(2)}, u32[]{:S(2)}) collective-permute-start(f32[64,512]{1,0:T(8,128)S(1)} %fusion.9), channel_id=1, source_target_pairs={{0,128},{64,192},{128,0},{192,64},{1,129},{65,193},{129,1},{193,65... | collective-permute-start | bytes 393224 | tf_op jit(solution)/shard_map/ppermute | solution.py:234
  26.4 12.2 %copy-start.3 = (bf16[64,2048]{1,0:T(8,128)(2,1)S(1)}, bf16[64,2048]{1,0:T(8,128)(2,1)}, u32[]{:S(2)}) copy-start(bf16[64,2048]{1,0:T(8,128)(2,1)} %param.19) | copy-start | bytes 786436
  26.4 7.4 %collective-permute-start.5 = (f32[64,512]{1,0:T(8,128)S(1)}, f32[64,512]{1,0:T(8,128)S(1)}, u32[]{:S(2)}, u32[]{:S(2)}) collective-permute-start(f32[64,512]{1,0:T(8,128)S(1)} %fusion.10), channel_id=1, source_target_pairs={{0,64},{64,128},{128,192},{192,0},{1,65},{65,129},{129,193},{193,1... | collective-permute-start | bytes 393224 | tf_op jit(solution)/shard_map/ppermute | solution.py:234
  32.4 1.4 copy-start.4
  33.8 0.7 copy-start.5
  36.2 2.4 %collective-permute-start.6 = (f32[64,2048]{1,0:T(8,128)S(1)}, f32[64,2048]{1,0:T(8,128)S(1)}, u32[]{:S(2)}, u32[]{:S(2)}) collective-permute-start(f32[64,2048]{1,0:T(8,128)S(1)} %bitcast.44), channel_id=1, source_target_pairs={{0,1},{1,0},{2,3},{3,2},{4,5},{5,4},{6,7},{7,6},{8,9},{9,8},{10,11... | collective-permute-start | bytes 1572872 | tf_op jit(solution)/shard_map/ppermute | solution.py:203
  36.8 2.0 %dynamic-slice-start = ((f32[2048]{0:T(1024)}, s32[]{:T(128)}), f32[1024]{0:T(1024)S(1)}, s32[]{:S(2)}) async-start(f32[2048]{0:T(1024)} %param.20, s32[]{:T(128)} %select_n.33), calls=%async_computation.2 | async-start | bytes 8704 | tf_op jit(solution)/shard_map/dynamic_slice | solution.py:243
  38.1 2.1 %copy-start.2 = (s32[64,8]{1,0:T(8,128)}, s32[64,8]{1,0:T(8,128)S(1)}, u32[]{:S(2)}) copy-start(s32[64,8]{1,0:T(8,128)S(1)} %add.50.code_ref) | copy-start | bytes 6148
  95.9 3.8 %collective-permute-start.7 = (bf16[6144,128]{1,0:T(8,128)(2,1)}, bf16[6144,128]{1,0:T(8,128)(2,1)}, u32[]{:S(2)}, u32[]{:S(2)}) collective-permute-start(bf16[6144,128]{1,0:T(8,128)(2,1)} %bitcast.9.mine_ref), channel_id=1, source_target_pairs={{0,1},{1,0},{2,3},{3,2},{4,5},{5,4},{6,7},{7,6},{8,9},{9,8},{10,11... | collective-permute-start | bytes 4718600 | tf_op jit(solution)/shard_map/ppermute | solution.py:203
  97.1 9.4 %collective-permute-start.9 = (bf16[384,1024]{1,0:T(8,128)(2,1)S(1)}, bf16[384,1024]{1,0:T(8,128)(2,1)}, u32[]{:S(2)}, u32[]{:S(2)}) collective-permute-start(bf16[384,1024]{1,0:T(8,128)(2,1)S(1)} %dynamic-slice_bitcast_fusion), channel_id=1, source_target_pairs={{0,1},{1,0},{2,3},{3,2},{4,5},{5,4},{6,7},{7,6},{8,9},{9,8},{10,11... | collective-permute-start | bytes 2359304 | tf_op jit(solution)/shard_map/ppermute | solution.py:203
  106.3 2.2 %collective-permute-start.8 = (bf16[768,384]{1,0:T(8,128)(2,1)}, bf16[768,384]{1,0:T(8,128)(2,1)S(1)}, u32[]{:S(2)}, u32[]{:S(2)}) collective-permute-start(bf16[768,384]{1,0:T(8,128)(2,1)} %shard_map.128.act_mine), channel_id=1, source_target_pairs={{0,1},{1,0},{2,3},{3,2},{4,5},{5,4},{6,7},{7,6},{8,9},{9,8},{10,11... | collective-permute-start | bytes 1769480 | tf_op jit(solution)/shard_map/ppermute | solution.py:203
  108.6 0.8 copy-start.1
  114.5 7.7 %copy-start.7 = (f32[64,8]{0,1:T(8,128)S(1)}, f32[64,8]{0,1:T(8,128)}, u32[]{:S(2)}) copy-start(f32[64,8]{0,1:T(8,128)} %param.22) | copy-start | bytes 6148
  114.5 49.0 %all-to-all-start.1 = ((bf16[128,48,128]{2,1,0:T(8,128)(2,1)}), bf16[128,48,128]{2,1,0:T(8,128)(2,1)}, u32[]{:S(2)}, u32[]{:S(2)}) async-start(bf16[128,48,128]{2,1,0:T(8,128)(2,1)} %bitcast.41), calls=%async_computation.1 | async-start | bytes 3145728 | tf_op jit(solution)/shard_map/all_to_all | solution.py:268

commit v13 on v8

--- a/solution.py
+++ b/solution.py
@@ -167,6 +167,58 @@
     )(lane, act_mine, act_other, down_mat, down_other)
 
 
+def norm_dispatch_kernel(lane_ref, mine_ref, other_ref, res_ref, gain_ref, code_ref, hid_ref, out_ref, fold_ref):
+    half = hid_ref.shape[1]
+    fold = half // HEAD_WIDTH
+    rows = fold_ref.shape[0] // fold
+    top, tokens = code_ref.shape
+    hidden = res_ref[...].astype(jnp.float32) + (mine_ref[...] + other_ref[...])
+    mean_square = jnp.mean(hidden * hidden, axis=-1, keepdims=True)
+    normed = (hidden * lax.rsqrt(mean_square + 1e-06) * gain_ref[...]).astype(jnp.bfloat16)
+    first = lane_ref[0] == 0
+    hid_ref[...] = jnp.where(first, hidden[:, :half], hidden[:, half:])
+    normed_half = jnp.where(first, normed[:, :half], normed[:, half:])
+    places = lax.broadcasted_iota(jnp.int32, (rows, tokens), 0)
+    code = code_ref[...]
+    spread = jnp.zeros((rows, tokens), jnp.float32)
+    for k in range(top):
+        spread = spread + jnp.where(places == code[k:k + 1, :], jnp.float32(1.0), jnp.float32(0.0))
+    out = jnp.dot(spread.astype(jnp.bfloat16), normed_half, preferred_element_type=jnp.float32)
+    for j in range(fold):
+        fold_ref[pl.ds(j, rows, stride=fold), :] = out[:, j * HEAD_WIDTH:(j + 1) * HEAD_WIDTH]
+    out_ref[...] = fold_ref[...].astype(out_ref.dtype)
+
+
+def norm_dispatch(lane, mine, other, residual, gain, code_t, rows, interpret=False):
+    tokens, width = mine.shape
+    half = width // 2
+    fold = half // HEAD_WIDTH
+    return pl.pallas_call(
+        norm_dispatch_kernel,
+        grid_spec=pltpu.PrefetchScalarGridSpec(
+            num_scalar_prefetch=1,
+            grid=(1,),
+            in_specs=[
+                pl.BlockSpec((tokens, width), lambda i, lane_ref: (0, 0)),
+                pl.BlockSpec((tokens, width), lambda i, lane_ref: (0, 0)),
+                pl.BlockSpec((tokens, width), lambda i, lane_ref: (0, 0)),
+                pl.BlockSpec((1, width), lambda i, lane_ref: (0, 0)),
+                pl.BlockSpec(code_t.shape, lambda i, lane_ref: (0, 0)),
+            ],
+            out_specs=[
+                pl.BlockSpec((tokens, half), lambda i, lane_ref: (0, 0)),
+                pl.BlockSpec((rows * fold, HEAD_WIDTH), lambda i, lane_ref: (0, 0)),
+            ],
+            scratch_shapes=[pltpu.VMEM((rows * fold, HEAD_WIDTH), jnp.float32)],
+        ),
+        out_shape=[
+            jax.ShapeDtypeStruct((tokens, half), jnp.float32),
+            jax.ShapeDtypeStruct((rows * fold, HEAD_WIDTH), jnp.bfloat16),
+        ],
+        interpret=interpret,
+    )(lane, mine, other, residual, gain, code_t)
+
+
 def swap_pair(x):
     return lax.ppermute(x, "tensor", [(0, 1), (1, 0)])
 
@@ -203,12 +255,7 @@
     stacked = jnp.stack(blocks)
     order = (jnp.arange(groups) - here) % groups
     mine = stacked[order].transpose(1, 0, 2).reshape(tokens_here, D)
-    summed = mine + swap_pair(mine)
-    hidden = residual.astype(jnp.float32) + summed
-    mean_square = jnp.mean(hidden * hidden, axis=-1, keepdims=True)
-    normed = (hidden * lax.rsqrt(mean_square + 1e-06) * norm_gain).astype(jnp.bfloat16)
-    hidden_half = lax.dynamic_slice_in_dim(hidden, lane * half, half, 1)
-    normed_half = lax.dynamic_slice_in_dim(normed, lane * half, half, 1)
+    other_sum = swap_pair(mine)
 
     owners = lax.axis_size("dp") * lax.axis_size("expert")
     onehot = (expert_ids[:, :, None] == jnp.arange(owners)[None, None, :]).astype(jnp.int32)
@@ -217,18 +264,16 @@
     slot = jnp.sum(onehot * before[:, None, :], axis=-1)
     code = expert_ids * CAP + slot
     pick = (code[:, :, None] == jnp.arange(owners * CAP)[None, None, :]).astype(jnp.bfloat16)
-    spread = jnp.sum(pick, axis=1)
     lanes = 128
     width = half // lanes
-    outgoing = jnp.einsum(
-        "tr,tjl->rjl", spread, normed_half.reshape(tokens_here, width, lanes),
-        preferred_element_type=jnp.float32,
-    ).astype(jnp.bfloat16)
+    lane_id = lane.astype(jnp.int32).reshape(1)
+    hidden_half, outgoing = norm_dispatch(
+        lane_id, mine, other_sum, residual, norm_gain.reshape(1, -1), code.T, owners * CAP
+    )
     received = lax.all_to_all(
         outgoing.reshape(owners, CAP * width, lanes), ("dp", "expert"), split_axis=0, concat_axis=0, tiled=True
     ).reshape(owners * CAP * width, lanes)
     other = swap_pair(received)
-    lane_id = lane.astype(jnp.int32).reshape(1)
     down_other = swap_pair(lax.dynamic_slice_in_dim(w_down[0], (1 - lane) * half, half, 1))
     act = gate_up(lane_id, received, other, w_gate[0], w_up[0])
     expert_out = down(lane_id, act, swap_pair(act), w_down[0], down_other)

time: 166 us -> 169 us (1.018)
  Pallas kernels: 20.3 us -> 23.9 us
    pallas_call x0 -> x1, Pallas kernels: none -> 3.53 us  [norm_dispatch(): pl.pallas_call(norm_dispatch_kernel, grid_spec=pltpu.PrefetchScalarGridSp...]
    ppermute x3, waiting for transfers between devices: 5.87 us -> 8.39 us  [per_device(): arrived = lax.ppermute(attended, 'dp', onward)]
    reduce_sum x2 -> x0, other arithmetic: 1.76 us -> none  [the longest x1 1.23 us: per_device(): mean_square = jnp.mean(hidden * hidden, axis=-1, keepdims=True)]
  transfers between devices with their start and end apart: 11 -> 11, of which waited for: 8 -> 7; matrix products, arithmetic and copies ran while one was open for 4% -> 4% of each run, Pallas kernels for 4% -> 4%
where the time goes in v13:
time: 169 us
  waiting for transfers between devices  58.5 us (35%)
  blocking collectives  55.7 us (33%)
  Pallas kernels  23.9 us (14%)
  starting transfers between devices  18.2 us (11%)
  matrix products  5.68 us (3%)
  local copies, waits for them, and re-layouts  3.77 us (2%)
  other arithmetic  2.87 us (2%)
    all_to_all x1, blocking collectives, per_device(): lax.all_to_all(outgoing.reshape(owners, CAP * width, lanes), ('dp', 'expe...  55.7 us
    all_to_all x1, waiting for transfers between devices, per_device(): lax.all_to_all(expert_out.reshape(owners, CAP * width, lanes), ('dp', 'ex...  41.2 us
    pallas_call x1, Pallas kernels, attend_kernel(): pl.pallas_call(attention_kernel, grid=(kv_here,), in_specs=[pl.BlockSpec(...  8.48 us
    ppermute x3, waiting for transfers between devices, per_device(): arrived = lax.ppermute(attended, 'dp', onward)  8.39 us
    all_to_all x1, starting transfers between devices, per_device(): lax.all_to_all(expert_out.reshape(owners, CAP * width, lanes), ('dp', 'ex...  7.66 us
    pallas_call x1, Pallas kernels, gate_up(): pl.pallas_call(gate_up_kernel, grid_spec=pltpu.PrefetchScalarGridSpec(num...  6.68 us
    ppermute x3, starting transfers between devices, per_device(): blocks.append(lax.ppermute(product, 'dp', backward))  5.25 us
    pallas_call x1, Pallas kernels, down(): pl.pallas_call(down_kernel, grid_spec=pltpu.PrefetchScalarGridSpec(num_sc...  5.16 us
  transfers between devices with their start and end apart: 11, of which 7 were waited for; matrix products, arithmetic and copies ran while one was open for 4% of the time, Pallas kernels for 4%

profile of v13, /device:TPU:32, one launch (start us, length us, event | category | flops | bytes accessed | tf_op | source)
XLA Modules:
  0.0 168.8 jit_solution(11348536848850460017)
XLA Ops:
  0.0 0.0 copy-start
  0.0 8.5 %shard_map.127 = bf16[64,2048]{1,0:T(8,128)(2,1)} custom-call(bf16[64,2048]{1,0:T(8,128)(2,1)} %q_ref.1, bf16[64,256]{1,0:T(8,128)(2,1)} %kn_ref.1, bf16[64,256]{1,0:T(8,128)(2,1)} %vn_ref.1, bf16[1,2048,256]{2,1,0:T(8,128)(2,1)} %kr_ref.1, bf16[1,2048,256]{2,1,0:T(8,128)(2,1)} %vr_ref.1), custom_call_target="tpu_custom_call" | custom-call | tf_op jit(solution)/shard_map/pallas_call | solution.py:80
  8.5 2.8 %collective-permute-start.4 = (bf16[64,2048]{1,0:T(8,128)(2,1)}, bf16[64,2048]{1,0:T(8,128)(2,1)S(1)}, u32[]{:S(2)}, u32[]{:S(2)}) collective-permute-start(bf16[64,2048]{1,0:T(8,128)(2,1)} %shard_map.127), channel_id=1, source_target_pairs={{0,192},{64,0},{128,64},{192,128},{1,193},{65,1},{129,65},{193,129... | collective-permute-start | bytes 786440 | tf_op jit(solution)/shard_map/ppermute | solution.py:252
  11.2 0.8 collective-permute-start.2
  12.0 0.9 collective-permute-start
  12.9 0.0 copy-done
  12.9 1.4 convolution_bitcast_fusion
  14.4 8.4 %collective-permute-done.4 = bf16[64,2048]{1,0:T(8,128)(2,1)S(1)} collective-permute-done((bf16[64,2048]{1,0:T(8,128)(2,1)}, bf16[64,2048]{1,0:T(8,128)(2,1)S(1)}, u32[]{:S(2)}, u32[]{:S(2)}) %collective-permute-start.4) | collective-permute-done | bytes 262176 | tf_op jit(solution)/shard_map/ppermute | solution.py:252
  22.8 0.5 fusion.10
  23.2 0.1 collective-permute-start.5
  23.3 0.0 collective-permute-done.2
  23.4 0.5 fusion.9
  23.8 5.1 %collective-permute-start.3 = (f32[64,512]{1,0:T(8,128)S(1)}, f32[64,512]{1,0:T(8,128)S(1)}, u32[]{:S(2)}, u32[]{:S(2)}) collective-permute-start(f32[64,512]{1,0:T(8,128)S(1)} %fusion.9), channel_id=1, source_target_pairs={{0,128},{64,192},{128,0},{192,64},{1,129},{65,193},{129,1},{193,65... | collective-permute-start | bytes 393224 | tf_op jit(solution)/shard_map/ppermute | solution.py:254
  28.9 0.0 collective-permute-done
  28.9 0.5 fusion.8
  29.4 0.0 copy-start.6
  29.4 0.1 collective-permute-start.1
  29.5 1.4 collective-permute-done.5
  30.9 2.6 %collective-permute-done.3 = f32[64,512]{1,0:T(8,128)S(1)} collective-permute-done((f32[64,512]{1,0:T(8,128)S(1)}, f32[64,512]{1,0:T(8,128)S(1)}, u32[]{:S(2)}, u32[]{:S(2)}) %collective-permute-start.3) | collective-permute-done | bytes 131104 | tf_op jit(solution)/shard_map/ppermute | solution.py:254
  33.5 0.9 collective-permute-done.1
  34.5 0.6 gather_fusion
  35.1 0.0 copy-start.1
  35.1 0.1 collective-permute-start.6
  35.2 0.0 copy-done.6
  35.2 0.1 copy.24
  35.3 0.1 convert_reduce_fusion
  35.5 0.1 reduce_window_sum.11
  35.6 1.2 select_reduce_fusion
  36.8 0.1 copy.25
  36.9 0.6 multiply_add_fusion
  37.5 0.0 collective-permute-done.6.other_ref
  37.5 0.0 copy-start.3
  37.5 0.0 copy-done.1
  37.5 0.8 copy-done.3
  38.3 3.5 %shard_map.128 = (f32[64,1024]{1,0:T(8,128)}, bf16[6144,128]{1,0:T(8,128)(2,1)}) custom-call(s32[1]{0:T(128)} %bitcast.lane_ref, f32[64,2048]{1,0:T(8,128)} %bitcast.50, f32[64,2048]{1,0:T(8,128)} %copy-done.3, bf16[64,2048]{1,0:T(8,128)(2,1)} %res_ref.1, f32[1,2048]{1,0:T(1,128)} %bitcast.58, s32[8,64]{1,0:T(8,128)} %bitcast.57), custom_call_target="tpu_custom_call" | custom-call | tf_op jit(solution)/shard_map/pallas_call | solution.py:196
  41.8 55.7 %all_to_all.10 = bf16[128,48,128]{2,1,0:T(8,128)(2,1)} all-to-all(bf16[128,48,128]{2,1,0:T(8,128)(2,1)} %bitcast.52), channel_id=1, replica_groups=mesh['dp'=4,'expert'=32,'tensor'=2] {'dp','expert'}, dimensions={0} | all-to-all | bytes 3145728 | tf_op jit(solution)/shard_map/all_to_all | solution.py:273
  97.6 0.0 collective-permute-start.7
  97.6 1.2 dynamic-slice_bitcast_fusion
  98.8 0.6 collective-permute-start.9
  99.4 2.0 %collective-permute-done.7.other_ref = bf16[6144,128]{1,0:T(8,128)(2,1)} collective-permute-done((bf16[6144,128]{1,0:T(8,128)(2,1)}, bf16[6144,128]{1,0:T(8,128)(2,1)}, u32[]{:S(2)}, u32[]{:S(2)}) %collective-permute-start.7) | collective-permute-done | bytes 1572896 | tf_op jit(solution)/shard_map/ppermute | solution.py:223
  101.3 6.7 %shard_map.129.act_mine = bf16[768,384]{1,0:T(8,128)(2,1)} custom-call(s32[1]{0:T(128)} %bitcast.lane_ref, bf16[6144,128]{1,0:T(8,128)(2,1)} %bitcast.12.mine_ref, bf16[6144,128]{1,0:T(8,128)(2,1)} %collective-permute-done.7.other_ref, bf16[2048,384]{1,0:T(8,128)(2,1)} %bitcast.43, bf16[2048,384]{1,0:T(8,128)(2,1)} %bitcast.44, bf16[2048,384]{1,0:T(8,128)(2,1)} %bitcast.45, ...), custom_call_target="tpu_custom_call" | custom-call | tf_op jit(solution)/shard_map/pallas_call | solution.py:133
  108.0 0.1 collective-permute-start.8
  108.2 0.0 collective-permute-done.9.d_other
  108.2 2.1 %collective-permute-done.8.act_other = bf16[768,384]{1,0:T(8,128)(2,1)S(1)} collective-permute-done((bf16[768,384]{1,0:T(8,128)(2,1)}, bf16[768,384]{1,0:T(8,128)(2,1)S(1)}, u32[]{:S(2)}, u32[]{:S(2)}) %collective-permute-start.8) | collective-permute-done | bytes 589856 | tf_op jit(solution)/shard_map/ppermute | solution.py:223
  110.2 0.0 copy-start.2
  110.2 0.8 copy-done.2
  111.1 5.2 %shard_map.130 = bf16[6144,128]{1,0:T(8,128)(2,1)} custom-call(s32[1]{0:T(128)} %bitcast.lane_ref, bf16[768,384]{1,0:T(8,128)(2,1)} %shard_map.129.act_mine, bf16[768,384]{1,0:T(8,128)(2,1)} %copy-done.2, bf16[384,2048]{1,0:T(8,128)(2,1)} %bitcast.48, bf16[384,1024]{1,0:T(8,128)(2,1)} %collective-permute-done.9.d_other), custom_call_target="tpu_custom_call" | custom-call | tf_op jit(solution)/shard_map/pallas_call | solution.py:151
  116.2 0.0 copy-start.5
  116.2 0.0 copy-start.7
  116.2 7.7 %all-to-all-start.1 = ((bf16[128,48,128]{2,1,0:T(8,128)(2,1)}), bf16[128,48,128]{2,1,0:T(8,128)(2,1)}, u32[]{:S(2)}, u32[]{:S(2)}) async-start(bf16[128,48,128]{2,1,0:T(8,128)(2,1)} %bitcast.47), calls=%async_computation.1 | async-start | bytes 3145728 | tf_op jit(solution)/shard_map/all_to_all | solution.py:281
  123.9 0.0 copy-done.5
  123.9 0.1 copy.27
  124.0 0.0 copy-done.7
  124.0 0.1 copy.26
  124.1 41.2 %all-to-all-done.1 = bf16[128,48,128]{2,1,0:T(8,128)(2,1)} async-done(((bf16[128,48,128]{2,1,0:T(8,128)(2,1)}), bf16[128,48,128]{2,1,0:T(8,128)(2,1)}, u32[]{:S(2)}, u32[]{:S(2)}) %all-to-all-start.1) | async-done | bytes 1572896 | tf_op jit(solution)/shard_map/all_to_all | solution.py:281
  165.3 0.0 copy-start.4
  165.3 2.8 %multiply_reduce_fusion = f32[64,8,128]{2,1,0:T(8,128)S(1)} fusion(bf16[768,8,128]{2,1,0:T(8,128)(2,1)} %bitcast.18, f32[64,8]{1,0:T(8,128)S(1)} %copy.26, s32[64,8]{1,0:T(8,128)S(1)} %copy.27), kind=kOutput, calls=%fused_computation.1 | convolution fusion | flops 806682624 | bytes 1839104 | tf_op jit(solution)/shard_map/tkr,rjl->tkjl/dot_general | solution.py:284
  168.1 0.0 copy-done.4
  168.1 0.7 fusion.5
  (5 shorter events, 0.1 us)
Async XLA Ops:
  0.0 12.9 %copy-start = (bf16[2048,512]{1,0:T(8,128)(2,1)S(1)}, bf16[2048,512]{1,0:T(8,128)(2,1)}, u32[]{:S(2)}) copy-start(bf16[2048,512]{1,0:T(8,128)(2,1)} %param.18) | copy-start | bytes 6291460
  8.5 14.3 %collective-permute-start.4 = (bf16[64,2048]{1,0:T(8,128)(2,1)}, bf16[64,2048]{1,0:T(8,128)(2,1)S(1)}, u32[]{:S(2)}, u32[]{:S(2)}) collective-permute-start(bf16[64,2048]{1,0:T(8,128)(2,1)} %shard_map.127), channel_id=1, source_target_pairs={{0,192},{64,0},{128,64},{192,128},{1,193},{65,1},{129,65},{193,129... | collective-permute-start | bytes 786440 | tf_op jit(solution)/shard_map/ppermute | solution.py:252
  11.2 12.1 %collective-permute-start.2 = (bf16[64,2048]{1,0:T(8,128)(2,1)}, bf16[64,2048]{1,0:T(8,128)(2,1)S(1)}, u32[]{:S(2)}, u32[]{:S(2)}) collective-permute-start(bf16[64,2048]{1,0:T(8,128)(2,1)} %shard_map.127), channel_id=1, source_target_pairs={{0,128},{64,192},{128,0},{192,64},{1,129},{65,193},{129,1},{193,65... | collective-permute-start | bytes 786440 | tf_op jit(solution)/shard_map/ppermute | solution.py:252
  12.0 16.9 %collective-permute-start = (bf16[64,2048]{1,0:T(8,128)(2,1)}, bf16[64,2048]{1,0:T(8,128)(2,1)S(1)}, u32[]{:S(2)}, u32[]{:S(2)}) collective-permute-start(bf16[64,2048]{1,0:T(8,128)(2,1)} %shard_map.127), channel_id=1, source_target_pairs={{0,64},{64,128},{128,192},{192,0},{1,65},{65,129},{129,193},{193,1... | collective-permute-start | bytes 786440 | tf_op jit(solution)/shard_map/ppermute | solution.py:252
  23.2 7.7 %collective-permute-start.5 = (f32[64,512]{1,0:T(8,128)S(1)}, f32[64,512]{1,0:T(8,128)S(1)}, u32[]{:S(2)}, u32[]{:S(2)}) collective-permute-start(f32[64,512]{1,0:T(8,128)S(1)} %fusion.10), channel_id=1, source_target_pairs={{0,64},{64,128},{128,192},{192,0},{1,65},{65,129},{129,193},{193,1... | collective-permute-start | bytes 393224 | tf_op jit(solution)/shard_map/ppermute | solution.py:254
  23.8 9.7 %collective-permute-start.3 = (f32[64,512]{1,0:T(8,128)S(1)}, f32[64,512]{1,0:T(8,128)S(1)}, u32[]{:S(2)}, u32[]{:S(2)}) collective-permute-start(f32[64,512]{1,0:T(8,128)S(1)} %fusion.9), channel_id=1, source_target_pairs={{0,128},{64,192},{128,0},{192,64},{1,129},{65,193},{129,1},{193,65... | collective-permute-start | bytes 393224 | tf_op jit(solution)/shard_map/ppermute | solution.py:254
  29.4 5.8 %copy-start.6 = (s32[64,8]{0,1:T(8,128)S(1)}, s32[64,8]{0,1:T(8,128)}, u32[]{:S(2)}) copy-start(s32[64,8]{0,1:T(8,128)} %param.21) | copy-start | bytes 6148
  29.4 5.0 %collective-permute-start.1 = (f32[64,512]{1,0:T(8,128)S(1)}, f32[64,512]{1,0:T(8,128)S(1)}, u32[]{:S(2)}, u32[]{:S(2)}) collective-permute-start(f32[64,512]{1,0:T(8,128)S(1)} %fusion.8), channel_id=1, source_target_pairs={{0,192},{64,0},{128,64},{192,128},{1,193},{65,1},{129,65},{193,129... | collective-permute-start | bytes 393224 | tf_op jit(solution)/shard_map/ppermute | solution.py:254
  35.1 2.4 %copy-start.1 = (f32[4,8,8,512]{3,2,0,1:T(8,128)}, f32[4,8,8,512]{3,2,0,1:T(8,128)S(1)}, u32[]{:S(2)}) copy-start(f32[4,8,8,512]{3,2,0,1:T(8,128)S(1)} %copy.30) | copy-start | bytes 1572868
  35.1 2.4 %collective-permute-start.6 = (f32[64,2048]{1,0:T(8,128)S(1)}, f32[64,2048]{1,0:T(8,128)S(1)}, u32[]{:S(2)}, u32[]{:S(2)}) collective-permute-start(f32[64,2048]{1,0:T(8,128)S(1)} %bitcast.49), channel_id=1, source_target_pairs={{0,1},{1,0},{2,3},{3,2},{4,5},{5,4},{6,7},{7,6},{8,9},{9,8},{10,11... | collective-permute-start | bytes 1572872 | tf_op jit(solution)/shard_map/ppermute | solution.py:223
  37.5 0.8 copy-start.3
  97.6 3.8 %collective-permute-start.7 = (bf16[6144,128]{1,0:T(8,128)(2,1)}, bf16[6144,128]{1,0:T(8,128)(2,1)}, u32[]{:S(2)}, u32[]{:S(2)}) collective-permute-start(bf16[6144,128]{1,0:T(8,128)(2,1)} %bitcast.12.mine_ref), channel_id=1, source_target_pairs={{0,1},{1,0},{2,3},{3,2},{4,5},{5,4},{6,7},{7,6},{8,9},{9,8},{10,11... | collective-permute-start | bytes 4718600 | tf_op jit(solution)/shard_map/ppermute | solution.py:223
  98.8 9.4 %collective-permute-start.9 = (bf16[384,1024]{1,0:T(8,128)(2,1)S(1)}, bf16[384,1024]{1,0:T(8,128)(2,1)}, u32[]{:S(2)}, u32[]{:S(2)}) collective-permute-start(bf16[384,1024]{1,0:T(8,128)(2,1)S(1)} %dynamic-slice_bitcast_fusion), channel_id=1, source_target_pairs={{0,1},{1,0},{2,3},{3,2},{4,5},{5,4},{6,7},{7,6},{8,9},{9,8},{10,11... | collective-permute-start | bytes 2359304 | tf_op jit(solution)/shard_map/ppermute | solution.py:223
  108.0 2.2 %collective-permute-start.8 = (bf16[768,384]{1,0:T(8,128)(2,1)}, bf16[768,384]{1,0:T(8,128)(2,1)S(1)}, u32[]{:S(2)}, u32[]{:S(2)}) collective-permute-start(bf16[768,384]{1,0:T(8,128)(2,1)} %shard_map.129.act_mine), channel_id=1, source_target_pairs={{0,1},{1,0},{2,3},{3,2},{4,5},{5,4},{6,7},{7,6},{8,9},{9,8},{10,11... | collective-permute-start | bytes 1769480 | tf_op jit(solution)/shard_map/ppermute | solution.py:223
  110.2 0.8 copy-start.2
  116.2 7.7 %copy-start.5 = (s32[64,8]{0,1:T(8,128)S(1)}, s32[64,8]{0,1:T(8,128)}, u32[]{:S(2)}) copy-start(s32[64,8]{0,1:T(8,128)} %multiply_add_fusion) | copy-start | bytes 6148
  116.2 7.8 %copy-start.7 = (f32[64,8]{0,1:T(8,128)S(1)}, f32[64,8]{0,1:T(8,128)}, u32[]{:S(2)}) copy-start(f32[64,8]{0,1:T(8,128)} %param.22) | copy-start | bytes 6148
  116.2 49.0 %all-to-all-start.1 = ((bf16[128,48,128]{2,1,0:T(8,128)(2,1)}), bf16[128,48,128]{2,1,0:T(8,128)(2,1)}, u32[]{:S(2)}, u32[]{:S(2)}) async-start(bf16[128,48,128]{2,1,0:T(8,128)(2,1)} %bitcast.47), calls=%async_computation.1 | async-start | bytes 3145728 | tf_op jit(solution)/shard_map/all_to_all | solution.py:281
  165.3 2.8 %copy-start.4 = (f32[64,1024]{1,0:T(8,128)S(1)}, f32[64,1024]{1,0:T(8,128)}, u32[]{:S(2)}) copy-start(f32[64,1024]{1,0:T(8,128)} %get-tuple-element.7) | copy-start | bytes 786436

commit v14 on v8

--- a/solution.py
+++ b/solution.py
@@ -199,7 +199,7 @@
         backward = [(i, (i - shift) % groups) for i in range(groups)]
         arrived = lax.ppermute(attended, "dp", onward)
         product = jnp.dot(arrived, out_weight, preferred_element_type=jnp.float32)
-        blocks.append(lax.ppermute(product, "dp", backward))
+        blocks.append(lax.ppermute(product.astype(jnp.bfloat16), "dp", backward).astype(jnp.float32))
     stacked = jnp.stack(blocks)
     order = (jnp.arange(groups) - here) % groups
     mine = stacked[order].transpose(1, 0, 2).reshape(tokens_here, D)

time: 166 us -> 166 us (level)
    ppermute x3, waiting for transfers between devices: 5.87 us -> 8.3 us  [per_device(): arrived = lax.ppermute(attended, 'dp', onward)]
    ppermute x3, waiting for transfers between devices: 6.49 us -> 4.22 us  [per_device(): lax.ppermute(product.astype(jnp.bfloat16), 'dp', backward)]
  transfers between devices with their start and end apart: 11 -> 11, of which waited for: 8 -> 7; matrix products, arithmetic and copies ran while one was open for 4% -> 4% of each run, Pallas kernels for 4% -> 4%
where the time goes in v14:
time: 166 us; the launch traced here: 165 us
  waiting for transfers between devices  58 us (35%)
  blocking collectives  55 us (33%)
  Pallas kernels  20.3 us (12%)
  starting transfers between devices  18.4 us (11%)
  matrix products  6.24 us (4%)
  other arithmetic  4.07 us (2%)
  local copies, waits for them, and re-layouts  3.16 us (2%)
    all_to_all x1, blocking collectives, per_device(): lax.all_to_all(outgoing.reshape(owners, CAP * width, lanes), ('dp', 'expe...  55 us
    all_to_all x1, waiting for transfers between devices, per_device(): lax.all_to_all(expert_out.reshape(owners, CAP * width, lanes), ('dp', 'ex...  41.3 us
    pallas_call x1, Pallas kernels, attend_kernel(): pl.pallas_call(attention_kernel, grid=(kv_here,), in_specs=[pl.BlockSpec(...  8.47 us
    ppermute x3, waiting for transfers between devices, per_device(): arrived = lax.ppermute(attended, 'dp', onward)  8.3 us
    all_to_all x1, starting transfers between devices, per_device(): lax.all_to_all(expert_out.reshape(owners, CAP * width, lanes), ('dp', 'ex...  7.66 us
    pallas_call x1, Pallas kernels, gate_up(): pl.pallas_call(gate_up_kernel, grid_spec=pltpu.PrefetchScalarGridSpec(num...  6.68 us
    ppermute x3, starting transfers between devices, per_device(): lax.ppermute(product.astype(jnp.bfloat16), 'dp', backward)  5.25 us
    pallas_call x1, Pallas kernels, down(): pl.pallas_call(down_kernel, grid_spec=pltpu.PrefetchScalarGridSpec(num_sc...  5.14 us
  transfers between devices with their start and end apart: 11, of which 7 were waited for; matrix products, arithmetic and copies ran while one was open for 4% of the time, Pallas kernels for 4%

profile of v14, /device:TPU:32, one launch (start us, length us, event | category | flops | bytes accessed | tf_op | source)
XLA Modules:
  0.0 165.4 jit_solution(10429106604801899857)
XLA Ops:
  0.0 0.0 copy-start
  0.0 0.0 copy-start.2
  0.0 8.5 %shard_map.127 = bf16[64,2048]{1,0:T(8,128)(2,1)} custom-call(bf16[64,2048]{1,0:T(8,128)(2,1)} %q_ref.1, bf16[64,256]{1,0:T(8,128)(2,1)} %kn_ref.1, bf16[64,256]{1,0:T(8,128)(2,1)} %vn_ref.1, bf16[1,2048,256]{2,1,0:T(8,128)(2,1)} %kr_ref.1, bf16[1,2048,256]{2,1,0:T(8,128)(2,1)} %vr_ref.1), custom_call_target="tpu_custom_call" | custom-call | tf_op jit(solution)/shard_map/pallas_call | solution.py:80
  8.5 2.8 %collective-permute-start.4 = (bf16[64,2048]{1,0:T(8,128)(2,1)}, bf16[64,2048]{1,0:T(8,128)(2,1)S(1)}, u32[]{:S(2)}, u32[]{:S(2)}) collective-permute-start(bf16[64,2048]{1,0:T(8,128)(2,1)} %shard_map.127), channel_id=1, source_target_pairs={{0,192},{64,0},{128,64},{192,128},{1,193},{65,1},{129,65},{193,129... | collective-permute-start | bytes 786440 | tf_op jit(solution)/shard_map/ppermute | solution.py:200
  11.2 0.8 collective-permute-start.2
  12.0 0.9 collective-permute-start
  13.0 0.0 copy-done.2
  13.0 0.1 copy.34
  13.0 0.0 copy-done
  13.0 1.4 convolution_bitcast_fusion
  14.5 8.3 %collective-permute-done.4 = bf16[64,2048]{1,0:T(8,128)(2,1)S(1)} collective-permute-done((bf16[64,2048]{1,0:T(8,128)(2,1)}, bf16[64,2048]{1,0:T(8,128)(2,1)S(1)}, u32[]{:S(2)}, u32[]{:S(2)}) %collective-permute-start.4) | collective-permute-done | bytes 262176 | tf_op jit(solution)/shard_map/ppermute | solution.py:200
  22.8 0.5 convolution_convert_fusion.1
  23.3 0.1 collective-permute-start.5
  23.3 0.0 collective-permute-done.2
  23.4 0.5 convolution_convert_fusion.2
  23.8 5.1 %collective-permute-start.3 = (bf16[64,512]{1,0:T(8,128)(2,1)S(1)}, bf16[64,512]{1,0:T(8,128)(2,1)S(1)}, u32[]{:S(2)}, u32[]{:S(2)}) collective-permute-start(bf16[64,512]{1,0:T(8,128)(2,1)S(1)} %convolution_convert_fusion.2), channel_id=1, source_target_pairs={{0,128},{64,192},{128,0},{192,64},{1,129},{65,193},{129,1},{193,65... | collective-permute-start | bytes 196616 | tf_op jit(solution)/shard_map/ppermute | solution.py:202
  28.9 0.0 collective-permute-done
  28.9 0.5 convolution_convert_fusion.3
  29.4 0.1 collective-permute-start.1
  29.5 0.3 collective-permute-done.5
  29.8 1.4 collective-permute-done.3
  31.3 2.4 %collective-permute-done.1 = bf16[64,512]{1,0:T(8,128)(2,1)S(1)} collective-permute-done((bf16[64,512]{1,0:T(8,128)(2,1)S(1)}, bf16[64,512]{1,0:T(8,128)(2,1)S(1)}, u32[]{:S(2)}, u32[]{:S(2)}) %collective-permute-start.1) | collective-permute-done | bytes 65568 | tf_op jit(solution)/shard_map/ppermute | solution.py:202
  33.8 0.0 copy-start.1
  33.8 0.6 gather_fusion
  34.4 0.3 collective-permute-start.6
  34.7 0.1 convert_reduce_fusion
  34.9 0.1 reduce_window_sum.11
  35.0 1.2 select_reduce_fusion
  36.2 0.1 copy.35
  36.3 0.1 copy.36
  36.4 0.0 dynamic-slice-start
  36.4 0.5 fusion.5
  36.9 0.0 collective-permute-done.6
  37.0 0.0 copy-done.1
  37.0 1.2 multiply_reduce_fusion.1
  38.2 0.0 dynamic-slice-done
  38.2 0.6 convolution_convert_fusion
  38.9 1.0 copy.38
  39.9 55.0 %all_to_all.10 = bf16[128,48,128]{2,1,0:T(8,128)(2,1)} all-to-all(bf16[128,48,128]{2,1,0:T(8,128)(2,1)S(1)} %bitcast.61), channel_id=1, replica_groups=mesh['dp'=4,'expert'=32,'tensor'=2] {'dp','expert'}, dimensions={0} | all-to-all | bytes 3145728 | tf_op jit(solution)/shard_map/all_to_all | solution.py:227
  94.9 0.0 collective-permute-start.7
  94.9 1.2 dynamic-slice_bitcast_fusion
  96.1 0.6 collective-permute-start.9
  96.7 2.0 %collective-permute-done.7.other_ref = bf16[6144,128]{1,0:T(8,128)(2,1)} collective-permute-done((bf16[6144,128]{1,0:T(8,128)(2,1)}, bf16[6144,128]{1,0:T(8,128)(2,1)}, u32[]{:S(2)}, u32[]{:S(2)}) %collective-permute-start.7) | collective-permute-done | bytes 1572896 | tf_op jit(solution)/shard_map/ppermute | solution.py:171
  98.6 6.7 %shard_map.128.act_mine = bf16[768,384]{1,0:T(8,128)(2,1)} custom-call(s32[1]{0:T(128)} %bitcast.8.lane_ref, bf16[6144,128]{1,0:T(8,128)(2,1)} %bitcast.11.mine_ref, bf16[6144,128]{1,0:T(8,128)(2,1)} %collective-permute-done.7.other_ref, bf16[2048,384]{1,0:T(8,128)(2,1)} %bitcast.57, bf16[2048,384]{1,0:T(8,128)(2,1)} %bitcast.58, ...), custom_call_target="tpu_custom_call" | custom-call | tf_op jit(solution)/shard_map/pallas_call | solution.py:133
  105.3 0.1 collective-permute-start.8
  105.5 0.0 collective-permute-done.9.d_other
  105.5 2.2 %collective-permute-done.8.act_other = bf16[768,384]{1,0:T(8,128)(2,1)} collective-permute-done((bf16[768,384]{1,0:T(8,128)(2,1)}, bf16[768,384]{1,0:T(8,128)(2,1)}, u32[]{:S(2)}, u32[]{:S(2)}) %collective-permute-start.8) | collective-permute-done | bytes 589856 | tf_op jit(solution)/shard_map/ppermute | solution.py:171
  107.7 5.1 %shard_map.129 = bf16[6144,128]{1,0:T(8,128)(2,1)} custom-call(s32[1]{0:T(128)} %bitcast.8.lane_ref, bf16[768,384]{1,0:T(8,128)(2,1)} %shard_map.128.act_mine, bf16[768,384]{1,0:T(8,128)(2,1)} %collective-permute-done.8.act_other, bf16[384,2048]{1,0:T(8,128)(2,1)} %bitcast.63, bf16[384,1024]{1,0:T(8,128)(2,1)} %collective-permute-done.9.d_other), custom_call_target="tpu_custom_call" | custom-call | tf_op jit(solution)/shard_map/pallas_call | solution.py:151
  112.8 0.0 copy-start.3
  112.8 7.7 %all-to-all-start.1 = ((bf16[128,48,128]{2,1,0:T(8,128)(2,1)}), bf16[128,48,128]{2,1,0:T(8,128)(2,1)}, u32[]{:S(2)}, u32[]{:S(2)}) async-start(bf16[128,48,128]{2,1,0:T(8,128)(2,1)} %bitcast.62), calls=%async_computation.1 | async-start | bytes 3145728 | tf_op jit(solution)/shard_map/all_to_all | solution.py:236
  120.5 0.0 copy-done.3
  120.5 0.1 copy.33
  120.6 41.3 %all-to-all-done.1 = bf16[128,48,128]{2,1,0:T(8,128)(2,1)} async-done(((bf16[128,48,128]{2,1,0:T(8,128)(2,1)}), bf16[128,48,128]{2,1,0:T(8,128)(2,1)}, u32[]{:S(2)}, u32[]{:S(2)}) %all-to-all-start.1) | async-done | bytes 1572896 | tf_op jit(solution)/shard_map/all_to_all | solution.py:236
  161.8 2.8 %multiply_reduce_fusion = f32[64,8,128]{2,1,0:T(8,128)S(1)} fusion(bf16[768,8,128]{2,1,0:T(8,128)(2,1)} %bitcast.17, f32[64,8]{1,0:T(8,128)S(1)} %copy.33, s32[64,8]{1,0:T(8,128)S(1)} %copy.36), kind=kOutput, calls=%fused_computation.1 | convolution fusion | flops 806682624 | bytes 1839104 | tf_op jit(solution)/shard_map/tkr,rjl->tkjl/dot_general | solution.py:239
  164.6 0.7 fusion.7
  (10 shorter events, 0.1 us)
Async XLA Ops:
  0.0 13.0 %copy-start = (bf16[2048,512]{1,0:T(8,128)(2,1)S(1)}, bf16[2048,512]{1,0:T(8,128)(2,1)}, u32[]{:S(2)}) copy-start(bf16[2048,512]{1,0:T(8,128)(2,1)} %param.18) | copy-start | bytes 6291460
  0.0 12.9 %copy-start.2 = (s32[64,8]{0,1:T(8,128)S(1)}, s32[64,8]{0,1:T(8,128)}, u32[]{:S(2)}) copy-start(s32[64,8]{0,1:T(8,128)} %param.21) | copy-start | bytes 6148
  8.5 14.3 %collective-permute-start.4 = (bf16[64,2048]{1,0:T(8,128)(2,1)}, bf16[64,2048]{1,0:T(8,128)(2,1)S(1)}, u32[]{:S(2)}, u32[]{:S(2)}) collective-permute-start(bf16[64,2048]{1,0:T(8,128)(2,1)} %shard_map.127), channel_id=1, source_target_pairs={{0,192},{64,0},{128,64},{192,128},{1,193},{65,1},{129,65},{193,129... | collective-permute-start | bytes 786440 | tf_op jit(solution)/shard_map/ppermute | solution.py:200
  11.2 12.1 %collective-permute-start.2 = (bf16[64,2048]{1,0:T(8,128)(2,1)}, bf16[64,2048]{1,0:T(8,128)(2,1)S(1)}, u32[]{:S(2)}, u32[]{:S(2)}) collective-permute-start(bf16[64,2048]{1,0:T(8,128)(2,1)} %shard_map.127), channel_id=1, source_target_pairs={{0,128},{64,192},{128,0},{192,64},{1,129},{65,193},{129,1},{193,65... | collective-permute-start | bytes 786440 | tf_op jit(solution)/shard_map/ppermute | solution.py:200
  12.0 16.9 %collective-permute-start = (bf16[64,2048]{1,0:T(8,128)(2,1)}, bf16[64,2048]{1,0:T(8,128)(2,1)S(1)}, u32[]{:S(2)}, u32[]{:S(2)}) collective-permute-start(bf16[64,2048]{1,0:T(8,128)(2,1)} %shard_map.127), channel_id=1, source_target_pairs={{0,64},{64,128},{128,192},{192,0},{1,65},{65,129},{129,193},{193,1... | collective-permute-start | bytes 786440 | tf_op jit(solution)/shard_map/ppermute | solution.py:200
  23.3 6.6 %collective-permute-start.5 = (bf16[64,512]{1,0:T(8,128)(2,1)S(1)}, bf16[64,512]{1,0:T(8,128)(2,1)S(1)}, u32[]{:S(2)}, u32[]{:S(2)}) collective-permute-start(bf16[64,512]{1,0:T(8,128)(2,1)S(1)} %convolution_convert_fusion.1), channel_id=1, source_target_pairs={{0,64},{64,128},{128,192},{192,0},{1,65},{65,129},{129,193},{193,1... | collective-permute-start | bytes 196616 | tf_op jit(solution)/shard_map/ppermute | solution.py:202
  23.8 7.5 %collective-permute-start.3 = (bf16[64,512]{1,0:T(8,128)(2,1)S(1)}, bf16[64,512]{1,0:T(8,128)(2,1)S(1)}, u32[]{:S(2)}, u32[]{:S(2)}) collective-permute-start(bf16[64,512]{1,0:T(8,128)(2,1)S(1)} %convolution_convert_fusion.2), channel_id=1, source_target_pairs={{0,128},{64,192},{128,0},{192,64},{1,129},{65,193},{129,1},{193,65... | collective-permute-start | bytes 196616 | tf_op jit(solution)/shard_map/ppermute | solution.py:202
  29.4 4.3 %collective-permute-start.1 = (bf16[64,512]{1,0:T(8,128)(2,1)S(1)}, bf16[64,512]{1,0:T(8,128)(2,1)S(1)}, u32[]{:S(2)}, u32[]{:S(2)}) collective-permute-start(bf16[64,512]{1,0:T(8,128)(2,1)S(1)} %convolution_convert_fusion.3), channel_id=1, source_target_pairs={{0,192},{64,0},{128,64},{192,128},{1,193},{65,1},{129,65},{193,129... | collective-permute-start | bytes 196616 | tf_op jit(solution)/shard_map/ppermute | solution.py:202
  33.8 3.2 %copy-start.1 = (bf16[64,2048]{1,0:T(8,128)(2,1)S(1)}, bf16[64,2048]{1,0:T(8,128)(2,1)}, u32[]{:S(2)}) copy-start(bf16[64,2048]{1,0:T(8,128)(2,1)} %param.19) | copy-start | bytes 786436
  34.4 2.5 %collective-permute-start.6 = (f32[64,2048]{1,0:T(8,128)S(1)}, f32[64,2048]{1,0:T(8,128)}, u32[]{:S(2)}, u32[]{:S(2)}) collective-permute-start(f32[64,2048]{1,0:T(8,128)S(1)} %bitcast.65), channel_id=1, source_target_pairs={{0,1},{1,0},{2,3},{3,2},{4,5},{5,4},{6,7},{7,6},{8,9},{9,8},{10,11... | collective-permute-start | bytes 1572872 | tf_op jit(solution)/shard_map/ppermute | solution.py:171
  36.4 1.8 %dynamic-slice-start = ((f32[2048]{0:T(1024)}, s32[]{:T(128)}), f32[1024]{0:T(1024)S(1)}, s32[]{:S(2)}) async-start(f32[2048]{0:T(1024)} %param.20, s32[]{:T(128)} %select_n.33), calls=%async_computation.2 | async-start | bytes 8704 | tf_op jit(solution)/shard_map/dynamic_slice | solution.py:211
  94.9 3.8 %collective-permute-start.7 = (bf16[6144,128]{1,0:T(8,128)(2,1)}, bf16[6144,128]{1,0:T(8,128)(2,1)}, u32[]{:S(2)}, u32[]{:S(2)}) collective-permute-start(bf16[6144,128]{1,0:T(8,128)(2,1)} %bitcast.11.mine_ref), channel_id=1, source_target_pairs={{0,1},{1,0},{2,3},{3,2},{4,5},{5,4},{6,7},{7,6},{8,9},{9,8},{10,11... | collective-permute-start | bytes 4718600 | tf_op jit(solution)/shard_map/ppermute | solution.py:171
  96.1 9.4 %collective-permute-start.9 = (bf16[384,1024]{1,0:T(8,128)(2,1)S(1)}, bf16[384,1024]{1,0:T(8,128)(2,1)}, u32[]{:S(2)}, u32[]{:S(2)}) collective-permute-start(bf16[384,1024]{1,0:T(8,128)(2,1)S(1)} %dynamic-slice_bitcast_fusion), channel_id=1, source_target_pairs={{0,1},{1,0},{2,3},{3,2},{4,5},{5,4},{6,7},{7,6},{8,9},{9,8},{10,11... | collective-permute-start | bytes 2359304 | tf_op jit(solution)/shard_map/ppermute | solution.py:171
  105.3 2.3 %collective-permute-start.8 = (bf16[768,384]{1,0:T(8,128)(2,1)}, bf16[768,384]{1,0:T(8,128)(2,1)}, u32[]{:S(2)}, u32[]{:S(2)}) collective-permute-start(bf16[768,384]{1,0:T(8,128)(2,1)} %shard_map.128.act_mine), channel_id=1, source_target_pairs={{0,1},{1,0},{2,3},{3,2},{4,5},{5,4},{6,7},{7,6},{8,9},{9,8},{10,11... | collective-permute-start | bytes 1769480 | tf_op jit(solution)/shard_map/ppermute | solution.py:171
  112.8 7.7 %copy-start.3 = (f32[64,8]{0,1:T(8,128)S(1)}, f32[64,8]{0,1:T(8,128)}, u32[]{:S(2)}) copy-start(f32[64,8]{0,1:T(8,128)} %param.22) | copy-start | bytes 6148
  112.8 49.0 %all-to-all-start.1 = ((bf16[128,48,128]{2,1,0:T(8,128)(2,1)}), bf16[128,48,128]{2,1,0:T(8,128)(2,1)}, u32[]{:S(2)}, u32[]{:S(2)}) async-start(bf16[128,48,128]{2,1,0:T(8,128)(2,1)} %bitcast.62), calls=%async_computation.1 | async-start | bytes 3145728 | tf_op jit(solution)/shard_map/all_to_all | solution.py:236

commit v15 on v8

--- a/solution.py
+++ b/solution.py
@@ -143,7 +143,7 @@
     )(lane, mine, other, gate_mat, gate_mat, up_mat, up_mat)
 
 
-def down(lane, act_mine, act_other, down_mat, down_other, block_rows=256, interpret=False):
+def down(lane, act_mine, act_other, down_mat, down_other, block_rows=768, interpret=False):
     rows, hidden = act_mine.shape
     half = down_other.shape[1]
     fold = half // HEAD_WIDTH

time: 166 us -> 165 us (level)
  no operation moved by 1% of the time
where the time goes in v15:
time: 165 us
  waiting for transfers between devices  57.8 us (35%)
  blocking collectives  54.7 us (33%)
  Pallas kernels  20.1 us (12%)
  starting transfers between devices  18.6 us (11%)
  matrix products  6.26 us (4%)
  other arithmetic  4.04 us (2%)
  local copies, waits for them, and re-layouts  3.16 us (2%)
    all_to_all x1, blocking collectives, per_device(): lax.all_to_all(outgoing.reshape(owners, CAP * width, lanes), ('dp', 'expe...  54.7 us
    all_to_all x1, waiting for transfers between devices, per_device(): lax.all_to_all(expert_out.reshape(owners, CAP * width, lanes), ('dp', 'ex...  41.3 us
    pallas_call x1, Pallas kernels, attend_kernel(): pl.pallas_call(attention_kernel, grid=(kv_here,), in_specs=[pl.BlockSpec(...  8.47 us
    all_to_all x1, starting transfers between devices, per_device(): lax.all_to_all(expert_out.reshape(owners, CAP * width, lanes), ('dp', 'ex...  7.66 us
    pallas_call x1, Pallas kernels, gate_up(): pl.pallas_call(gate_up_kernel, grid_spec=pltpu.PrefetchScalarGridSpec(num...  6.68 us
    ppermute x3, waiting for transfers between devices, per_device(): blocks.append(lax.ppermute(product, 'dp', backward))  6.49 us
    ppermute x3, waiting for transfers between devices, per_device(): arrived = lax.ppermute(attended, 'dp', onward)  5.87 us
    ppermute x3, starting transfers between devices, per_device(): arrived = lax.ppermute(attended, 'dp', onward)  5.66 us
  transfers between devices with their start and end apart: 11, of which 8 were waited for; matrix products, arithmetic and copies ran while one was open for 4% of the time, Pallas kernels for 4%

profile of v15, /device:TPU:32, one launch (start us, length us, event | category | flops | bytes accessed | tf_op | source)
XLA Modules:
  0.0 164.9 jit_solution(5574121193757758406)
XLA Ops:
  0.0 0.0 copy-start
  0.0 8.5 %shard_map.127 = bf16[64,2048]{1,0:T(8,128)(2,1)} custom-call(bf16[64,2048]{1,0:T(8,128)(2,1)} %q_ref.1, bf16[64,256]{1,0:T(8,128)(2,1)} %kn_ref.1, bf16[64,256]{1,0:T(8,128)(2,1)} %vn_ref.1, bf16[1,2048,256]{2,1,0:T(8,128)(2,1)} %kr_ref.1, bf16[1,2048,256]{2,1,0:T(8,128)(2,1)} %vr_ref.1), custom_call_target="tpu_custom_call" | custom-call | tf_op jit(solution)/shard_map/pallas_call | solution.py:80
  8.5 1.5 collective-permute-start
  10.0 2.7 %collective-permute-start.2 = (bf16[64,2048]{1,0:T(8,128)(2,1)}, bf16[64,2048]{1,0:T(8,128)(2,1)S(1)}, u32[]{:S(2)}, u32[]{:S(2)}) collective-permute-start(bf16[64,2048]{1,0:T(8,128)(2,1)} %shard_map.127), channel_id=1, source_target_pairs={{0,128},{64,192},{128,0},{192,64},{1,129},{65,193},{129,1},{193,65... | collective-permute-start | bytes 786440 | tf_op jit(solution)/shard_map/ppermute | solution.py:200
  12.7 1.4 collective-permute-start.4
  14.1 0.0 copy-done
  14.1 1.4 convolution_bitcast_fusion
  15.6 2.5 %collective-permute-done = bf16[64,2048]{1,0:T(8,128)(2,1)S(1)} collective-permute-done((bf16[64,2048]{1,0:T(8,128)(2,1)}, bf16[64,2048]{1,0:T(8,128)(2,1)S(1)}, u32[]{:S(2)}, u32[]{:S(2)}) %collective-permute-start) | collective-permute-done | bytes 262176 | tf_op jit(solution)/shard_map/ppermute | solution.py:200
  18.1 0.5 fusion.14
  18.6 2.6 %collective-permute-start.1 = (f32[64,512]{1,0:T(8,128)S(1)}, f32[64,512]{1,0:T(8,128)S(1)}, u32[]{:S(2)}, u32[]{:S(2)}) collective-permute-start(f32[64,512]{1,0:T(8,128)S(1)} %fusion.14), channel_id=1, source_target_pairs={{0,192},{64,0},{128,64},{192,128},{1,193},{65,1},{129,65},{193,129... | collective-permute-start | bytes 393224 | tf_op jit(solution)/shard_map/ppermute | solution.py:202
  21.2 3.4 %collective-permute-done.2 = bf16[64,2048]{1,0:T(8,128)(2,1)S(1)} collective-permute-done((bf16[64,2048]{1,0:T(8,128)(2,1)}, bf16[64,2048]{1,0:T(8,128)(2,1)S(1)}, u32[]{:S(2)}, u32[]{:S(2)}) %collective-permute-start.2) | collective-permute-done | bytes 262176 | tf_op jit(solution)/shard_map/ppermute | solution.py:200
  24.5 0.5 fusion.15
  25.0 0.0 copy-start.2
  25.0 0.9 collective-permute-start.3
  25.9 0.0 collective-permute-done.4
  25.9 0.5 fusion.16
  26.4 0.8 collective-permute-start.5
  27.2 0.0 copy-done.2
  27.2 0.1 copy.34
  27.3 1.1 collective-permute-done.1
  28.4 4.0 %collective-permute-done.3 = f32[64,512]{1,0:T(8,128)S(1)} collective-permute-done((f32[64,512]{1,0:T(8,128)S(1)}, f32[64,512]{1,0:T(8,128)S(1)}, u32[]{:S(2)}, u32[]{:S(2)}) %collective-permute-start.3) | collective-permute-done | bytes 131104 | tf_op jit(solution)/shard_map/ppermute | solution.py:202
  32.4 1.4 collective-permute-done.5
  33.9 0.0 copy-start.1
  33.9 0.6 gather_fusion
  34.5 0.3 collective-permute-start.6
  34.8 0.1 convert_reduce_fusion
  34.9 0.1 reduce_window_sum.11
  35.0 1.2 select_reduce_fusion
  36.3 0.1 copy.35
  36.4 0.1 copy.36
  36.4 0.0 dynamic-slice-start
  36.5 0.5 fusion.5
  37.0 0.0 collective-permute-done.6
  37.0 0.0 copy-done.1
  37.0 1.2 multiply_reduce_fusion.1
  38.3 0.0 dynamic-slice-done
  38.3 0.6 convolution_convert_fusion
  38.9 1.0 copy.38
  39.9 54.7 %all_to_all.10 = bf16[128,48,128]{2,1,0:T(8,128)(2,1)} all-to-all(bf16[128,48,128]{2,1,0:T(8,128)(2,1)S(1)} %bitcast.55), channel_id=1, replica_groups=mesh['dp'=4,'expert'=32,'tensor'=2] {'dp','expert'}, dimensions={0} | all-to-all | bytes 3145728 | tf_op jit(solution)/shard_map/all_to_all | solution.py:227
  94.6 0.0 collective-permute-start.7
  94.6 1.2 dynamic-slice_bitcast_fusion
  95.8 0.6 collective-permute-start.9
  96.4 2.0 %collective-permute-done.7.other_ref = bf16[6144,128]{1,0:T(8,128)(2,1)} collective-permute-done((bf16[6144,128]{1,0:T(8,128)(2,1)}, bf16[6144,128]{1,0:T(8,128)(2,1)}, u32[]{:S(2)}, u32[]{:S(2)}) %collective-permute-start.7) | collective-permute-done | bytes 1572896 | tf_op jit(solution)/shard_map/ppermute | solution.py:171
  98.4 6.7 %shard_map.128.act_mine = bf16[768,384]{1,0:T(8,128)(2,1)} custom-call(s32[1]{0:T(128)} %bitcast.8.lane_ref, bf16[6144,128]{1,0:T(8,128)(2,1)} %bitcast.11.mine_ref, bf16[6144,128]{1,0:T(8,128)(2,1)} %collective-permute-done.7.other_ref, bf16[2048,384]{1,0:T(8,128)(2,1)} %bitcast.51, bf16[2048,384]{1,0:T(8,128)(2,1)} %bitcast.52, ...), custom_call_target="tpu_custom_call" | custom-call | tf_op jit(solution)/shard_map/pallas_call | solution.py:133
  105.1 0.1 collective-permute-start.8
  105.2 0.0 collective-permute-done.9.d_other
  105.2 2.2 %collective-permute-done.8.act_other = bf16[768,384]{1,0:T(8,128)(2,1)} collective-permute-done((bf16[768,384]{1,0:T(8,128)(2,1)}, bf16[768,384]{1,0:T(8,128)(2,1)}, u32[]{:S(2)}, u32[]{:S(2)}) %collective-permute-start.8) | collective-permute-done | bytes 589856 | tf_op jit(solution)/shard_map/ppermute | solution.py:171
  107.4 4.9 %shard_map.129 = bf16[6144,128]{1,0:T(8,128)(2,1)} custom-call(s32[1]{0:T(128)} %bitcast.8.lane_ref, bf16[768,384]{1,0:T(8,128)(2,1)} %shard_map.128.act_mine, bf16[768,384]{1,0:T(8,128)(2,1)} %collective-permute-done.8.act_other, bf16[384,2048]{1,0:T(8,128)(2,1)} %bitcast.57, bf16[384,1024]{1,0:T(8,128)(2,1)} %collective-permute-done.9.d_other), custom_call_target="tpu_custom_call" | custom-call | tf_op jit(solution)/shard_map/pallas_call | solution.py:151
  112.3 0.0 copy-start.3
  112.3 7.7 %all-to-all-start.1 = ((bf16[128,48,128]{2,1,0:T(8,128)(2,1)}), bf16[128,48,128]{2,1,0:T(8,128)(2,1)}, u32[]{:S(2)}, u32[]{:S(2)}) async-start(bf16[128,48,128]{2,1,0:T(8,128)(2,1)} %bitcast.56), calls=%async_computation.1 | async-start | bytes 3145728 | tf_op jit(solution)/shard_map/all_to_all | solution.py:236
  120.0 0.0 copy-done.3
  120.0 0.1 copy.33
  120.1 41.3 %all-to-all-done.1 = bf16[128,48,128]{2,1,0:T(8,128)(2,1)} async-done(((bf16[128,48,128]{2,1,0:T(8,128)(2,1)}), bf16[128,48,128]{2,1,0:T(8,128)(2,1)}, u32[]{:S(2)}, u32[]{:S(2)}) %all-to-all-start.1) | async-done | bytes 1572896 | tf_op jit(solution)/shard_map/all_to_all | solution.py:236
  161.4 2.8 %multiply_reduce_fusion = f32[64,8,128]{2,1,0:T(8,128)S(1)} fusion(bf16[768,8,128]{2,1,0:T(8,128)(2,1)} %bitcast.17, f32[64,8]{1,0:T(8,128)S(1)} %copy.33, s32[64,8]{1,0:T(8,128)S(1)} %copy.36), kind=kOutput, calls=%fused_computation.1 | convolution fusion | flops 806682624 | bytes 1839104 | tf_op jit(solution)/shard_map/tkr,rjl->tkjl/dot_general | solution.py:239
  164.2 0.7 fusion.7
  (7 shorter events, 0.1 us)
Async XLA Ops:
  0.0 14.1 %copy-start = (bf16[2048,512]{1,0:T(8,128)(2,1)S(1)}, bf16[2048,512]{1,0:T(8,128)(2,1)}, u32[]{:S(2)}) copy-start(bf16[2048,512]{1,0:T(8,128)(2,1)} %param.18) | copy-start | bytes 6291460
  8.5 9.6 %collective-permute-start = (bf16[64,2048]{1,0:T(8,128)(2,1)}, bf16[64,2048]{1,0:T(8,128)(2,1)S(1)}, u32[]{:S(2)}, u32[]{:S(2)}) collective-permute-start(bf16[64,2048]{1,0:T(8,128)(2,1)} %shard_map.127), channel_id=1, source_target_pairs={{0,64},{64,128},{128,192},{192,0},{1,65},{65,129},{129,193},{193,1... | collective-permute-start | bytes 786440 | tf_op jit(solution)/shard_map/ppermute | solution.py:200
  10.0 14.6 %collective-permute-start.2 = (bf16[64,2048]{1,0:T(8,128)(2,1)}, bf16[64,2048]{1,0:T(8,128)(2,1)S(1)}, u32[]{:S(2)}, u32[]{:S(2)}) collective-permute-start(bf16[64,2048]{1,0:T(8,128)(2,1)} %shard_map.127), channel_id=1, source_target_pairs={{0,128},{64,192},{128,0},{192,64},{1,129},{65,193},{129,1},{193,65... | collective-permute-start | bytes 786440 | tf_op jit(solution)/shard_map/ppermute | solution.py:200
  12.7 13.3 %collective-permute-start.4 = (bf16[64,2048]{1,0:T(8,128)(2,1)}, bf16[64,2048]{1,0:T(8,128)(2,1)S(1)}, u32[]{:S(2)}, u32[]{:S(2)}) collective-permute-start(bf16[64,2048]{1,0:T(8,128)(2,1)} %shard_map.127), channel_id=1, source_target_pairs={{0,192},{64,0},{128,64},{192,128},{1,193},{65,1},{129,65},{193,129... | collective-permute-start | bytes 786440 | tf_op jit(solution)/shard_map/ppermute | solution.py:200
  18.6 9.8 %collective-permute-start.1 = (f32[64,512]{1,0:T(8,128)S(1)}, f32[64,512]{1,0:T(8,128)S(1)}, u32[]{:S(2)}, u32[]{:S(2)}) collective-permute-start(f32[64,512]{1,0:T(8,128)S(1)} %fusion.14), channel_id=1, source_target_pairs={{0,192},{64,0},{128,64},{192,128},{1,193},{65,1},{129,65},{193,129... | collective-permute-start | bytes 393224 | tf_op jit(solution)/shard_map/ppermute | solution.py:202
  25.0 2.2 %copy-start.2 = (s32[64,8]{0,1:T(8,128)S(1)}, s32[64,8]{0,1:T(8,128)}, u32[]{:S(2)}) copy-start(s32[64,8]{0,1:T(8,128)} %param.21) | copy-start | bytes 6148
  25.0 7.4 %collective-permute-start.3 = (f32[64,512]{1,0:T(8,128)S(1)}, f32[64,512]{1,0:T(8,128)S(1)}, u32[]{:S(2)}, u32[]{:S(2)}) collective-permute-start(f32[64,512]{1,0:T(8,128)S(1)} %fusion.15), channel_id=1, source_target_pairs={{0,128},{64,192},{128,0},{192,64},{1,129},{65,193},{129,1},{193,65... | collective-permute-start | bytes 393224 | tf_op jit(solution)/shard_map/ppermute | solution.py:202
  26.4 7.4 %collective-permute-start.5 = (f32[64,512]{1,0:T(8,128)S(1)}, f32[64,512]{1,0:T(8,128)S(1)}, u32[]{:S(2)}, u32[]{:S(2)}) collective-permute-start(f32[64,512]{1,0:T(8,128)S(1)} %fusion.16), channel_id=1, source_target_pairs={{0,64},{64,128},{128,192},{192,0},{1,65},{65,129},{129,193},{193,1... | collective-permute-start | bytes 393224 | tf_op jit(solution)/shard_map/ppermute | solution.py:202
  33.9 3.2 %copy-start.1 = (bf16[64,2048]{1,0:T(8,128)(2,1)S(1)}, bf16[64,2048]{1,0:T(8,128)(2,1)}, u32[]{:S(2)}) copy-start(bf16[64,2048]{1,0:T(8,128)(2,1)} %param.19) | copy-start | bytes 786436
  34.5 2.5 %collective-permute-start.6 = (f32[64,2048]{1,0:T(8,128)S(1)}, f32[64,2048]{1,0:T(8,128)}, u32[]{:S(2)}, u32[]{:S(2)}) collective-permute-start(f32[64,2048]{1,0:T(8,128)S(1)} %bitcast.59), channel_id=1, source_target_pairs={{0,1},{1,0},{2,3},{3,2},{4,5},{5,4},{6,7},{7,6},{8,9},{9,8},{10,11... | collective-permute-start | bytes 1572872 | tf_op jit(solution)/shard_map/ppermute | solution.py:171
  36.4 1.8 %dynamic-slice-start = ((f32[2048]{0:T(1024)}, s32[]{:T(128)}), f32[1024]{0:T(1024)S(1)}, s32[]{:S(2)}) async-start(f32[2048]{0:T(1024)} %param.20, s32[]{:T(128)} %select_n.33), calls=%async_computation.2 | async-start | bytes 8704 | tf_op jit(solution)/shard_map/dynamic_slice | solution.py:211
  94.6 3.8 %collective-permute-start.7 = (bf16[6144,128]{1,0:T(8,128)(2,1)}, bf16[6144,128]{1,0:T(8,128)(2,1)}, u32[]{:S(2)}, u32[]{:S(2)}) collective-permute-start(bf16[6144,128]{1,0:T(8,128)(2,1)} %bitcast.11.mine_ref), channel_id=1, source_target_pairs={{0,1},{1,0},{2,3},{3,2},{4,5},{5,4},{6,7},{7,6},{8,9},{9,8},{10,11... | collective-permute-start | bytes 4718600 | tf_op jit(solution)/shard_map/ppermute | solution.py:171
  95.8 9.4 %collective-permute-start.9 = (bf16[384,1024]{1,0:T(8,128)(2,1)S(1)}, bf16[384,1024]{1,0:T(8,128)(2,1)}, u32[]{:S(2)}, u32[]{:S(2)}) collective-permute-start(bf16[384,1024]{1,0:T(8,128)(2,1)S(1)} %dynamic-slice_bitcast_fusion), channel_id=1, source_target_pairs={{0,1},{1,0},{2,3},{3,2},{4,5},{5,4},{6,7},{7,6},{8,9},{9,8},{10,11... | collective-permute-start | bytes 2359304 | tf_op jit(solution)/shard_map/ppermute | solution.py:171
  105.1 2.3 %collective-permute-start.8 = (bf16[768,384]{1,0:T(8,128)(2,1)}, bf16[768,384]{1,0:T(8,128)(2,1)}, u32[]{:S(2)}, u32[]{:S(2)}) collective-permute-start(bf16[768,384]{1,0:T(8,128)(2,1)} %shard_map.128.act_mine), channel_id=1, source_target_pairs={{0,1},{1,0},{2,3},{3,2},{4,5},{5,4},{6,7},{7,6},{8,9},{9,8},{10,11... | collective-permute-start | bytes 1769480 | tf_op jit(solution)/shard_map/ppermute | solution.py:171
  112.3 7.7 %copy-start.3 = (f32[64,8]{0,1:T(8,128)S(1)}, f32[64,8]{0,1:T(8,128)}, u32[]{:S(2)}) copy-start(f32[64,8]{0,1:T(8,128)} %param.22) | copy-start | bytes 6148
  112.3 49.0 %all-to-all-start.1 = ((bf16[128,48,128]{2,1,0:T(8,128)(2,1)}), bf16[128,48,128]{2,1,0:T(8,128)(2,1)}, u32[]{:S(2)}, u32[]{:S(2)}) async-start(bf16[128,48,128]{2,1,0:T(8,128)(2,1)} %bitcast.56), calls=%async_computation.1 | async-start | bytes 3145728 | tf_op jit(solution)/shard_map/all_to_all | solution.py:236
